TPU v7x, 512 devices: a whole 4x4x16 slice. The times are simulated.
512 devices in a mesh: req: 64 (over z, y), hid: 8 (over x, core).
Axes of the slice: x: 4, y: 4, z: 16, core: 2. Of those that a mesh axis runs over, the one named last changes fastest.
Arguments:
- resid: bfloat16 [8192, 1024], P('req'), may hold values from -6 to 6
- attn_gain: float32 [1024], replicated, may hold values from 0.25 to 1.75
- w_query: bfloat16 [1024, 1024], P(None, 'hid'), may hold values from -4 to 4
- w_key: bfloat16 [1024, 1024], P(None, 'hid'), may hold values from -1 to 1
- w_value: bfloat16 [1024, 1024], P(None, 'hid'), may hold values from -0.1875 to 0.1875
- w_attn_out: bfloat16 [1024, 1024], P('hid'), may hold values from -0.1875 to 0.1875
- cache: bfloat16 [2048, 2, 16, 1024], P('req', None, None, 'hid'), may hold values from -48 to 48
- cache_lens: int32 [2048], P('req'), may hold values from 1 to 16
- seg_ids: int32 [64, 96], P('req'), may hold values from 0 to 3, never falling along the last dimension, each value on 1 to 48 neighbouring positions
- ffn_gain: float32 [1024], replicated, may hold values from 0.25 to 1.75
- router: bfloat16 [1024, 16], replicated, may hold values from -0.078125 to 0.078125
- routes: int32 [8192, 2], P('req'), may hold values from 0 to 15, all different within a row; in each aligned block of 16 rows (0 to 15, 16 to 31, ...) at most 3 rows name the same one
- w_in: bfloat16 [2, 1024, 45056], P(None, None, ('req', 'hid')), may hold values from -0.1875 to 0.1875
- w_out: bfloat16 [45056, 1024], P('req'), may hold values from -0.109375 to 0.109375
Outputs:
- layer_out: bfloat16 [8192, 1024], P(('req', 'hid'))
Inputs may be any that keep to these rules, and one draw needn't show every extreme that they name: `routes`: in every aligned block of 16 rows no expert is named more than 3 times, so no assignment is dropped.
All inputs are finite; a program needn't handle non-finite values.
Results may differ from a plain program's by a relative error of at most 0.012.
The roundings to bfloat16 on the way count: a program that leaves them out, or rounds other values in their place, can miss the bound.
Values may be sent and summed in bfloat16 or wider, within the bound.
No kernel may reach another device: no remote copies, remote signals or barrier semaphores. Data moves between devices by JAX's collectives and lax.ppermute only.
A program may use at most 64 MiB of HBM per device.

v0:
```python
import functools

import jax
import jax.numpy as jnp
from jax import lax
from jax.experimental import pallas as pl
from jax.experimental.pallas import tpu as pltpu
from jax.sharding import Mesh
from jax.sharding import PartitionSpec as P

HDIM = 64
EPS = 1e-06
BF = jnp.bfloat16
F32 = jnp.float32
LANES = 128
CAPACITY = 3


def dot(a, b):
    return jnp.dot(a, b, preferred_element_type=F32)


def dot_nt(a, b):
    return lax.dot_general(a, b, (((1,), (1,)), ((), ())), preferred_element_type=F32)


def dot_tn(a, b):
    return lax.dot_general(a, b, (((0,), (0,)), ((), ())), preferred_element_type=F32)


def iota(shape, dim):
    return lax.broadcasted_iota(jnp.int32, shape, dim)


def to_column(row, size):
    diagonal = iota((size, size), 0) == iota((size, size), 1)
    return jnp.sum(jnp.where(diagonal, jnp.broadcast_to(row, (size, size)), 0), axis=1, keepdims=True)


def attention_kernel(
    index_ref, resid_hbm, gain_hbm, wq_hbm, wk_hbm, wv_hbm, wo_hbm, cache_hbm, lens_hbm, seg_hbm,
    ffn_gain_hbm, router_hbm, out_ref, own_ref, ffn_gain_ref, router_ref,
    resid_ref, gain_ref, wq_ref, wk_ref, wv_ref, wo_ref, cache_ref, lens_ref, seg_ref, seg_row, sems
):
    sources = (
        resid_hbm, gain_hbm, wq_hbm, wk_hbm, wv_hbm, seg_hbm, lens_hbm, cache_hbm, wo_hbm, ffn_gain_hbm, router_hbm
    )
    targets = (
        resid_ref, gain_ref, wq_ref, wk_ref, wv_ref, seg_ref, lens_ref, cache_ref, wo_ref, ffn_gain_ref, router_ref
    )
    copies = [pltpu.make_async_copy(a, b, sems.at[i]) for i, (a, b) in enumerate(zip(sources, targets))]
    for copy in copies:
        copy.start()
    total = resid_ref.shape[0]
    packed = seg_ref.shape[1]
    decoded, _, slots, width = cache_ref.shape
    heads = width // HDIM
    scale = HDIM ** (-0.5)
    copies[0].wait()
    copies[1].wait()
    x = resid_ref[...].astype(F32)
    inverse = lax.rsqrt(jnp.mean(x * x, axis=-1, keepdims=True) + EPS)
    normed = (x * inverse * gain_ref[...]).astype(BF)
    copies[2].wait()
    query = dot(normed, wq_ref[...]).astype(BF)
    copies[3].wait()
    keys = dot(normed, wk_ref[...]).astype(BF)
    copies[4].wait()
    values = dot(normed, wv_ref[...]).astype(BF)
    copies[5].wait()
    copies[6].wait()
    copies[7].wait()

    seg_row[...] = iota((1, total), 1) + (1 << 20)
    seg_row[:, :packed] = seg_ref[...]
    segments = seg_row[...]
    allowed = (iota((total, total), 1) <= iota((total, total), 0)) & (to_column(segments, total) == segments)
    lengths = to_column(lens_ref[...], decoded)
    slot_at = iota((decoded, decoded * slots), 1)
    own_cache = (slot_at // slots == iota((decoded, decoded * slots), 0)) & (slot_at % slots < lengths)

    cached_keys = cache_ref[:, 0].reshape(decoded * slots, width)
    cached_values = cache_ref[:, 1].reshape(decoded * slots, width)
    lane_head = iota((total, width), 1) // HDIM
    context = jnp.zeros((total, width), F32)
    for head in range(heads):
        mine = lane_head == head
        head_query = jnp.where(mine, query, jnp.zeros_like(query))
        scores = jnp.where(allowed, dot_nt(head_query, keys) * scale, -jnp.inf)
        highest = jnp.max(scores, axis=-1, keepdims=True)
        cached = jnp.where(own_cache, dot_nt(head_query[packed:], cached_keys) * scale, -jnp.inf)
        top_dec = jnp.maximum(highest[packed:], jnp.max(cached, axis=-1, keepdims=True))
        highest = jnp.concatenate([highest[:packed], top_dec], axis=0)
        weights = jnp.exp(scores - highest)
        weights_cache = jnp.exp(cached - top_dec)
        norm = jnp.sum(weights, axis=-1, keepdims=True)
        norm_dec = norm[packed:] + jnp.sum(weights_cache, axis=-1, keepdims=True)
        norm = jnp.concatenate([norm[:packed], norm_dec], axis=0)
        part = dot((weights / norm).astype(BF), values)
        part_cache = dot((weights_cache / norm_dec).astype(BF), cached_values)
        part = jnp.concatenate([part[:packed], part[packed:] + part_cache], axis=0)
        context = jnp.where(mine, part, context)
    copies[8].wait()
    out_ref[...] = dot(context.astype(BF), wo_ref[...]).astype(out_ref.dtype)

    block = own_ref.shape[0]
    index = index_ref[0]
    own_ref[...] = resid_ref[pl.ds(pl.multiple_of(index * block, block), block), :].astype(F32)
    copies[9].wait()
    copies[10].wait()


def own_routes(routes_ref, which, index, block):
    lane = iota((1, LANES), 1)
    row = pltpu.roll(routes_ref[pl.ds(which, 1), :], (LANES - index * block) % LANES, 1)
    size = block
    while size < LANES:
        row = jnp.where(lane < size, row, pltpu.roll(row, size, 1))
        size *= 2
    return row


def placement(row, columns, block, capacity):
    token = iota((block, LANES), 1) % block
    before = iota((block, LANES), 0) < token
    slot = jnp.zeros((1, LANES), jnp.int32)
    for column in columns:
        slot = slot + jnp.sum(((column == row) & before).astype(jnp.int32), axis=0, keepdims=True)
    return row * capacity + slot


def slot_rows(rows, capacity, chunks):
    at = iota((rows, LANES), 0)
    expert = at // (chunks * capacity)
    rest = at - expert * (chunks * capacity)
    chunk = rest // capacity
    return expert * capacity + rest - chunk * capacity, chunk


def route_columns(rows, block):
    size = (block, LANES)
    diagonal = iota(size, 0) == iota(size, 1)
    return [
        jnp.sum(jnp.where(diagonal, jnp.broadcast_to(row, size), 0), axis=1, keepdims=True) for row in rows
    ]


def routing_kernel(index_ref, routes_ref, gain_ref, chosen_ref, select_ref, column_ref):
    block = column_ref.shape[1]
    chunks = gain_ref.shape[1] // LANES
    rows = [own_routes(routes_ref, which, index_ref[0], block) for which in range(2)]
    columns = route_columns(rows, block)
    wanted, chunk = slot_rows(chosen_ref.shape[0], CAPACITY, chunks)
    same = chunk == iota(chunk.shape, 1) // block
    both = None
    for which in range(2):
        target = placement(rows[which], columns, block, CAPACITY)
        here = jnp.where(same & (wanted == target), 1.0, 0.0)
        select_ref[which] = here.astype(BF)
        both = here if both is None else both + here
        column_ref[which] = jnp.broadcast_to(columns[which], (block, LANES))
    chosen_ref[...] = both.astype(BF)


def dispatch_kernel(parts_ref, own_ref, gain_ref, chosen_ref, out_ref, after_ref, ffn_in_ref):
    sources, block, width = parts_ref.shape
    chunks = width // LANES
    mixed = parts_ref[0].astype(F32)
    for source in range(1, sources):
        mixed = mixed + parts_ref[source].astype(F32)
    after = own_ref[...] + mixed
    after_ref[...] = after
    inverse = lax.rsqrt(jnp.mean(after * after, axis=-1, keepdims=True) + EPS)
    ffn_in = (after * inverse * gain_ref[...]).astype(BF)
    ffn_in_ref[...] = ffn_in
    stacked = jnp.concatenate([ffn_in[:, at * LANES : (at + 1) * LANES] for at in range(chunks)], axis=0)
    out_ref[...] = dot(chosen_ref[...], stacked).astype(BF)


def gates_kernel(ffn_in_ref, router_ref, column_ref, gates_ref):
    block = ffn_in_ref.shape[0]
    experts = router_ref.shape[0]
    logits = dot_nt(ffn_in_ref[...], router_ref[...])
    expert_at = iota((block, experts), 1)
    for which in range(2):
        mine = expert_at == column_ref[which][:, :experts]
        picked = jnp.sum(jnp.where(mine, logits, 0.0), axis=1, keepdims=True)
        gates_ref[which] = jnp.broadcast_to(jax.nn.sigmoid(picked), (block, LANES))


def order_kernel(chunks, tokens_ref, order_ref):
    chunk_rows = order_ref.shape[0]
    each = chunk_rows // chunks
    at = iota((chunk_rows, chunk_rows), 0)
    chunk = at // each
    rest = at - chunk * each
    source = rest // CAPACITY
    wanted = source * (chunks * CAPACITY) + chunk * CAPACITY + rest - source * CAPACITY
    order_ref[...] = jnp.where(wanted == iota((chunk_rows, chunk_rows), 1), 1.0, 0.0).astype(BF)


def unpack_kernel(tokens_ref, order_ref, rows_ref):
    groups, chunk_rows, _ = tokens_ref.shape
    chunks = rows_ref.shape[1] // LANES
    each = chunk_rows // chunks
    for group in range(groups):
        unpacked = dot(order_ref[...], tokens_ref[group]).astype(BF)
        for at in range(chunks):
            rows_ref[group * each : (group + 1) * each, at * LANES : (at + 1) * LANES] = unpacked[
                at * each : (at + 1) * each
            ]


def ffn_kernel(index_ref, rows_ref, order_ref, down_ref, *refs):
    *pieces, out_ref, total_ref = refs
    groups, chunk_rows, _ = out_ref.shape
    width = rows_ref.shape[1]
    chunks = width // LANES
    each = chunk_rows // chunks
    chips = len(pieces) // 2
    both = pieces[0].shape[0]
    columns = both // 2
    core = index_ref[0] % 2
    chip = index_ref[0] // 2

    def experts_part(first, second):
        total = None
        for shift in range(chips):
            came = (chip - shift + chips) % chips
            hidden = []
            for piece in (first[shift], second[shift]):
                projected = dot_nt(rows_ref[...], piece[...])
                gate_val, up_val = projected[:, :columns], projected[:, columns:]
                hidden.append(jax.nn.gelu(gate_val, approximate=True) * up_val)
            hidden = jnp.concatenate(hidden, axis=1).astype(BF)
            part = dot(hidden, down_ref[pl.ds(pl.multiple_of(came * both, 16), both), :])
            total = part if total is None else total + part
        total_ref[...] = total.astype(BF)

    @pl.when(core == 0)
    def _():
        experts_part(pieces[:chips], pieces[chips:])

    @pl.when(core != 0)
    def _():
        experts_part(pieces[chips:], pieces[:chips])

    for group in range(groups):
        mine = total_ref[group * each : (group + 1) * each]
        stacked = jnp.concatenate([mine[:, at * LANES : (at + 1) * LANES] for at in range(chunks)], axis=0)
        out_ref[group] = dot_tn(order_ref[...], stacked).astype(BF)


def sum_kernel(parts_ref, out_ref):
    total = parts_ref[0].astype(F32)
    for at in range(1, parts_ref.shape[0]):
        total = total + parts_ref[at].astype(F32)
    out_ref[...] = total.astype(BF)


def combine_kernel(experts_ref, after_ref, gates_ref, select_ref, out_ref):
    block, width = after_ref.shape
    chunks = width // LANES
    picked = [dot_tn(select_ref[which], experts_ref[...]) for which in range(2)]
    for at in range(chunks):
        lanes = slice(at * LANES, (at + 1) * LANES)
        mine = slice(at * block, (at + 1) * block)
        total = gates_ref[0] * picked[0][mine] + gates_ref[1] * picked[1][mine]
        out_ref[:, lanes] = (after_ref[:, lanes] + total).astype(BF)


VMEM = pl.BlockSpec(memory_space=pltpu.VMEM)
HBM = pl.BlockSpec(memory_space=pltpu.HBM)
SMEM = pl.BlockSpec(memory_space=pltpu.SMEM)


def in_hbm(array):
    return pltpu.with_memory_space_constraint(array, pltpu.HBM)


PARAMS = pltpu.CompilerParams(vmem_limit_bytes=16 * 1024 * 1024)


def body(
    resid, attn_gain, w_query, w_key, w_value, w_attn_out, cache, cache_lens, seg_ids, ffn_gain, router, routes, w_in, w_out
):
    hid = ("x", "c")
    hid_count = lax.axis_size(hid)
    hid_index = lax.axis_index(hid).astype(jnp.int32).reshape(1)
    group_rows, width = resid.shape
    experts = router.shape[1]
    block = group_rows // hid_count
    capacity = CAPACITY
    chunks = width // LANES
    slot_count = experts * chunks * capacity
    split = lax.axis_size("y")
    w_cols = jnp.transpose(w_in, (0, 2, 1))
    row = lax.axis_size("x")

    operands = (
        resid,
        attn_gain.reshape(1, width),
        w_query,
        w_key,
        w_value,
        w_attn_out,
        cache,
        cache_lens.reshape(1, -1),
        seg_ids,
        ffn_gain.reshape(1, width),
        router.T,
    )
    partial_mix, own, gain, router_rows = pl.pallas_call(
        attention_kernel,
        out_shape=(
            jax.ShapeDtypeStruct((group_rows, width), BF),
            jax.ShapeDtypeStruct((block, width), F32),
            jax.ShapeDtypeStruct((1, width), F32),
            jax.ShapeDtypeStruct((experts, width), BF),
        ),
        in_specs=[SMEM] + [HBM] * len(operands),
        out_specs=(VMEM,) * 4,
        scratch_shapes=[pltpu.VMEM(each.shape, each.dtype) for each in operands[:9]]
        + [pltpu.VMEM((1, group_rows), jnp.int32), pltpu.SemaphoreType.DMA((len(operands),))],
        compiler_params=PARAMS,
        name="attention",
    )(hid_index, *map(in_hbm, operands))
    chosen, select, column = pl.pallas_call(
        routing_kernel,
        out_shape=(
            jax.ShapeDtypeStruct((slot_count, LANES), BF),
            jax.ShapeDtypeStruct((2, slot_count, LANES), BF),
            jax.ShapeDtypeStruct((2, block, LANES), jnp.int32),
        ),
        in_specs=[SMEM, VMEM, VMEM],
        out_specs=(VMEM,) * 3,
        compiler_params=PARAMS,
        name="routing",
    )(hid_index, routes.T, gain)
    parts = lax.all_to_all(partial_mix.reshape(hid_count, block, width), hid, 0, 0, tiled=True)
    outgoing, after, ffn_in = pl.pallas_call(
        dispatch_kernel,
        out_shape=(
            jax.ShapeDtypeStruct((slot_count, LANES), BF),
            jax.ShapeDtypeStruct((block, width), F32),
            jax.ShapeDtypeStruct((block, width), BF),
        ),
        in_specs=[VMEM] * 4,
        out_specs=(VMEM,) * 3,
        compiler_params=PARAMS,
        name="dispatch",
    )(parts, own, gain, chosen)
    gates = pl.pallas_call(
        gates_kernel,
        out_shape=jax.ShapeDtypeStruct((2, block, LANES), F32),
        in_specs=[VMEM] * 3,
        out_specs=VMEM,
        compiler_params=PARAMS,
        name="gates",
    )(ffn_in, router_rows, column)
    gates, w_cols = lax.optimization_barrier((gates, w_cols))
    exchanged = (experts, chunks * CAPACITY, LANES)
    arrived = lax.all_to_all(outgoing.reshape(exchanged), "z", 0, 0, tiled=True)
    own_core = [w_cols]
    for shift in range(1, row):
        own_core.append(lax.ppermute(w_cols, "x", [(at, (at + shift) % row) for at in range(row)]))
    spread = jnp.broadcast_to(arrived.reshape(1, slot_count, LANES), (split, slot_count, LANES))
    order = pl.pallas_call(
        functools.partial(order_kernel, chunks),
        out_shape=jax.ShapeDtypeStruct((slot_count, slot_count), BF),
        in_specs=[VMEM],
        out_specs=VMEM,
        compiler_params=PARAMS,
        name="order",
    )(spread)
    order, *own_core = lax.optimization_barrier((order, *own_core))
    other_core = [lax.ppermute(cols, "c", [(0, 1), (1, 0)]) for cols in own_core]
    tokens = lax.all_to_all(spread, "y", 0, 0, tiled=True)
    rows = pl.pallas_call(
        unpack_kernel,
        out_shape=jax.ShapeDtypeStruct((split * experts * CAPACITY, width), BF),
        in_specs=[VMEM] * 2,
        out_specs=VMEM,
        compiler_params=PARAMS,
        cost_estimate=pl.CostEstimate(flops=10**10, transcendentals=0, bytes_accessed=1 << 21),
        name="unpack",
    )(tokens, order)
    pieces = [cols.reshape(-1, width) for cols in (*own_core, *other_core)]
    projected = pl.pallas_call(
        ffn_kernel,
        out_shape=jax.ShapeDtypeStruct((split, slot_count, LANES), BF),
        in_specs=[SMEM] + [VMEM] * (3 + len(pieces)),
        out_specs=VMEM,
        scratch_shapes=[pltpu.VMEM((split * experts * CAPACITY, width), BF)],
        compiler_params=PARAMS,
        name="ffn",
    )(hid_index, rows, order, w_out, *pieces)
    quarters = lax.all_to_all(projected, "y", 0, 0, tiled=True)
    summed = pl.pallas_call(
        sum_kernel,
        out_shape=jax.ShapeDtypeStruct((slot_count, LANES), BF),
        in_specs=[VMEM],
        out_specs=VMEM,
        compiler_params=PARAMS,
        name="sum_quarters",
    )(quarters)
    returned = lax.all_to_all(summed.reshape(exchanged), "z", 0, 0, tiled=True)
    return pl.pallas_call(
        combine_kernel,
        out_shape=jax.ShapeDtypeStruct((block, width), BF),
        in_specs=[VMEM] * 4,
        out_specs=VMEM,
        compiler_params=PARAMS,
        name="combine",
    )(returned.reshape(slot_count, LANES), after, gates, select)


def solution(mesh):
    fine = Mesh(mesh.devices.reshape(16, 4, 4, 2), ("z", "y", "x", "c"))
    req = ("z", "y")
    hid = ("x", "c")
    in_specs = (
        P(req, None),
        P(),
        P(None, hid),
        P(None, hid),
        P(None, hid),
        P(hid, None),
        P(req, None, None, hid),
        P(req),
        P(req, None),
        P(),
        P(),
        P(req, None),
        P(None, None, req + hid),
        P(req, None),
    )
    out_specs = P(req + hid, None)
    return jax.shard_map(body, mesh=fine, in_specs=in_specs, out_specs=out_specs, check_vma=False)
```

profile of v0, /device:TPU:6, one launch (start us, length us, event | category | flops | bytes accessed | tf_op | source)
XLA Modules:
  0.0 106.4 jit_solution(14076290527470829503)
XLA Ops:
  0.0 0.0 copy-start.2
  0.0 0.0 copy-start.1
  0.0 4.0 %attention.1 = (bf16[128,1024]{1,0:T(8,128)(2,1)}, f32[16,1024]{1,0:T(8,128)S(1)}, f32[1,1024]{1,0:T(1,128)S(1)}, bf16[16,1024]{1,0:T(8,128)(2,1)S(1)}) custom-call(s32[1]{0:T(128)} %bitcast.index_ref, bf16[128,1024]{1,0:T(8,128)(2,1)} %resid_hbm.1, f32[1,1024]{1,0:T(1,128)} %bitcast.32, bf16[1024,128]{1,0:T(8,128)(2,1)} %wq_hbm.1, ...), custom_call_target="tpu_custom_call" | custom-call | tf_op jit(solution)/shard_map/attention/pallas_call | solution.py:313
  4.0 9.2 %all-to-all-start = ((bf16[8,16,1024]{2,1,0:T(8,128)(2,1)}), bf16[8,16,1024]{2,1,0:T(8,128)(2,1)S(1)}, u32[]{:S(2)}, u32[]{:S(2)}) async-start(bf16[8,16,1024]{2,1,0:T(8,128)(2,1)} %bitcast.5), calls=%async_computation | async-start | bytes 524288 | tf_op jit(solution)/shard_map/all_to_all | solution.py:340
  13.2 0.0 copy-done.2
  13.2 0.6 routing.1
  13.9 4.8 %all-to-all-done.parts_ref = bf16[8,16,1024]{2,1,0:T(8,128)(2,1)S(1)} async-done(((bf16[8,16,1024]{2,1,0:T(8,128)(2,1)}), bf16[8,16,1024]{2,1,0:T(8,128)(2,1)S(1)}, u32[]{:S(2)}, u32[]{:S(2)}) %all-to-all-start) | async-done | bytes 262176 | tf_op jit(solution)/shard_map/all_to_all | solution.py:340
  18.7 0.9 dispatch.1
  19.6 10.8 %all-to-all-start.1 = ((bf16[16,24,128]{2,1,0:T(8,128)(2,1)}), bf16[16,24,128]{2,1,0:T(8,128)(2,1)S(1)}, u32[]{:S(2)}, u32[]{:S(2)}) async-start(bf16[16,24,128]{2,1,0:T(8,128)(2,1)} %bitcast.7), calls=%async_computation.1 | async-start | bytes 196608 | tf_op jit(solution)/shard_map/all_to_all | solution.py:363
  30.4 0.2 gates.1.gates_ref
  30.6 0.0 copy-done.1
  30.6 1.9 %collective-permute-start.2 = (bf16[2,88,1024]{2,1,0:T(8,128)(2,1)S(1)}, bf16[2,88,1024]{2,1,0:T(8,128)(2,1)S(1)}, u32[]{:S(2)}, u32[]{:S(2)}) collective-permute-start(bf16[2,88,1024]{2,1,0:T(8,128)(2,1)S(1)} %bitcast.22), channel_id=1, source_target_pairs={{0,6},{2,0},{4,2},{6,4},{1,7},{3,1},{5,3},{7,5},{8,14},{10,8},{12,... | collective-permute-start | bytes 1081352 | tf_op jit(solution)/shard_map/ppermute | solution.py:366
  32.6 5.4 %collective-permute-start.1 = (bf16[2,88,1024]{2,1,0:T(8,128)(2,1)S(1)}, bf16[2,88,1024]{2,1,0:T(8,128)(2,1)S(1)}, u32[]{:S(2)}, u32[]{:S(2)}) collective-permute-start(bf16[2,88,1024]{2,1,0:T(8,128)(2,1)S(1)} %bitcast.23), channel_id=1, source_target_pairs={{0,4},{2,6},{4,0},{6,2},{1,5},{3,7},{5,1},{7,3},{8,12},{10,14},{12... | collective-permute-start | bytes 1081352 | tf_op jit(solution)/shard_map/ppermute | solution.py:366
  38.0 3.1 %collective-permute-start = (bf16[2,88,1024]{2,1,0:T(8,128)(2,1)S(1)}, bf16[2,88,1024]{2,1,0:T(8,128)(2,1)}, u32[]{:S(2)}, u32[]{:S(2)}) collective-permute-start(bf16[2,88,1024]{2,1,0:T(8,128)(2,1)S(1)} %bitcast.24), channel_id=1, source_target_pairs={{0,2},{2,4},{4,6},{6,0},{1,3},{3,5},{5,7},{7,1},{8,10},{10,12},{12... | collective-permute-start | bytes 1081352 | tf_op jit(solution)/shard_map/ppermute | solution.py:366
  41.1 2.5 %all-to-all-done.1 = bf16[16,24,128]{2,1,0:T(8,128)(2,1)S(1)} async-done(((bf16[16,24,128]{2,1,0:T(8,128)(2,1)}), bf16[16,24,128]{2,1,0:T(8,128)(2,1)S(1)}, u32[]{:S(2)}, u32[]{:S(2)}) %all-to-all-start.1) | async-done | bytes 98336 | tf_op jit(solution)/shard_map/all_to_all | solution.py:363
  43.6 0.8 broadcast_in_dim.8.tokens_ref
  44.4 4.5 %all-to-all-start.2 = ((bf16[4,384,128]{2,1,0:T(8,128)(2,1)}), bf16[4,384,128]{2,1,0:T(8,128)(2,1)S(1)}, u32[]{:S(2)}, u32[]{:S(2)}) async-start(bf16[4,384,128]{2,1,0:T(8,128)(2,1)} %broadcast_in_dim.8.tokens_ref), calls=%async_computation.2 | async-start | bytes 786432 | tf_op jit(solution)/shard_map/all_to_all | solution.py:378
  48.9 1.3 %order.1.order_ref = bf16[384,384]{1,0:T(8,128)(2,1)S(1)} custom-call(bf16[4,384,128]{2,1,0:T(8,128)(2,1)} %broadcast_in_dim.8.tokens_ref), custom_call_target="tpu_custom_call" | custom-call | tf_op jit(solution)/shard_map/order/pallas_call | solution.py:368
  50.2 0.0 copy-start
  50.2 0.0 collective-permute-done.2
  50.2 1.1 %collective-permute-done.1 = bf16[2,88,1024]{2,1,0:T(8,128)(2,1)S(1)} collective-permute-done((bf16[2,88,1024]{2,1,0:T(8,128)(2,1)S(1)}, bf16[2,88,1024]{2,1,0:T(8,128)(2,1)S(1)}, u32[]{:S(2)}, u32[]{:S(2)}) %collective-permute-start.1) | collective-permute-done | bytes 360480 | tf_op jit(solution)/shard_map/ppermute | solution.py:366
  51.3 2.3 %collective-permute-done = bf16[2,88,1024]{2,1,0:T(8,128)(2,1)} collective-permute-done((bf16[2,88,1024]{2,1,0:T(8,128)(2,1)S(1)}, bf16[2,88,1024]{2,1,0:T(8,128)(2,1)}, u32[]{:S(2)}, u32[]{:S(2)}) %collective-permute-start) | collective-permute-done | bytes 360480 | tf_op jit(solution)/shard_map/ppermute | solution.py:366
  53.6 1.9 %collective-permute-start.3 = (bf16[2,88,1024]{2,1,0:T(8,128)(2,1)S(1)}, bf16[2,88,1024]{2,1,0:T(8,128)(2,1)}, u32[]{:S(2)}, u32[]{:S(2)}) collective-permute-start(bf16[2,88,1024]{2,1,0:T(8,128)(2,1)S(1)} %bitcast.25), channel_id=1, source_target_pairs={{0,1},{1,0},{2,3},{3,2},{4,5},{5,4},{6,7},{7,6},{8,9},{9,8},{10,11... | collective-permute-start | bytes 1081352 | tf_op jit(solution)/shard_map/ppermute | solution.py:377
  55.5 2.4 %collective-permute-start.4 = (bf16[2,88,1024]{2,1,0:T(8,128)(2,1)}, bf16[2,88,1024]{2,1,0:T(8,128)(2,1)}, u32[]{:S(2)}, u32[]{:S(2)}) collective-permute-start(bf16[2,88,1024]{2,1,0:T(8,128)(2,1)} %collective-permute-done), channel_id=1, source_target_pairs={{0,1},{1,0},{2,3},{3,2},{4,5},{5,4},{6,7},{7,6},{8,9},{9,8},{10,11... | collective-permute-start | bytes 1081352 | tf_op jit(solution)/shard_map/ppermute | solution.py:377
  57.9 1.9 %collective-permute-start.5 = (bf16[2,88,1024]{2,1,0:T(8,128)(2,1)S(1)}, bf16[2,88,1024]{2,1,0:T(8,128)(2,1)}, u32[]{:S(2)}, u32[]{:S(2)}) collective-permute-start(bf16[2,88,1024]{2,1,0:T(8,128)(2,1)S(1)} %collective-permute-done.1), channel_id=1, source_target_pairs={{0,1},{1,0},{2,3},{3,2},{4,5},{5,4},{6,7},{7,6},{8,9},{9,8},{10,11... | collective-permute-start | bytes 1081352 | tf_op jit(solution)/shard_map/ppermute | solution.py:377
  59.9 2.4 %collective-permute-start.6 = (bf16[2,88,1024]{2,1,0:T(8,128)(2,1)S(1)}, bf16[2,88,1024]{2,1,0:T(8,128)(2,1)}, u32[]{:S(2)}, u32[]{:S(2)}) collective-permute-start(bf16[2,88,1024]{2,1,0:T(8,128)(2,1)S(1)} %collective-permute-done.2), channel_id=1, source_target_pairs={{0,1},{1,0},{2,3},{3,2},{4,5},{5,4},{6,7},{7,6},{8,9},{9,8},{10,11... | collective-permute-start | bytes 1081352 | tf_op jit(solution)/shard_map/ppermute | solution.py:377
  62.3 0.0 all-to-all-done.2.tokens_ref
  62.3 0.5 unpack.1.rows_ref
  62.8 0.0 collective-permute-done.3
  62.8 0.0 collective-permute-done.4
  62.8 0.0 collective-permute-done.5
  62.8 0.9 collective-permute-done.6
  63.7 0.0 copy-done
  63.7 4.1 %ffn.1 = bf16[4,384,128]{2,1,0:T(8,128)(2,1)S(1)} custom-call(s32[1]{0:T(128)} %bitcast.index_ref, bf16[192,1024]{1,0:T(8,128)(2,1)S(1)} %unpack.1.rows_ref, bf16[384,384]{1,0:T(8,128)(2,1)S(1)} %order.1.order_ref, bf16[704,1024]{1,0:T(8,128)(2,1)S(1)} %copy-done, bf16[176,1024]{1,0:T(8,128)(2,1)S(1)} %bitcast.26, bf16[176,1024]{1,0:T(8,128)(2,1)} %bitcast.11.refs_1_, ...), custom_call_target="tpu_custom_call" | custom-call | tf_op jit(solution)/shard_map/ffn/pallas_call | solution.py:389
  67.8 12.9 %all_to_all.25.parts_ref = bf16[4,384,128]{2,1,0:T(8,128)(2,1)S(1)} all-to-all(bf16[4,384,128]{2,1,0:T(8,128)(2,1)S(1)} %ffn.1), channel_id=1, replica_groups=mesh['z'=16,'y'=4,'x'=4,'c'=2] {'y'}, dimensions={0} | all-to-all | bytes 786432 | tf_op jit(solution)/shard_map/all_to_all | solution.py:398
  80.7 0.1 sum_quarters.1
  80.8 24.8 %all_to_all.26 = bf16[16,24,128]{2,1,0:T(8,128)(2,1)S(1)} all-to-all(bf16[16,24,128]{2,1,0:T(8,128)(2,1)S(1)} %bitcast.21), channel_id=1, replica_groups=mesh['z'=16,'y'=4,'x'=4,'c'=2] {'z'}, dimensions={0} | all-to-all | bytes 196608 | tf_op jit(solution)/shard_map/all_to_all | solution.py:407
  105.5 0.9 combine.1
Async XLA Ops:
  0.0 13.2 %copy-start.2 = (s32[128,2]{0,1:T(2,128)S(1)}, s32[128,2]{0,1:T(2,128)}, u32[]{:S(2)}) copy-start(s32[128,2]{0,1:T(2,128)} %param.25) | copy-start | bytes 3076
  0.0 30.6 %copy-start.1 = (bf16[2,1024,88]{1,2,0:T(8,128)(2,1)S(1)}, bf16[2,1024,88]{1,2,0:T(8,128)(2,1)}, u32[]{:S(2)}) copy-start(bf16[2,1024,88]{1,2,0:T(8,128)(2,1)} %param.26) | copy-start | bytes 1081348
  4.0 14.7 %all-to-all-start = ((bf16[8,16,1024]{2,1,0:T(8,128)(2,1)}), bf16[8,16,1024]{2,1,0:T(8,128)(2,1)S(1)}, u32[]{:S(2)}, u32[]{:S(2)}) async-start(bf16[8,16,1024]{2,1,0:T(8,128)(2,1)} %bitcast.5), calls=%async_computation | async-start | bytes 524288 | tf_op jit(solution)/shard_map/all_to_all | solution.py:340
  19.6 24.0 %all-to-all-start.1 = ((bf16[16,24,128]{2,1,0:T(8,128)(2,1)}), bf16[16,24,128]{2,1,0:T(8,128)(2,1)S(1)}, u32[]{:S(2)}, u32[]{:S(2)}) async-start(bf16[16,24,128]{2,1,0:T(8,128)(2,1)} %bitcast.7), calls=%async_computation.1 | async-start | bytes 196608 | tf_op jit(solution)/shard_map/all_to_all | solution.py:363
  30.6 19.5 %collective-permute-start.2 = (bf16[2,88,1024]{2,1,0:T(8,128)(2,1)S(1)}, bf16[2,88,1024]{2,1,0:T(8,128)(2,1)S(1)}, u32[]{:S(2)}, u32[]{:S(2)}) collective-permute-start(bf16[2,88,1024]{2,1,0:T(8,128)(2,1)S(1)} %bitcast.22), channel_id=1, source_target_pairs={{0,6},{2,0},{4,2},{6,4},{1,7},{3,1},{5,3},{7,5},{8,14},{10,8},{12,... | collective-permute-start | bytes 1081352 | tf_op jit(solution)/shard_map/ppermute | solution.py:366
  32.6 18.7 %collective-permute-start.1 = (bf16[2,88,1024]{2,1,0:T(8,128)(2,1)S(1)}, bf16[2,88,1024]{2,1,0:T(8,128)(2,1)S(1)}, u32[]{:S(2)}, u32[]{:S(2)}) collective-permute-start(bf16[2,88,1024]{2,1,0:T(8,128)(2,1)S(1)} %bitcast.23), channel_id=1, source_target_pairs={{0,4},{2,6},{4,0},{6,2},{1,5},{3,7},{5,1},{7,3},{8,12},{10,14},{12... | collective-permute-start | bytes 1081352 | tf_op jit(solution)/shard_map/ppermute | solution.py:366
  38.0 15.6 %collective-permute-start = (bf16[2,88,1024]{2,1,0:T(8,128)(2,1)S(1)}, bf16[2,88,1024]{2,1,0:T(8,128)(2,1)}, u32[]{:S(2)}, u32[]{:S(2)}) collective-permute-start(bf16[2,88,1024]{2,1,0:T(8,128)(2,1)S(1)} %bitcast.24), channel_id=1, source_target_pairs={{0,2},{2,4},{4,6},{6,0},{1,3},{3,5},{5,7},{7,1},{8,10},{10,12},{12... | collective-permute-start | bytes 1081352 | tf_op jit(solution)/shard_map/ppermute | solution.py:366
  44.4 17.9 %all-to-all-start.2 = ((bf16[4,384,128]{2,1,0:T(8,128)(2,1)}), bf16[4,384,128]{2,1,0:T(8,128)(2,1)S(1)}, u32[]{:S(2)}, u32[]{:S(2)}) async-start(bf16[4,384,128]{2,1,0:T(8,128)(2,1)} %broadcast_in_dim.8.tokens_ref), calls=%async_computation.2 | async-start | bytes 786432 | tf_op jit(solution)/shard_map/all_to_all | solution.py:378
  50.2 13.5 %copy-start = (bf16[704,1024]{1,0:T(8,128)(2,1)S(1)}, bf16[704,1024]{1,0:T(8,128)(2,1)}, u32[]{:S(2)}) copy-start(bf16[704,1024]{1,0:T(8,128)(2,1)} %down_ref.1) | copy-start | bytes 4325380
  53.6 9.2 %collective-permute-start.3 = (bf16[2,88,1024]{2,1,0:T(8,128)(2,1)S(1)}, bf16[2,88,1024]{2,1,0:T(8,128)(2,1)}, u32[]{:S(2)}, u32[]{:S(2)}) collective-permute-start(bf16[2,88,1024]{2,1,0:T(8,128)(2,1)S(1)} %bitcast.25), channel_id=1, source_target_pairs={{0,1},{1,0},{2,3},{3,2},{4,5},{5,4},{6,7},{7,6},{8,9},{9,8},{10,11... | collective-permute-start | bytes 1081352 | tf_op jit(solution)/shard_map/ppermute | solution.py:377
  55.5 7.3 %collective-permute-start.4 = (bf16[2,88,1024]{2,1,0:T(8,128)(2,1)}, bf16[2,88,1024]{2,1,0:T(8,128)(2,1)}, u32[]{:S(2)}, u32[]{:S(2)}) collective-permute-start(bf16[2,88,1024]{2,1,0:T(8,128)(2,1)} %collective-permute-done), channel_id=1, source_target_pairs={{0,1},{1,0},{2,3},{3,2},{4,5},{5,4},{6,7},{7,6},{8,9},{9,8},{10,11... | collective-permute-start | bytes 1081352 | tf_op jit(solution)/shard_map/ppermute | solution.py:377
  57.9 4.8 %collective-permute-start.5 = (bf16[2,88,1024]{2,1,0:T(8,128)(2,1)S(1)}, bf16[2,88,1024]{2,1,0:T(8,128)(2,1)}, u32[]{:S(2)}, u32[]{:S(2)}) collective-permute-start(bf16[2,88,1024]{2,1,0:T(8,128)(2,1)S(1)} %collective-permute-done.1), channel_id=1, source_target_pairs={{0,1},{1,0},{2,3},{3,2},{4,5},{5,4},{6,7},{7,6},{8,9},{9,8},{10,11... | collective-permute-start | bytes 1081352 | tf_op jit(solution)/shard_map/ppermute | solution.py:377
  59.9 3.8 %collective-permute-start.6 = (bf16[2,88,1024]{2,1,0:T(8,128)(2,1)S(1)}, bf16[2,88,1024]{2,1,0:T(8,128)(2,1)}, u32[]{:S(2)}, u32[]{:S(2)}) collective-permute-start(bf16[2,88,1024]{2,1,0:T(8,128)(2,1)S(1)} %collective-permute-done.2), channel_id=1, source_target_pairs={{0,1},{1,0},{2,3},{3,2},{4,5},{5,4},{6,7},{7,6},{8,9},{9,8},{10,11... | collective-permute-start | bytes 1081352 | tf_op jit(solution)/shard_map/ppermute | solution.py:377
where the time goes:
time: 108 us; the launch traced here: 106 us
  starting transfers between devices  43.6 us (40%)
  blocking collectives  37.6 us (35%)
  Pallas kernels  12.6 us (12%)
  waiting for transfers between devices  11.6 us (11%)
    all_to_all x1, blocking collectives, body(): returned = lax.all_to_all(summed.reshape(exchanged), 'z', 0, 0, tiled=True)  24.8 us
    all_to_all x1, blocking collectives, body(): quarters = lax.all_to_all(projected, 'y', 0, 0, tiled=True)  12.9 us
    all_to_all x1, starting transfers between devices, body(): arrived = lax.all_to_all(outgoing.reshape(exchanged), 'z', 0, 0, tiled=True)  10.8 us
    ppermute x3, starting transfers between devices, body(): lax.ppermute(w_cols, 'x', [(at, (at + shift) % row) for at in range(row)])  10.4 us
    all_to_all x1, starting transfers between devices, body(): lax.all_to_all(partial_mix.reshape(hid_count, block, width), hid, 0, 0, t...  9.21 us
    ppermute x4, starting transfers between devices, body(): lax.ppermute(cols, 'c', [(0, 1), (1, 0)])  8.65 us
    all_to_all x1, waiting for transfers between devices, body(): lax.all_to_all(partial_mix.reshape(hid_count, block, width), hid, 0, 0, t...  4.8 us
    all_to_all x1, starting transfers between devices, body(): tokens = lax.all_to_all(spread, 'y', 0, 0, tiled=True)  4.47 us
  transfers between devices with their start and end apart: 10, of which 5 were waited for; matrix products, arithmetic and copies ran while one was open for 1% of the time, Pallas kernels for 2%

commit v1 on v0

--- a/solution.py
+++ b/solution.py
@@ -162,18 +162,19 @@
     chosen_ref[...] = both.astype(BF)
 
 
-def dispatch_kernel(parts_ref, own_ref, gain_ref, chosen_ref, out_ref, after_ref, ffn_in_ref):
-    sources, block, width = parts_ref.shape
-    chunks = width // LANES
+def mix_kernel(parts_ref, own_ref, gain_ref, after_ref, ffn_in_ref):
     mixed = parts_ref[0].astype(F32)
-    for source in range(1, sources):
+    for source in range(1, parts_ref.shape[0]):
         mixed = mixed + parts_ref[source].astype(F32)
     after = own_ref[...] + mixed
     after_ref[...] = after
     inverse = lax.rsqrt(jnp.mean(after * after, axis=-1, keepdims=True) + EPS)
-    ffn_in = (after * inverse * gain_ref[...]).astype(BF)
-    ffn_in_ref[...] = ffn_in
-    stacked = jnp.concatenate([ffn_in[:, at * LANES : (at + 1) * LANES] for at in range(chunks)], axis=0)
+    ffn_in_ref[...] = (after * inverse * gain_ref[...]).astype(BF)
+
+
+def dispatch_kernel(ffn_in_ref, chosen_ref, out_ref):
+    chunks = ffn_in_ref.shape[1] // LANES
+    stacked = jnp.concatenate([ffn_in_ref[:, at * LANES : (at + 1) * LANES] for at in range(chunks)], axis=0)
     out_ref[...] = dot(chosen_ref[...], stacked).astype(BF)
 
 
@@ -278,6 +279,7 @@
     return pltpu.with_memory_space_constraint(array, pltpu.HBM)
 
 
+LONG = pl.CostEstimate(flops=10**10, transcendentals=0, bytes_accessed=1 << 21)
 PARAMS = pltpu.CompilerParams(vmem_limit_bytes=16 * 1024 * 1024)
 
 
@@ -337,19 +339,28 @@
         compiler_params=PARAMS,
         name="routing",
     )(hid_index, routes.T, gain)
+    column, w_cols = lax.optimization_barrier((column, w_cols))
+    before = lax.ppermute(w_cols, "x", [(at, (at + 1) % row) for at in range(row)])
+    after_it = lax.ppermute(w_cols, "x", [(at, (at - 1) % row) for at in range(row)])
     parts = lax.all_to_all(partial_mix.reshape(hid_count, block, width), hid, 0, 0, tiled=True)
-    outgoing, after, ffn_in = pl.pallas_call(
+    after, ffn_in = pl.pallas_call(
+        mix_kernel,
+        out_shape=(jax.ShapeDtypeStruct((block, width), F32), jax.ShapeDtypeStruct((block, width), BF)),
+        in_specs=[VMEM] * 3,
+        out_specs=(VMEM,) * 2,
+        compiler_params=PARAMS,
+        cost_estimate=LONG,
+        name="mix",
+    )(parts, own, gain)
+    ffn_in, before, after_it = lax.optimization_barrier((ffn_in, before, after_it))
+    outgoing = pl.pallas_call(
         dispatch_kernel,
-        out_shape=(
-            jax.ShapeDtypeStruct((slot_count, LANES), BF),
-            jax.ShapeDtypeStruct((block, width), F32),
-            jax.ShapeDtypeStruct((block, width), BF),
-        ),
-        in_specs=[VMEM] * 4,
-        out_specs=(VMEM,) * 3,
+        out_shape=jax.ShapeDtypeStruct((slot_count, LANES), BF),
+        in_specs=[VMEM] * 2,
+        out_specs=VMEM,
         compiler_params=PARAMS,
         name="dispatch",
-    )(parts, own, gain, chosen)
+    )(ffn_in, chosen)
     gates = pl.pallas_call(
         gates_kernel,
         out_shape=jax.ShapeDtypeStruct((2, block, LANES), F32),
@@ -358,13 +369,8 @@
         compiler_params=PARAMS,
         name="gates",
     )(ffn_in, router_rows, column)
-    gates, w_cols = lax.optimization_barrier((gates, w_cols))
     exchanged = (experts, chunks * CAPACITY, LANES)
     arrived = lax.all_to_all(outgoing.reshape(exchanged), "z", 0, 0, tiled=True)
-    own_core = [w_cols]
-    for shift in range(1, row):
-        own_core.append(lax.ppermute(w_cols, "x", [(at, (at + shift) % row) for at in range(row)]))
-    spread = jnp.broadcast_to(arrived.reshape(1, slot_count, LANES), (split, slot_count, LANES))
     order = pl.pallas_call(
         functools.partial(order_kernel, chunks),
         out_shape=jax.ShapeDtypeStruct((slot_count, slot_count), BF),
@@ -372,17 +378,19 @@
         out_specs=VMEM,
         compiler_params=PARAMS,
         name="order",
-    )(spread)
-    order, *own_core = lax.optimization_barrier((order, *own_core))
+    )(gates)
+    order, w_cols, before, after_it = lax.optimization_barrier((order, w_cols, before, after_it))
+    across = lax.ppermute(w_cols, "x", [(at, (at + 2) % row) for at in range(row)])
+    own_core = (w_cols, before, across, after_it)
     other_core = [lax.ppermute(cols, "c", [(0, 1), (1, 0)]) for cols in own_core]
-    tokens = lax.all_to_all(spread, "y", 0, 0, tiled=True)
+    tokens = lax.all_gather(arrived.reshape(slot_count, LANES), "y", axis=0)
     rows = pl.pallas_call(
         unpack_kernel,
         out_shape=jax.ShapeDtypeStruct((split * experts * CAPACITY, width), BF),
         in_specs=[VMEM] * 2,
         out_specs=VMEM,
         compiler_params=PARAMS,
-        cost_estimate=pl.CostEstimate(flops=10**10, transcendentals=0, bytes_accessed=1 << 21),
+        cost_estimate=LONG,
         name="unpack",
     )(tokens, order)
     pieces = [cols.reshape(-1, width) for cols in (*own_core, *other_core)]

time: 108 us -> 112 us (1.037)
  the two profiles are of different devices: /device:TPU:6 before, /device:TPU:32 now
where the time goes in v1:
time: 112 us
  blocking collectives  48.6 us (43%)
  starting transfers between devices  36.7 us (33%)
  waiting for transfers between devices  15.2 us (14%)
  Pallas kernels  10.1 us (9%)
    all_to_all x1, blocking collectives, body(): returned = lax.all_to_all(summed.reshape(exchanged), 'z', 0, 0, tiled=True)  24.2 us
    all_to_all x1, starting transfers between devices, body(): arrived = lax.all_to_all(outgoing.reshape(exchanged), 'z', 0, 0, tiled=True)  15.2 us
    all_gather x1, blocking collectives, body(): tokens = lax.all_gather(arrived.reshape(slot_count, LANES), 'y', axis=0)  13.1 us
    all_to_all x1, blocking collectives, body(): quarters = lax.all_to_all(projected, 'y', 0, 0, tiled=True)  11.3 us
    ppermute x4, starting transfers between devices, body(): lax.ppermute(cols, 'c', [(0, 1), (1, 0)])  8.16 us
    ppermute x1, waiting for transfers between devices, body(): lax.ppermute(w_cols, 'x', [(at, (at - 1) % row) for at in range(row)])  5.9 us
    ppermute x1, waiting for transfers between devices, body(): lax.ppermute(w_cols, 'x', [(at, (at + 1) % row) for at in range(row)])  5.33 us
    ppermute x1, starting transfers between devices, body(): lax.ppermute(w_cols, 'x', [(at, (at - 1) % row) for at in range(row)])  5.14 us
  transfers between devices with their start and end apart: 9, of which 3 were waited for; matrix products, arithmetic and copies ran while one was open for 0% of the time, Pallas kernels for 2%

profile of v1, /device:TPU:32, one launch (start us, length us, event | category | flops | bytes accessed | tf_op | source)
XLA Modules:
  0.0 111.6 jit_solution(15230875332674929757)
XLA Ops:
  0.0 0.0 copy-start.2
  0.0 0.0 copy-start.1
  0.0 4.0 %attention.1 = (bf16[128,1024]{1,0:T(8,128)(2,1)}, f32[16,1024]{1,0:T(8,128)S(1)}, f32[1,1024]{1,0:T(1,128)S(1)}, bf16[16,1024]{1,0:T(8,128)(2,1)S(1)}) custom-call(s32[1]{0:T(128)} %bitcast.index_ref, bf16[128,1024]{1,0:T(8,128)(2,1)} %resid_hbm.1, f32[1,1024]{1,0:T(1,128)} %bitcast.37, bf16[1024,128]{1,0:T(8,128)(2,1)} %wq_hbm.1, ...), custom_call_target="tpu_custom_call" | custom-call | tf_op jit(solution)/shard_map/attention/pallas_call | solution.py:315
  4.0 4.3 %all-to-all-start = ((bf16[8,16,1024]{2,1,0:T(8,128)(2,1)}), bf16[8,16,1024]{2,1,0:T(8,128)(2,1)S(1)}, u32[]{:S(2)}, u32[]{:S(2)}) async-start(bf16[8,16,1024]{2,1,0:T(8,128)(2,1)} %bitcast.5), calls=%async_computation | async-start | bytes 524288 | tf_op jit(solution)/shard_map/all_to_all | solution.py:345
  8.3 0.0 copy-done.2
  8.3 0.6 routing.1
  9.0 0.0 copy-done.1
  9.0 5.1 %collective-permute-start.1 = (bf16[2,88,1024]{2,1,0:T(8,128)(2,1)S(1)}, bf16[2,88,1024]{2,1,0:T(8,128)(2,1)S(1)}, u32[]{:S(2)}, u32[]{:S(2)}) collective-permute-start(bf16[2,88,1024]{2,1,0:T(8,128)(2,1)S(1)} %bitcast.22), channel_id=1, source_target_pairs={{0,6},{2,0},{4,2},{6,4},{1,7},{3,1},{5,3},{7,5},{8,14},{10,8},{12,... | collective-permute-start | bytes 1081352 | tf_op jit(solution)/shard_map/ppermute | solution.py:344
  14.1 1.9 %collective-permute-start = (bf16[2,88,1024]{2,1,0:T(8,128)(2,1)S(1)}, bf16[2,88,1024]{2,1,0:T(8,128)(2,1)S(1)}, u32[]{:S(2)}, u32[]{:S(2)}) collective-permute-start(bf16[2,88,1024]{2,1,0:T(8,128)(2,1)S(1)} %bitcast.23), channel_id=1, source_target_pairs={{0,2},{2,4},{4,6},{6,0},{1,3},{3,5},{5,7},{7,1},{8,10},{10,12},{12... | collective-permute-start | bytes 1081352 | tf_op jit(solution)/shard_map/ppermute | solution.py:343
  16.0 0.0 all-to-all-done.parts_ref
  16.1 0.1 mix.1
  16.2 5.9 %collective-permute-done.1 = bf16[2,88,1024]{2,1,0:T(8,128)(2,1)S(1)} collective-permute-done((bf16[2,88,1024]{2,1,0:T(8,128)(2,1)S(1)}, bf16[2,88,1024]{2,1,0:T(8,128)(2,1)S(1)}, u32[]{:S(2)}, u32[]{:S(2)}) %collective-permute-start.1) | collective-permute-done | bytes 360480 | tf_op jit(solution)/shard_map/ppermute | solution.py:344
  22.1 5.3 %collective-permute-done = bf16[2,88,1024]{2,1,0:T(8,128)(2,1)S(1)} collective-permute-done((bf16[2,88,1024]{2,1,0:T(8,128)(2,1)S(1)}, bf16[2,88,1024]{2,1,0:T(8,128)(2,1)S(1)}, u32[]{:S(2)}, u32[]{:S(2)}) %collective-permute-start) | collective-permute-done | bytes 360480 | tf_op jit(solution)/shard_map/ppermute | solution.py:343
  27.4 0.8 dispatch.1
  28.2 15.2 %all-to-all-start.1 = ((bf16[16,24,128]{2,1,0:T(8,128)(2,1)}), bf16[16,24,128]{2,1,0:T(8,128)(2,1)S(1)}, u32[]{:S(2)}, u32[]{:S(2)}) async-start(bf16[16,24,128]{2,1,0:T(8,128)(2,1)} %bitcast.8), calls=%async_computation.1 | async-start | bytes 196608 | tf_op jit(solution)/shard_map/all_to_all | solution.py:373
  43.4 0.2 gates.1.tokens_ref.gates_ref
  43.6 0.3 order.1.order_ref
  43.9 1.9 %collective-permute-start.2 = (bf16[2,88,1024]{2,1,0:T(8,128)(2,1)S(1)}, bf16[2,88,1024]{2,1,0:T(8,128)(2,1)S(1)}, u32[]{:S(2)}, u32[]{:S(2)}) collective-permute-start(bf16[2,88,1024]{2,1,0:T(8,128)(2,1)S(1)} %bitcast.24), channel_id=1, source_target_pairs={{0,4},{2,6},{4,0},{6,2},{1,5},{3,7},{5,1},{7,3},{8,12},{10,14},{12... | collective-permute-start | bytes 1081352 | tf_op jit(solution)/shard_map/ppermute | solution.py:383
  45.8 1.9 %collective-permute-start.3 = (bf16[2,88,1024]{2,1,0:T(8,128)(2,1)S(1)}, bf16[2,88,1024]{2,1,0:T(8,128)(2,1)S(1)}, u32[]{:S(2)}, u32[]{:S(2)}) collective-permute-start(bf16[2,88,1024]{2,1,0:T(8,128)(2,1)S(1)} %bitcast.25), channel_id=1, source_target_pairs={{0,1},{1,0},{2,3},{3,2},{4,5},{5,4},{6,7},{7,6},{8,9},{9,8},{10,11... | collective-permute-start | bytes 1081352 | tf_op jit(solution)/shard_map/ppermute | solution.py:385
  47.8 2.4 %collective-permute-start.4 = (bf16[2,88,1024]{2,1,0:T(8,128)(2,1)S(1)}, bf16[2,88,1024]{2,1,0:T(8,128)(2,1)S(1)}, u32[]{:S(2)}, u32[]{:S(2)}) collective-permute-start(bf16[2,88,1024]{2,1,0:T(8,128)(2,1)S(1)} %collective-permute-done), channel_id=1, source_target_pairs={{0,1},{1,0},{2,3},{3,2},{4,5},{5,4},{6,7},{7,6},{8,9},{9,8},{10,11... | collective-permute-start | bytes 1081352 | tf_op jit(solution)/shard_map/ppermute | solution.py:385
  50.2 1.9 %collective-permute-start.6 = (bf16[2,88,1024]{2,1,0:T(8,128)(2,1)S(1)}, bf16[2,88,1024]{2,1,0:T(8,128)(2,1)S(1)}, u32[]{:S(2)}, u32[]{:S(2)}) collective-permute-start(bf16[2,88,1024]{2,1,0:T(8,128)(2,1)S(1)} %collective-permute-done.1), channel_id=1, source_target_pairs={{0,1},{1,0},{2,3},{3,2},{4,5},{5,4},{6,7},{7,6},{8,9},{9,8},{10,11... | collective-permute-start | bytes 1081352 | tf_op jit(solution)/shard_map/ppermute | solution.py:385
  52.1 4.0 %collective-permute-done.2 = bf16[2,88,1024]{2,1,0:T(8,128)(2,1)S(1)} collective-permute-done((bf16[2,88,1024]{2,1,0:T(8,128)(2,1)S(1)}, bf16[2,88,1024]{2,1,0:T(8,128)(2,1)S(1)}, u32[]{:S(2)}, u32[]{:S(2)}) %collective-permute-start.2) | collective-permute-done | bytes 360480 | tf_op jit(solution)/shard_map/ppermute | solution.py:383
  56.1 1.9 %collective-permute-start.5 = (bf16[2,88,1024]{2,1,0:T(8,128)(2,1)S(1)}, bf16[2,88,1024]{2,1,0:T(8,128)(2,1)S(1)}, u32[]{:S(2)}, u32[]{:S(2)}) collective-permute-start(bf16[2,88,1024]{2,1,0:T(8,128)(2,1)S(1)} %collective-permute-done.2), channel_id=1, source_target_pairs={{0,1},{1,0},{2,3},{3,2},{4,5},{5,4},{6,7},{7,6},{8,9},{9,8},{10,11... | collective-permute-start | bytes 1081352 | tf_op jit(solution)/shard_map/ppermute | solution.py:385
  58.0 0.0 all-to-all-done.1
  58.0 13.1 %all_gather.3.tokens_ref = bf16[4,384,128]{2,1,0:T(8,128)(2,1)S(1)} all-gather(bf16[1,384,128]{2,1,0:T(8,128)(2,1)S(1)} %bitcast.35), channel_id=1, replica_groups=mesh['z'=16,'y'=4,'x'=4,'c'=2] {'y'}, dimensions={0}, use_global_device_ids=true | all-gather | bytes 491520 | tf_op jit(solution)/shard_map/all_gather | solution.py:386
  71.1 0.0 copy-start
  71.1 0.5 unpack.1.rows_ref
  71.6 0.0 collective-permute-done.4
  71.6 0.0 collective-permute-done.6
  71.6 0.0 collective-permute-done.3
  71.6 0.0 collective-permute-done.5
  71.6 0.8 copy-done
  72.5 2.7 %ffn.1 = bf16[4,384,128]{2,1,0:T(8,128)(2,1)S(1)} custom-call(s32[1]{0:T(128)} %bitcast.index_ref, bf16[192,1024]{1,0:T(8,128)(2,1)S(1)} %unpack.1.rows_ref, bf16[384,384]{1,0:T(8,128)(2,1)S(1)} %order.1.order_ref, bf16[704,1024]{1,0:T(8,128)(2,1)S(1)} %copy-done, bf16[176,1024]{1,0:T(8,128)(2,1)S(1)} %bitcast.26, bf16[176,1024]{1,0:T(8,128)(2,1)S(1)} %bitcast.28, ...), custom_call_target="tpu_custom_call" | custom-call | tf_op jit(solution)/shard_map/ffn/pallas_call | solution.py:397
  75.2 11.3 %all_to_all.20.parts_ref = bf16[4,384,128]{2,1,0:T(8,128)(2,1)S(1)} all-to-all(bf16[4,384,128]{2,1,0:T(8,128)(2,1)S(1)} %ffn.1), channel_id=1, replica_groups=mesh['z'=16,'y'=4,'x'=4,'c'=2] {'y'}, dimensions={0} | all-to-all | bytes 786432 | tf_op jit(solution)/shard_map/all_to_all | solution.py:406
  86.5 0.1 sum_quarters.1
  86.5 24.2 %all_to_all.21 = bf16[16,24,128]{2,1,0:T(8,128)(2,1)S(1)} all-to-all(bf16[16,24,128]{2,1,0:T(8,128)(2,1)S(1)} %bitcast.21), channel_id=1, replica_groups=mesh['z'=16,'y'=4,'x'=4,'c'=2] {'z'}, dimensions={0} | all-to-all | bytes 196608 | tf_op jit(solution)/shard_map/all_to_all | solution.py:415
  110.7 0.9 combine.1
Async XLA Ops:
  0.0 8.3 %copy-start.2 = (s32[128,2]{0,1:T(2,128)S(1)}, s32[128,2]{0,1:T(2,128)}, u32[]{:S(2)}) copy-start(s32[128,2]{0,1:T(2,128)} %param.25) | copy-start | bytes 3076
  0.0 9.0 %copy-start.1 = (bf16[2,1024,88]{1,2,0:T(8,128)(2,1)S(1)}, bf16[2,1024,88]{1,2,0:T(8,128)(2,1)}, u32[]{:S(2)}) copy-start(bf16[2,1024,88]{1,2,0:T(8,128)(2,1)} %param.26) | copy-start | bytes 1081348
  4.0 12.1 %all-to-all-start = ((bf16[8,16,1024]{2,1,0:T(8,128)(2,1)}), bf16[8,16,1024]{2,1,0:T(8,128)(2,1)S(1)}, u32[]{:S(2)}, u32[]{:S(2)}) async-start(bf16[8,16,1024]{2,1,0:T(8,128)(2,1)} %bitcast.5), calls=%async_computation | async-start | bytes 524288 | tf_op jit(solution)/shard_map/all_to_all | solution.py:345
  9.0 13.1 %collective-permute-start.1 = (bf16[2,88,1024]{2,1,0:T(8,128)(2,1)S(1)}, bf16[2,88,1024]{2,1,0:T(8,128)(2,1)S(1)}, u32[]{:S(2)}, u32[]{:S(2)}) collective-permute-start(bf16[2,88,1024]{2,1,0:T(8,128)(2,1)S(1)} %bitcast.22), channel_id=1, source_target_pairs={{0,6},{2,0},{4,2},{6,4},{1,7},{3,1},{5,3},{7,5},{8,14},{10,8},{12,... | collective-permute-start | bytes 1081352 | tf_op jit(solution)/shard_map/ppermute | solution.py:344
  14.1 13.3 %collective-permute-start = (bf16[2,88,1024]{2,1,0:T(8,128)(2,1)S(1)}, bf16[2,88,1024]{2,1,0:T(8,128)(2,1)S(1)}, u32[]{:S(2)}, u32[]{:S(2)}) collective-permute-start(bf16[2,88,1024]{2,1,0:T(8,128)(2,1)S(1)} %bitcast.23), channel_id=1, source_target_pairs={{0,2},{2,4},{4,6},{6,0},{1,3},{3,5},{5,7},{7,1},{8,10},{10,12},{12... | collective-permute-start | bytes 1081352 | tf_op jit(solution)/shard_map/ppermute | solution.py:343
  28.2 29.8 %all-to-all-start.1 = ((bf16[16,24,128]{2,1,0:T(8,128)(2,1)}), bf16[16,24,128]{2,1,0:T(8,128)(2,1)S(1)}, u32[]{:S(2)}, u32[]{:S(2)}) async-start(bf16[16,24,128]{2,1,0:T(8,128)(2,1)} %bitcast.8), calls=%async_computation.1 | async-start | bytes 196608 | tf_op jit(solution)/shard_map/all_to_all | solution.py:373
  43.9 12.2 %collective-permute-start.2 = (bf16[2,88,1024]{2,1,0:T(8,128)(2,1)S(1)}, bf16[2,88,1024]{2,1,0:T(8,128)(2,1)S(1)}, u32[]{:S(2)}, u32[]{:S(2)}) collective-permute-start(bf16[2,88,1024]{2,1,0:T(8,128)(2,1)S(1)} %bitcast.24), channel_id=1, source_target_pairs={{0,4},{2,6},{4,0},{6,2},{1,5},{3,7},{5,1},{7,3},{8,12},{10,14},{12... | collective-permute-start | bytes 1081352 | tf_op jit(solution)/shard_map/ppermute | solution.py:383
  45.8 25.7 %collective-permute-start.3 = (bf16[2,88,1024]{2,1,0:T(8,128)(2,1)S(1)}, bf16[2,88,1024]{2,1,0:T(8,128)(2,1)S(1)}, u32[]{:S(2)}, u32[]{:S(2)}) collective-permute-start(bf16[2,88,1024]{2,1,0:T(8,128)(2,1)S(1)} %bitcast.25), channel_id=1, source_target_pairs={{0,1},{1,0},{2,3},{3,2},{4,5},{5,4},{6,7},{7,6},{8,9},{9,8},{10,11... | collective-permute-start | bytes 1081352 | tf_op jit(solution)/shard_map/ppermute | solution.py:385
  47.8 23.8 %collective-permute-start.4 = (bf16[2,88,1024]{2,1,0:T(8,128)(2,1)S(1)}, bf16[2,88,1024]{2,1,0:T(8,128)(2,1)S(1)}, u32[]{:S(2)}, u32[]{:S(2)}) collective-permute-start(bf16[2,88,1024]{2,1,0:T(8,128)(2,1)S(1)} %collective-permute-done), channel_id=1, source_target_pairs={{0,1},{1,0},{2,3},{3,2},{4,5},{5,4},{6,7},{7,6},{8,9},{9,8},{10,11... | collective-permute-start | bytes 1081352 | tf_op jit(solution)/shard_map/ppermute | solution.py:385
  50.2 21.4 %collective-permute-start.6 = (bf16[2,88,1024]{2,1,0:T(8,128)(2,1)S(1)}, bf16[2,88,1024]{2,1,0:T(8,128)(2,1)S(1)}, u32[]{:S(2)}, u32[]{:S(2)}) collective-permute-start(bf16[2,88,1024]{2,1,0:T(8,128)(2,1)S(1)} %collective-permute-done.1), channel_id=1, source_target_pairs={{0,1},{1,0},{2,3},{3,2},{4,5},{5,4},{6,7},{7,6},{8,9},{9,8},{10,11... | collective-permute-start | bytes 1081352 | tf_op jit(solution)/shard_map/ppermute | solution.py:385
  56.1 15.5 %collective-permute-start.5 = (bf16[2,88,1024]{2,1,0:T(8,128)(2,1)S(1)}, bf16[2,88,1024]{2,1,0:T(8,128)(2,1)S(1)}, u32[]{:S(2)}, u32[]{:S(2)}) collective-permute-start(bf16[2,88,1024]{2,1,0:T(8,128)(2,1)S(1)} %collective-permute-done.2), channel_id=1, source_target_pairs={{0,1},{1,0},{2,3},{3,2},{4,5},{5,4},{6,7},{7,6},{8,9},{9,8},{10,11... | collective-permute-start | bytes 1081352 | tf_op jit(solution)/shard_map/ppermute | solution.py:385
  71.1 1.4 %copy-start = (bf16[704,1024]{1,0:T(8,128)(2,1)S(1)}, bf16[704,1024]{1,0:T(8,128)(2,1)}, u32[]{:S(2)}) copy-start(bf16[704,1024]{1,0:T(8,128)(2,1)} %down_ref.1) | copy-start | bytes 4325380

commit v2 on v1

--- a/solution.py
+++ b/solution.py
@@ -200,6 +200,12 @@
     order_ref[...] = jnp.where(wanted == iota((chunk_rows, chunk_rows), 1), 1.0, 0.0).astype(BF)
 
 
+def stack_kernel(*refs):
+    *pieces, out_ref = refs
+    for at, piece in enumerate(pieces):
+        out_ref[at] = piece[...]
+
+
 def unpack_kernel(tokens_ref, order_ref, rows_ref):
     groups, chunk_rows, _ = tokens_ref.shape
     chunks = rows_ref.shape[1] // LANES
@@ -212,14 +218,12 @@
             ]
 
 
-def ffn_kernel(index_ref, rows_ref, order_ref, down_ref, *refs):
-    *pieces, out_ref, total_ref = refs
+def ffn_kernel(index_ref, rows_ref, order_ref, down_ref, own_ref, other_ref, out_ref, total_ref):
     groups, chunk_rows, _ = out_ref.shape
     width = rows_ref.shape[1]
     chunks = width // LANES
     each = chunk_rows // chunks
-    chips = len(pieces) // 2
-    both = pieces[0].shape[0]
+    chips, both, _ = own_ref.shape
     columns = both // 2
     core = index_ref[0] % 2
     chip = index_ref[0] // 2
@@ -229,8 +233,8 @@
         for shift in range(chips):
             came = (chip - shift + chips) % chips
             hidden = []
-            for piece in (first[shift], second[shift]):
-                projected = dot_nt(rows_ref[...], piece[...])
+            for pieces in (first, second):
+                projected = dot_nt(rows_ref[...], pieces[shift])
                 gate_val, up_val = projected[:, :columns], projected[:, columns:]
                 hidden.append(jax.nn.gelu(gate_val, approximate=True) * up_val)
             hidden = jnp.concatenate(hidden, axis=1).astype(BF)
@@ -240,11 +244,11 @@
 
     @pl.when(core == 0)
     def _():
-        experts_part(pieces[:chips], pieces[chips:])
+        experts_part(own_ref, other_ref)
 
     @pl.when(core != 0)
     def _():
-        experts_part(pieces[chips:], pieces[:chips])
+        experts_part(other_ref, own_ref)
 
     for group in range(groups):
         mine = total_ref[group * each : (group + 1) * each]
@@ -340,8 +344,9 @@
         name="routing",
     )(hid_index, routes.T, gain)
     column, w_cols = lax.optimization_barrier((column, w_cols))
-    before = lax.ppermute(w_cols, "x", [(at, (at + 1) % row) for at in range(row)])
-    after_it = lax.ppermute(w_cols, "x", [(at, (at - 1) % row) for at in range(row)])
+    own_core = [w_cols]
+    for shift in range(1, row):
+        own_core.append(lax.ppermute(w_cols, "x", [(at, (at + shift) % row) for at in range(row)]))
     parts = lax.all_to_all(partial_mix.reshape(hid_count, block, width), hid, 0, 0, tiled=True)
     after, ffn_in = pl.pallas_call(
         mix_kernel,
@@ -352,13 +357,13 @@
         cost_estimate=LONG,
         name="mix",
     )(parts, own, gain)
-    ffn_in, before, after_it = lax.optimization_barrier((ffn_in, before, after_it))
     outgoing = pl.pallas_call(
         dispatch_kernel,
         out_shape=jax.ShapeDtypeStruct((slot_count, LANES), BF),
         in_specs=[VMEM] * 2,
         out_specs=VMEM,
         compiler_params=PARAMS,
+        cost_estimate=LONG,
         name="dispatch",
     )(ffn_in, chosen)
     gates = pl.pallas_call(
@@ -367,6 +372,7 @@
         in_specs=[VMEM] * 3,
         out_specs=VMEM,
         compiler_params=PARAMS,
+        cost_estimate=LONG,
         name="gates",
     )(ffn_in, router_rows, column)
     exchanged = (experts, chunks * CAPACITY, LANES)
@@ -377,12 +383,21 @@
         in_specs=[VMEM],
         out_specs=VMEM,
         compiler_params=PARAMS,
+        cost_estimate=LONG,
         name="order",
     )(gates)
-    order, w_cols, before, after_it = lax.optimization_barrier((order, w_cols, before, after_it))
-    across = lax.ppermute(w_cols, "x", [(at, (at + 2) % row) for at in range(row)])
-    own_core = (w_cols, before, across, after_it)
-    other_core = [lax.ppermute(cols, "c", [(0, 1), (1, 0)]) for cols in own_core]
+    order, *own_core = lax.optimization_barrier((order, *own_core))
+    own_core = [cols.reshape(-1, width) for cols in own_core]
+    stacked = pl.pallas_call(
+        stack_kernel,
+        out_shape=jax.ShapeDtypeStruct((row,) + own_core[0].shape, BF),
+        in_specs=[VMEM] * row,
+        out_specs=VMEM,
+        compiler_params=PARAMS,
+        cost_estimate=LONG,
+        name="stack",
+    )(*own_core)
+    other_core = lax.ppermute(stacked, "c", [(0, 1), (1, 0)])
     tokens = lax.all_gather(arrived.reshape(slot_count, LANES), "y", axis=0)
     rows = pl.pallas_call(
         unpack_kernel,
@@ -393,16 +408,15 @@
         cost_estimate=LONG,
         name="unpack",
     )(tokens, order)
-    pieces = [cols.reshape(-1, width) for cols in (*own_core, *other_core)]
     projected = pl.pallas_call(
         ffn_kernel,
         out_shape=jax.ShapeDtypeStruct((split, slot_count, LANES), BF),
-        in_specs=[SMEM] + [VMEM] * (3 + len(pieces)),
+        in_specs=[SMEM] + [VMEM] * 5,
         out_specs=VMEM,
         scratch_shapes=[pltpu.VMEM((split * experts * CAPACITY, width), BF)],
         compiler_params=PARAMS,
         name="ffn",
-    )(hid_index, rows, order, w_out, *pieces)
+    )(hid_index, rows, order, w_out, stacked, other_core)
     quarters = lax.all_to_all(projected, "y", 0, 0, tiled=True)
     summed = pl.pallas_call(
         sum_kernel,

time: 112 us -> 95.1 us (0.85)
  the two profiles are of different devices: /device:TPU:32 before, /device:TPU:6 now
where the time goes in v2:
time: 95.1 us; the launch traced here: 93.9 us
  blocking collectives  40.3 us (42%)
  starting transfers between devices  31.7 us (33%)
  waiting for transfers between devices  10.6 us (11%)
  Pallas kernels  10.2 us (11%)
    all_to_all x1, blocking collectives, body(): returned = lax.all_to_all(summed.reshape(exchanged), 'z', 0, 0, tiled=True)  16.4 us
    all_gather x1, blocking collectives, body(): tokens = lax.all_gather(arrived.reshape(slot_count, LANES), 'y', axis=0)  13.5 us
    all_to_all x1, starting transfers between devices, body(): arrived = lax.all_to_all(outgoing.reshape(exchanged), 'z', 0, 0, tiled=True)  10.8 us
    all_to_all x1, blocking collectives, body(): quarters = lax.all_to_all(projected, 'y', 0, 0, tiled=True)  10.4 us
    ppermute x3, starting transfers between devices, body(): lax.ppermute(w_cols, 'x', [(at, (at + shift) % row) for at in range(row)])  9.79 us
    all_to_all x1, starting transfers between devices, body(): lax.all_to_all(partial_mix.reshape(hid_count, block, width), hid, 0, 0, t...  9.21 us
    all_to_all x1, waiting for transfers between devices, body(): arrived = lax.all_to_all(outgoing.reshape(exchanged), 'z', 0, 0, tiled=True)  8.87 us
    pallas_call x1, Pallas kernels, body(): pl.pallas_call(attention_kernel, out_shape=(jax.ShapeDtypeStruct((group_r...  3.98 us
  transfers between devices with their start and end apart: 6, of which 2 were waited for; matrix products, arithmetic and copies ran while one was open for 0% of the time, Pallas kernels for 3%

profile of v2, /device:TPU:6, one launch (start us, length us, event | category | flops | bytes accessed | tf_op | source)
XLA Modules:
  0.0 93.9 jit_solution(3455154413394420520)
XLA Ops:
  0.0 0.0 copy-start.1
  0.0 0.0 copy-start.2
  0.0 4.0 %attention.1 = (bf16[128,1024]{1,0:T(8,128)(2,1)}, f32[16,1024]{1,0:T(8,128)S(1)}, f32[1,1024]{1,0:T(1,128)S(1)}, bf16[16,1024]{1,0:T(8,128)(2,1)S(1)}) custom-call(s32[1]{0:T(128)} %bitcast.index_ref, bf16[128,1024]{1,0:T(8,128)(2,1)} %resid_hbm.1, f32[1,1024]{1,0:T(1,128)} %bitcast.28, bf16[1024,128]{1,0:T(8,128)(2,1)} %wq_hbm.1, ...), custom_call_target="tpu_custom_call" | custom-call | tf_op jit(solution)/shard_map/attention/pallas_call | solution.py:319
  4.0 9.2 %all-to-all-start = ((bf16[8,16,1024]{2,1,0:T(8,128)(2,1)}), bf16[8,16,1024]{2,1,0:T(8,128)(2,1)S(1)}, u32[]{:S(2)}, u32[]{:S(2)}) async-start(bf16[8,16,1024]{2,1,0:T(8,128)(2,1)} %bitcast.5), calls=%async_computation | async-start | bytes 524288 | tf_op jit(solution)/shard_map/all_to_all | solution.py:350
  13.2 0.0 copy-done.1
  13.2 0.6 routing.1
  13.9 0.0 copy-done.2
  13.9 2.8 %collective-permute-start.2 = (bf16[2,88,1024]{2,1,0:T(8,128)(2,1)S(1)}, bf16[2,88,1024]{2,1,0:T(8,128)(2,1)S(1)}, u32[]{:S(2)}, u32[]{:S(2)}) collective-permute-start(bf16[2,88,1024]{2,1,0:T(8,128)(2,1)S(1)} %bitcast.19), channel_id=1, source_target_pairs={{0,6},{2,0},{4,2},{6,4},{1,7},{3,1},{5,3},{7,5},{8,14},{10,8},{12,... | collective-permute-start | bytes 1081352 | tf_op jit(solution)/shard_map/ppermute | solution.py:349
  16.6 2.6 %collective-permute-start.1 = (bf16[2,88,1024]{2,1,0:T(8,128)(2,1)S(1)}, bf16[2,88,1024]{2,1,0:T(8,128)(2,1)S(1)}, u32[]{:S(2)}, u32[]{:S(2)}) collective-permute-start(bf16[2,88,1024]{2,1,0:T(8,128)(2,1)S(1)} %bitcast.20), channel_id=1, source_target_pairs={{0,4},{2,6},{4,0},{6,2},{1,5},{3,7},{5,1},{7,3},{8,12},{10,14},{12... | collective-permute-start | bytes 1081352 | tf_op jit(solution)/shard_map/ppermute | solution.py:349
  19.3 4.4 %collective-permute-start = (bf16[2,88,1024]{2,1,0:T(8,128)(2,1)S(1)}, bf16[2,88,1024]{2,1,0:T(8,128)(2,1)S(1)}, u32[]{:S(2)}, u32[]{:S(2)}) collective-permute-start(bf16[2,88,1024]{2,1,0:T(8,128)(2,1)S(1)} %bitcast.21), channel_id=1, source_target_pairs={{0,2},{2,4},{4,6},{6,0},{1,3},{3,5},{5,7},{7,1},{8,10},{10,12},{12... | collective-permute-start | bytes 1081352 | tf_op jit(solution)/shard_map/ppermute | solution.py:349
  23.7 0.0 all-to-all-done.parts_ref
  23.7 0.1 mix.1
  23.8 0.8 dispatch.1
  24.6 10.8 %all-to-all-start.1 = ((bf16[16,24,128]{2,1,0:T(8,128)(2,1)}), bf16[16,24,128]{2,1,0:T(8,128)(2,1)S(1)}, u32[]{:S(2)}, u32[]{:S(2)}) async-start(bf16[16,24,128]{2,1,0:T(8,128)(2,1)} %bitcast.7), calls=%async_computation.1 | async-start | bytes 196608 | tf_op jit(solution)/shard_map/all_to_all | solution.py:379
  35.4 0.2 gates.1.tokens_ref.gates_ref
  35.6 0.3 order.1.order_ref
  35.9 0.0 collective-permute-done.2
  35.9 0.0 collective-permute-done.1
  35.9 1.8 %collective-permute-done = bf16[2,88,1024]{2,1,0:T(8,128)(2,1)S(1)} collective-permute-done((bf16[2,88,1024]{2,1,0:T(8,128)(2,1)S(1)}, bf16[2,88,1024]{2,1,0:T(8,128)(2,1)S(1)}, u32[]{:S(2)}, u32[]{:S(2)}) %collective-permute-start) | collective-permute-done | bytes 360480 | tf_op jit(solution)/shard_map/ppermute | solution.py:349
  37.7 0.1 stack.1.own_ref
  37.8 1.9 %collective-permute-start.3 = (bf16[4,176,1024]{2,1,0:T(8,128)(2,1)S(1)}, bf16[4,176,1024]{2,1,0:T(8,128)(2,1)S(1)}, u32[]{:S(2)}, u32[]{:S(2)}) collective-permute-start(bf16[4,176,1024]{2,1,0:T(8,128)(2,1)S(1)} %stack.1.own_ref), channel_id=1, source_target_pairs={{0,1},{1,0},{2,3},{3,2},{4,5},{5,4},{6,7},{7,6},{8,9},{9,8},{10,11... | collective-permute-start | bytes 4325384 | tf_op jit(solution)/shard_map/ppermute | solution.py:400
  39.7 8.9 %all-to-all-done.1 = bf16[16,24,128]{2,1,0:T(8,128)(2,1)S(1)} async-done(((bf16[16,24,128]{2,1,0:T(8,128)(2,1)}), bf16[16,24,128]{2,1,0:T(8,128)(2,1)S(1)}, u32[]{:S(2)}, u32[]{:S(2)}) %all-to-all-start.1) | async-done | bytes 98336 | tf_op jit(solution)/shard_map/all_to_all | solution.py:379
  48.6 13.5 %all_gather.3.tokens_ref = bf16[4,384,128]{2,1,0:T(8,128)(2,1)S(1)} all-gather(bf16[1,384,128]{2,1,0:T(8,128)(2,1)S(1)} %bitcast.26), channel_id=1, replica_groups=mesh['z'=16,'y'=4,'x'=4,'c'=2] {'y'}, dimensions={0}, use_global_device_ids=true | all-gather | bytes 491520 | tf_op jit(solution)/shard_map/all_gather | solution.py:401
  62.1 0.0 copy-start
  62.1 0.5 unpack.1.rows_ref
  62.6 0.0 collective-permute-done.3.other_ref
  62.6 0.9 copy-done
  63.5 2.7 %ffn.1 = bf16[4,384,128]{2,1,0:T(8,128)(2,1)S(1)} custom-call(s32[1]{0:T(128)} %bitcast.index_ref, bf16[192,1024]{1,0:T(8,128)(2,1)S(1)} %unpack.1.rows_ref, bf16[384,384]{1,0:T(8,128)(2,1)S(1)} %order.1.order_ref, bf16[704,1024]{1,0:T(8,128)(2,1)S(1)} %copy-done, bf16[4,176,1024]{2,1,0:T(8,128)(2,1)S(1)} %stack.1.own_ref, ...), custom_call_target="tpu_custom_call" | custom-call | tf_op jit(solution)/shard_map/ffn/pallas_call | solution.py:411
  66.2 10.4 %all_to_all.20.parts_ref = bf16[4,384,128]{2,1,0:T(8,128)(2,1)S(1)} all-to-all(bf16[4,384,128]{2,1,0:T(8,128)(2,1)S(1)} %ffn.1), channel_id=1, replica_groups=mesh['z'=16,'y'=4,'x'=4,'c'=2] {'y'}, dimensions={0} | all-to-all | bytes 786432 | tf_op jit(solution)/shard_map/all_to_all | solution.py:420
  76.7 0.1 sum_quarters.1
  76.7 16.4 %all_to_all.21 = bf16[16,24,128]{2,1,0:T(8,128)(2,1)S(1)} all-to-all(bf16[16,24,128]{2,1,0:T(8,128)(2,1)S(1)} %bitcast.17), channel_id=1, replica_groups=mesh['z'=16,'y'=4,'x'=4,'c'=2] {'z'}, dimensions={0} | all-to-all | bytes 196608 | tf_op jit(solution)/shard_map/all_to_all | solution.py:429
  93.1 0.9 combine.1
Async XLA Ops:
  0.0 13.2 %copy-start.1 = (s32[128,2]{0,1:T(2,128)S(1)}, s32[128,2]{0,1:T(2,128)}, u32[]{:S(2)}) copy-start(s32[128,2]{0,1:T(2,128)} %param.25) | copy-start | bytes 3076
  0.0 13.9 %copy-start.2 = (bf16[2,1024,88]{1,2,0:T(8,128)(2,1)S(1)}, bf16[2,1024,88]{1,2,0:T(8,128)(2,1)}, u32[]{:S(2)}) copy-start(bf16[2,1024,88]{1,2,0:T(8,128)(2,1)} %param.26) | copy-start | bytes 1081348
  4.0 19.7 %all-to-all-start = ((bf16[8,16,1024]{2,1,0:T(8,128)(2,1)}), bf16[8,16,1024]{2,1,0:T(8,128)(2,1)S(1)}, u32[]{:S(2)}, u32[]{:S(2)}) async-start(bf16[8,16,1024]{2,1,0:T(8,128)(2,1)} %bitcast.5), calls=%async_computation | async-start | bytes 524288 | tf_op jit(solution)/shard_map/all_to_all | solution.py:350
  13.9 22.0 %collective-permute-start.2 = (bf16[2,88,1024]{2,1,0:T(8,128)(2,1)S(1)}, bf16[2,88,1024]{2,1,0:T(8,128)(2,1)S(1)}, u32[]{:S(2)}, u32[]{:S(2)}) collective-permute-start(bf16[2,88,1024]{2,1,0:T(8,128)(2,1)S(1)} %bitcast.19), channel_id=1, source_target_pairs={{0,6},{2,0},{4,2},{6,4},{1,7},{3,1},{5,3},{7,5},{8,14},{10,8},{12,... | collective-permute-start | bytes 1081352 | tf_op jit(solution)/shard_map/ppermute | solution.py:349
  16.6 19.3 %collective-permute-start.1 = (bf16[2,88,1024]{2,1,0:T(8,128)(2,1)S(1)}, bf16[2,88,1024]{2,1,0:T(8,128)(2,1)S(1)}, u32[]{:S(2)}, u32[]{:S(2)}) collective-permute-start(bf16[2,88,1024]{2,1,0:T(8,128)(2,1)S(1)} %bitcast.20), channel_id=1, source_target_pairs={{0,4},{2,6},{4,0},{6,2},{1,5},{3,7},{5,1},{7,3},{8,12},{10,14},{12... | collective-permute-start | bytes 1081352 | tf_op jit(solution)/shard_map/ppermute | solution.py:349
  19.3 18.4 %collective-permute-start = (bf16[2,88,1024]{2,1,0:T(8,128)(2,1)S(1)}, bf16[2,88,1024]{2,1,0:T(8,128)(2,1)S(1)}, u32[]{:S(2)}, u32[]{:S(2)}) collective-permute-start(bf16[2,88,1024]{2,1,0:T(8,128)(2,1)S(1)} %bitcast.21), channel_id=1, source_target_pairs={{0,2},{2,4},{4,6},{6,0},{1,3},{3,5},{5,7},{7,1},{8,10},{10,12},{12... | collective-permute-start | bytes 1081352 | tf_op jit(solution)/shard_map/ppermute | solution.py:349
  24.6 24.0 %all-to-all-start.1 = ((bf16[16,24,128]{2,1,0:T(8,128)(2,1)}), bf16[16,24,128]{2,1,0:T(8,128)(2,1)S(1)}, u32[]{:S(2)}, u32[]{:S(2)}) async-start(bf16[16,24,128]{2,1,0:T(8,128)(2,1)} %bitcast.7), calls=%async_computation.1 | async-start | bytes 196608 | tf_op jit(solution)/shard_map/all_to_all | solution.py:379
  37.8 24.8 %collective-permute-start.3 = (bf16[4,176,1024]{2,1,0:T(8,128)(2,1)S(1)}, bf16[4,176,1024]{2,1,0:T(8,128)(2,1)S(1)}, u32[]{:S(2)}, u32[]{:S(2)}) collective-permute-start(bf16[4,176,1024]{2,1,0:T(8,128)(2,1)S(1)} %stack.1.own_ref), channel_id=1, source_target_pairs={{0,1},{1,0},{2,3},{3,2},{4,5},{5,4},{6,7},{7,6},{8,9},{9,8},{10,11... | collective-permute-start | bytes 4325384 | tf_op jit(solution)/shard_map/ppermute | solution.py:400
  62.1 1.4 %copy-start = (bf16[704,1024]{1,0:T(8,128)(2,1)S(1)}, bf16[704,1024]{1,0:T(8,128)(2,1)}, u32[]{:S(2)}) copy-start(bf16[704,1024]{1,0:T(8,128)(2,1)} %down_ref.1) | copy-start | bytes 4325380

commit v3 on v2

--- a/solution.py
+++ b/solution.py
@@ -200,7 +200,12 @@
     order_ref[...] = jnp.where(wanted == iota((chunk_rows, chunk_rows), 1), 1.0, 0.0).astype(BF)
 
 
-def stack_kernel(*refs):
+def spread_kernel(tokens_ref, out_ref):
+    for at in range(out_ref.shape[0]):
+        out_ref[at] = tokens_ref[...]
+
+
+def stack_kernel(spread_ref, *refs):
     *pieces, out_ref = refs
     for at, piece in enumerate(pieces):
         out_ref[at] = piece[...]
@@ -284,6 +289,7 @@
 
 
 LONG = pl.CostEstimate(flops=10**10, transcendentals=0, bytes_accessed=1 << 21)
+VERY_LONG = pl.CostEstimate(flops=2 * 10**10, transcendentals=0, bytes_accessed=1 << 21)
 PARAMS = pltpu.CompilerParams(vmem_limit_bytes=16 * 1024 * 1024)
 
 
@@ -344,9 +350,8 @@
         name="routing",
     )(hid_index, routes.T, gain)
     column, w_cols = lax.optimization_barrier((column, w_cols))
-    own_core = [w_cols]
-    for shift in range(1, row):
-        own_core.append(lax.ppermute(w_cols, "x", [(at, (at + shift) % row) for at in range(row)]))
+    moves = [[(at, (at + shift) % row) for at in range(row)] for shift in range(row)]
+    own_core = [w_cols] + [lax.ppermute(w_cols, "x", move) for move in moves[1:-1]]
     parts = lax.all_to_all(partial_mix.reshape(hid_count, block, width), hid, 0, 0, tiled=True)
     after, ffn_in = pl.pallas_call(
         mix_kernel,
@@ -383,29 +388,36 @@
         in_specs=[VMEM],
         out_specs=VMEM,
         compiler_params=PARAMS,
-        cost_estimate=LONG,
         name="order",
     )(gates)
     order, *own_core = lax.optimization_barrier((order, *own_core))
+    own_core.append(lax.ppermute(own_core[0], "x", moves[-1]))
+    spread = pl.pallas_call(
+        spread_kernel,
+        out_shape=jax.ShapeDtypeStruct((split, slot_count, LANES), BF),
+        in_specs=[VMEM],
+        out_specs=VMEM,
+        compiler_params=PARAMS,
+        name="spread",
+    )(arrived.reshape(slot_count, LANES))
+    tokens = lax.all_to_all(spread, "y", 0, 0, tiled=True)
     own_core = [cols.reshape(-1, width) for cols in own_core]
     stacked = pl.pallas_call(
         stack_kernel,
         out_shape=jax.ShapeDtypeStruct((row,) + own_core[0].shape, BF),
-        in_specs=[VMEM] * row,
-        out_specs=VMEM,
-        compiler_params=PARAMS,
-        cost_estimate=LONG,
+        in_specs=[pl.BlockSpec(memory_space=pl.ANY)] + [VMEM] * row,
+        out_specs=VMEM,
+        compiler_params=PARAMS,
         name="stack",
-    )(*own_core)
+    )(spread, *own_core)
     other_core = lax.ppermute(stacked, "c", [(0, 1), (1, 0)])
-    tokens = lax.all_gather(arrived.reshape(slot_count, LANES), "y", axis=0)
     rows = pl.pallas_call(
         unpack_kernel,
         out_shape=jax.ShapeDtypeStruct((split * experts * CAPACITY, width), BF),
         in_specs=[VMEM] * 2,
         out_specs=VMEM,
         compiler_params=PARAMS,
-        cost_estimate=LONG,
+        cost_estimate=VERY_LONG,
         name="unpack",
     )(tokens, order)
     projected = pl.pallas_call(

time: 95.1 us -> 95.1 us (level)
  blocking collectives: 40.3 us -> 28.2 us
  starting transfers between devices: 31.7 us -> 38.5 us
  Pallas kernels: 10.2 us -> 13.4 us
  waiting for transfers between devices: 10.6 us -> 13.6 us
    all_gather x1 -> x0, blocking collectives: 13.5 us -> none  [body(): tokens = lax.all_gather(arrived.reshape(slot_count, LANES), 'y', axis=0)]
    all_to_all x0 -> x1, waiting for transfers between devices: none -> 5.31 us  [body(): tokens = lax.all_to_all(spread, 'y', 0, 0, tiled=True)]
    all_to_all x0 -> x1, starting transfers between devices: none -> 4.48 us  [body(): tokens = lax.all_to_all(spread, 'y', 0, 0, tiled=True)]
    ppermute x3, starting transfers between devices: 9.79 us -> 12 us  [the longest x2 7.33 us: body(): lax.ppermute(w_cols, 'x', move)]
    all_to_all x1, blocking collectives: 16.4 us -> 18.4 us  [body(): returned = lax.all_to_all(summed.reshape(exchanged), 'z', 0, 0, tiled=True)]
    ppermute x3, waiting for transfers between devices: 1.77 us -> 0.1 us  [the longest x2 0.09 us: body(): lax.ppermute(w_cols, 'x', move)]
    pallas_call x1, Pallas kernels: 2.73 us -> 4.08 us  [body(): pl.pallas_call(ffn_kernel, out_shape=jax.ShapeDtypeStruct((split, slot_co...]
    pallas_call x1, Pallas kernels: 0.46 us -> 1.46 us  [body(): pl.pallas_call(unpack_kernel, out_shape=jax.ShapeDtypeStruct((split * exp...]
  transfers between devices with their start and end apart: 6 -> 7, of which waited for: 2 -> 3; matrix products, arithmetic and copies ran while one was open for 0% -> 0% of each run, Pallas kernels for 3% -> 5%
where the time goes in v3:
time: 95.1 us; the launch traced here: 93.9 us
  starting transfers between devices  38.5 us (40%)
  blocking collectives  28.2 us (30%)
  waiting for transfers between devices  13.6 us (14%)
  Pallas kernels  13.4 us (14%)
    all_to_all x1, blocking collectives, body(): returned = lax.all_to_all(summed.reshape(exchanged), 'z', 0, 0, tiled=True)  18.4 us
    all_to_all x1, starting transfers between devices, body(): arrived = lax.all_to_all(outgoing.reshape(exchanged), 'z', 0, 0, tiled=True)  10.8 us
    all_to_all x1, blocking collectives, body(): quarters = lax.all_to_all(projected, 'y', 0, 0, tiled=True)  9.77 us
    all_to_all x1, starting transfers between devices, body(): lax.all_to_all(partial_mix.reshape(hid_count, block, width), hid, 0, 0, t...  9.21 us
    all_to_all x1, waiting for transfers between devices, body(): arrived = lax.all_to_all(outgoing.reshape(exchanged), 'z', 0, 0, tiled=True)  8.21 us
    ppermute x2, starting transfers between devices, body(): lax.ppermute(w_cols, 'x', move)  7.33 us
    all_to_all x1, waiting for transfers between devices, body(): tokens = lax.all_to_all(spread, 'y', 0, 0, tiled=True)  5.31 us
    ppermute x1, starting transfers between devices, body(): own_core.append(lax.ppermute(own_core[0], 'x', moves[-1]))  4.64 us
  transfers between devices with their start and end apart: 7, of which 3 were waited for; matrix products, arithmetic and copies ran while one was open for 0% of the time, Pallas kernels for 5%

profile of v3, /device:TPU:6, one launch (start us, length us, event | category | flops | bytes accessed | tf_op | source)
XLA Modules:
  0.0 93.9 jit_solution(18022175777057690861)
XLA Ops:
  0.0 0.0 copy-start.2
  0.0 0.0 copy-start.1
  0.0 4.0 %attention.1 = (bf16[128,1024]{1,0:T(8,128)(2,1)}, f32[16,1024]{1,0:T(8,128)S(1)}, f32[1,1024]{1,0:T(1,128)S(1)}, bf16[16,1024]{1,0:T(8,128)(2,1)S(1)}) custom-call(s32[1]{0:T(128)} %bitcast.index_ref, bf16[128,1024]{1,0:T(8,128)(2,1)} %resid_hbm.1, f32[1,1024]{1,0:T(1,128)} %bitcast.28, bf16[1024,128]{1,0:T(8,128)(2,1)} %wq_hbm.1, ...), custom_call_target="tpu_custom_call" | custom-call | tf_op jit(solution)/shard_map/attention/pallas_call | solution.py:325
  4.0 9.2 %all-to-all-start = ((bf16[8,16,1024]{2,1,0:T(8,128)(2,1)}), bf16[8,16,1024]{2,1,0:T(8,128)(2,1)S(1)}, u32[]{:S(2)}, u32[]{:S(2)}) async-start(bf16[8,16,1024]{2,1,0:T(8,128)(2,1)} %bitcast.5), calls=%async_computation | async-start | bytes 524288 | tf_op jit(solution)/shard_map/all_to_all | solution.py:355
  13.2 0.0 copy-done.2
  13.2 0.6 routing.1
  13.9 0.0 copy-done.1
  13.9 3.3 %collective-permute-start.1 = (bf16[2,88,1024]{2,1,0:T(8,128)(2,1)S(1)}, bf16[2,88,1024]{2,1,0:T(8,128)(2,1)S(1)}, u32[]{:S(2)}, u32[]{:S(2)}) collective-permute-start(bf16[2,88,1024]{2,1,0:T(8,128)(2,1)S(1)} %bitcast.19), channel_id=1, source_target_pairs={{0,4},{2,6},{4,0},{6,2},{1,5},{3,7},{5,1},{7,3},{8,12},{10,14},{12... | collective-permute-start | bytes 1081352 | tf_op jit(solution)/shard_map/ppermute | solution.py:354
  17.2 4.0 %collective-permute-start = (bf16[2,88,1024]{2,1,0:T(8,128)(2,1)S(1)}, bf16[2,88,1024]{2,1,0:T(8,128)(2,1)S(1)}, u32[]{:S(2)}, u32[]{:S(2)}) collective-permute-start(bf16[2,88,1024]{2,1,0:T(8,128)(2,1)S(1)} %bitcast.20), channel_id=1, source_target_pairs={{0,2},{2,4},{4,6},{6,0},{1,3},{3,5},{5,7},{7,1},{8,10},{10,12},{12... | collective-permute-start | bytes 1081352 | tf_op jit(solution)/shard_map/ppermute | solution.py:354
  21.2 0.0 all-to-all-done.parts_ref
  21.2 0.1 mix.1
  21.4 0.8 dispatch.1
  22.2 10.8 %all-to-all-start.1 = ((bf16[16,24,128]{2,1,0:T(8,128)(2,1)}), bf16[16,24,128]{2,1,0:T(8,128)(2,1)S(1)}, u32[]{:S(2)}, u32[]{:S(2)}) async-start(bf16[16,24,128]{2,1,0:T(8,128)(2,1)} %bitcast.7), calls=%async_computation.1 | async-start | bytes 196608 | tf_op jit(solution)/shard_map/all_to_all | solution.py:384
  33.0 0.2 gates.1.tokens_ref.gates_ref
  33.2 0.3 order.1.order_ref
  33.5 0.0 collective-permute-done.1
  33.5 0.1 collective-permute-done
  33.6 4.6 %collective-permute-start.2 = (bf16[2,88,1024]{2,1,0:T(8,128)(2,1)S(1)}, bf16[2,88,1024]{2,1,0:T(8,128)(2,1)S(1)}, u32[]{:S(2)}, u32[]{:S(2)}) collective-permute-start(bf16[2,88,1024]{2,1,0:T(8,128)(2,1)S(1)} %bitcast.21), channel_id=1, source_target_pairs={{0,6},{2,0},{4,2},{6,4},{1,7},{3,1},{5,3},{7,5},{8,14},{10,8},{12,... | collective-permute-start | bytes 1081352 | tf_op jit(solution)/shard_map/ppermute | solution.py:394
  38.2 8.2 %all-to-all-done.1 = bf16[16,24,128]{2,1,0:T(8,128)(2,1)S(1)} async-done(((bf16[16,24,128]{2,1,0:T(8,128)(2,1)}), bf16[16,24,128]{2,1,0:T(8,128)(2,1)S(1)}, u32[]{:S(2)}, u32[]{:S(2)}) %all-to-all-start.1) | async-done | bytes 98336 | tf_op jit(solution)/shard_map/all_to_all | solution.py:384
  46.4 0.8 spread.1.spread_ref
  47.2 4.5 %all-to-all-start.2 = ((bf16[4,384,128]{2,1,0:T(8,128)(2,1)}), bf16[4,384,128]{2,1,0:T(8,128)(2,1)}, u32[]{:S(2)}, u32[]{:S(2)}) async-start(bf16[4,384,128]{2,1,0:T(8,128)(2,1)} %spread.1.spread_ref), calls=%async_computation.2 | async-start | bytes 786432 | tf_op jit(solution)/shard_map/all_to_all | solution.py:403
  51.7 0.0 collective-permute-done.2
  51.7 0.1 stack.1.own_ref
  51.8 0.0 copy-start
  51.8 2.1 %collective-permute-start.3 = (bf16[4,176,1024]{2,1,0:T(8,128)(2,1)S(1)}, bf16[4,176,1024]{2,1,0:T(8,128)(2,1)}, u32[]{:S(2)}, u32[]{:S(2)}) collective-permute-start(bf16[4,176,1024]{2,1,0:T(8,128)(2,1)S(1)} %stack.1.own_ref), channel_id=1, source_target_pairs={{0,1},{1,0},{2,3},{3,2},{4,5},{5,4},{6,7},{7,6},{8,9},{9,8},{10,11... | collective-permute-start | bytes 4325384 | tf_op jit(solution)/shard_map/ppermute | solution.py:413
  53.9 5.3 %all-to-all-done.2.tokens_ref = bf16[4,384,128]{2,1,0:T(8,128)(2,1)} async-done(((bf16[4,384,128]{2,1,0:T(8,128)(2,1)}), bf16[4,384,128]{2,1,0:T(8,128)(2,1)}, u32[]{:S(2)}, u32[]{:S(2)}) %all-to-all-start.2) | async-done | bytes 393248 | tf_op jit(solution)/shard_map/all_to_all | solution.py:403
  59.2 1.5 %unpack.1.rows_ref = bf16[192,1024]{1,0:T(8,128)(2,1)S(1)} custom-call(bf16[4,384,128]{2,1,0:T(8,128)(2,1)} %all-to-all-done.2.tokens_ref, bf16[384,384]{1,0:T(8,128)(2,1)S(1)} %order.1.order_ref), custom_call_target="tpu_custom_call" | custom-call | flops 20000000000 | bytes 2097152 | tf_op jit(solution)/shard_map/unpack/pallas_call | solution.py:414
  60.7 0.0 collective-permute-done.3.other_ref
  60.7 0.0 copy-done
  60.7 4.1 %ffn.1 = bf16[4,384,128]{2,1,0:T(8,128)(2,1)S(1)} custom-call(s32[1]{0:T(128)} %bitcast.index_ref, bf16[192,1024]{1,0:T(8,128)(2,1)S(1)} %unpack.1.rows_ref, bf16[384,384]{1,0:T(8,128)(2,1)S(1)} %order.1.order_ref, bf16[704,1024]{1,0:T(8,128)(2,1)S(1)} %copy-done, bf16[4,176,1024]{2,1,0:T(8,128)(2,1)S(1)} %stack.1.own_ref, ...), custom_call_target="tpu_custom_call" | custom-call | tf_op jit(solution)/shard_map/ffn/pallas_call | solution.py:423
  64.8 9.8 %all_to_all.25.parts_ref = bf16[4,384,128]{2,1,0:T(8,128)(2,1)S(1)} all-to-all(bf16[4,384,128]{2,1,0:T(8,128)(2,1)S(1)} %ffn.1), channel_id=1, replica_groups=mesh['z'=16,'y'=4,'x'=4,'c'=2] {'y'}, dimensions={0} | all-to-all | bytes 786432 | tf_op jit(solution)/shard_map/all_to_all | solution.py:432
  74.6 0.1 sum_quarters.1
  74.6 18.4 %all_to_all.26 = bf16[16,24,128]{2,1,0:T(8,128)(2,1)S(1)} all-to-all(bf16[16,24,128]{2,1,0:T(8,128)(2,1)S(1)} %bitcast.18), channel_id=1, replica_groups=mesh['z'=16,'y'=4,'x'=4,'c'=2] {'z'}, dimensions={0} | all-to-all | bytes 196608 | tf_op jit(solution)/shard_map/all_to_all | solution.py:441
  93.0 0.9 combine.1
Async XLA Ops:
  0.0 13.2 %copy-start.2 = (s32[128,2]{0,1:T(2,128)S(1)}, s32[128,2]{0,1:T(2,128)}, u32[]{:S(2)}) copy-start(s32[128,2]{0,1:T(2,128)} %param.25) | copy-start | bytes 3076
  0.0 13.9 %copy-start.1 = (bf16[2,1024,88]{1,2,0:T(8,128)(2,1)S(1)}, bf16[2,1024,88]{1,2,0:T(8,128)(2,1)}, u32[]{:S(2)}) copy-start(bf16[2,1024,88]{1,2,0:T(8,128)(2,1)} %param.26) | copy-start | bytes 1081348
  4.0 17.2 %all-to-all-start = ((bf16[8,16,1024]{2,1,0:T(8,128)(2,1)}), bf16[8,16,1024]{2,1,0:T(8,128)(2,1)S(1)}, u32[]{:S(2)}, u32[]{:S(2)}) async-start(bf16[8,16,1024]{2,1,0:T(8,128)(2,1)} %bitcast.5), calls=%async_computation | async-start | bytes 524288 | tf_op jit(solution)/shard_map/all_to_all | solution.py:355
  13.9 19.6 %collective-permute-start.1 = (bf16[2,88,1024]{2,1,0:T(8,128)(2,1)S(1)}, bf16[2,88,1024]{2,1,0:T(8,128)(2,1)S(1)}, u32[]{:S(2)}, u32[]{:S(2)}) collective-permute-start(bf16[2,88,1024]{2,1,0:T(8,128)(2,1)S(1)} %bitcast.19), channel_id=1, source_target_pairs={{0,4},{2,6},{4,0},{6,2},{1,5},{3,7},{5,1},{7,3},{8,12},{10,14},{12... | collective-permute-start | bytes 1081352 | tf_op jit(solution)/shard_map/ppermute | solution.py:354
  17.2 16.3 %collective-permute-start = (bf16[2,88,1024]{2,1,0:T(8,128)(2,1)S(1)}, bf16[2,88,1024]{2,1,0:T(8,128)(2,1)S(1)}, u32[]{:S(2)}, u32[]{:S(2)}) collective-permute-start(bf16[2,88,1024]{2,1,0:T(8,128)(2,1)S(1)} %bitcast.20), channel_id=1, source_target_pairs={{0,2},{2,4},{4,6},{6,0},{1,3},{3,5},{5,7},{7,1},{8,10},{10,12},{12... | collective-permute-start | bytes 1081352 | tf_op jit(solution)/shard_map/ppermute | solution.py:354
  22.2 24.2 %all-to-all-start.1 = ((bf16[16,24,128]{2,1,0:T(8,128)(2,1)}), bf16[16,24,128]{2,1,0:T(8,128)(2,1)S(1)}, u32[]{:S(2)}, u32[]{:S(2)}) async-start(bf16[16,24,128]{2,1,0:T(8,128)(2,1)} %bitcast.7), calls=%async_computation.1 | async-start | bytes 196608 | tf_op jit(solution)/shard_map/all_to_all | solution.py:384
  33.6 18.2 %collective-permute-start.2 = (bf16[2,88,1024]{2,1,0:T(8,128)(2,1)S(1)}, bf16[2,88,1024]{2,1,0:T(8,128)(2,1)S(1)}, u32[]{:S(2)}, u32[]{:S(2)}) collective-permute-start(bf16[2,88,1024]{2,1,0:T(8,128)(2,1)S(1)} %bitcast.21), channel_id=1, source_target_pairs={{0,6},{2,0},{4,2},{6,4},{1,7},{3,1},{5,3},{7,5},{8,14},{10,8},{12,... | collective-permute-start | bytes 1081352 | tf_op jit(solution)/shard_map/ppermute | solution.py:394
  47.2 12.0 %all-to-all-start.2 = ((bf16[4,384,128]{2,1,0:T(8,128)(2,1)}), bf16[4,384,128]{2,1,0:T(8,128)(2,1)}, u32[]{:S(2)}, u32[]{:S(2)}) async-start(bf16[4,384,128]{2,1,0:T(8,128)(2,1)} %spread.1.spread_ref), calls=%async_computation.2 | async-start | bytes 786432 | tf_op jit(solution)/shard_map/all_to_all | solution.py:403
  51.8 8.9 %copy-start = (bf16[704,1024]{1,0:T(8,128)(2,1)S(1)}, bf16[704,1024]{1,0:T(8,128)(2,1)}, u32[]{:S(2)}) copy-start(bf16[704,1024]{1,0:T(8,128)(2,1)} %down_ref.1) | copy-start | bytes 4325380
  51.8 8.8 %collective-permute-start.3 = (bf16[4,176,1024]{2,1,0:T(8,128)(2,1)S(1)}, bf16[4,176,1024]{2,1,0:T(8,128)(2,1)}, u32[]{:S(2)}, u32[]{:S(2)}) collective-permute-start(bf16[4,176,1024]{2,1,0:T(8,128)(2,1)S(1)} %stack.1.own_ref), channel_id=1, source_target_pairs={{0,1},{1,0},{2,3},{3,2},{4,5},{5,4},{6,7},{7,6},{8,9},{9,8},{10,11... | collective-permute-start | bytes 4325384 | tf_op jit(solution)/shard_map/ppermute | solution.py:413

commit v4 on v3

--- a/solution.py
+++ b/solution.py
@@ -211,49 +211,61 @@
         out_ref[at] = piece[...]
 
 
-def unpack_kernel(tokens_ref, order_ref, rows_ref):
+def hidden_of(rows, piece):
+    columns = piece.shape[0] // 2
+    projected = dot_nt(rows, piece)
+    gate_val, up_val = projected[:, :columns], projected[:, columns:]
+    return (jax.nn.gelu(gate_val, approximate=True) * up_val).astype(BF)
+
+
+def own_kernel(tokens_hbm, order_ref, own_ref, rows_ref, hidden_ref, tokens_ref, sems):
     groups, chunk_rows, _ = tokens_ref.shape
+    copies = [pltpu.make_async_copy(tokens_hbm.at[at], tokens_ref.at[at], sems.at[at]) for at in range(groups)]
+    for copy in copies:
+        copy.start()
     chunks = rows_ref.shape[1] // LANES
     each = chunk_rows // chunks
     for group in range(groups):
+        copies[group].wait()
         unpacked = dot(order_ref[...], tokens_ref[group]).astype(BF)
         for at in range(chunks):
             rows_ref[group * each : (group + 1) * each, at * LANES : (at + 1) * LANES] = unpacked[
                 at * each : (at + 1) * each
             ]
-
-
-def ffn_kernel(index_ref, rows_ref, order_ref, down_ref, own_ref, other_ref, out_ref, total_ref):
+    for shift in range(own_ref.shape[0]):
+        hidden_ref[shift] = hidden_of(rows_ref[...], own_ref[shift])
+
+
+def ffn_kernel(index_ref, rows_ref, order_ref, down_ref, own_hidden_ref, other_hbm, out_ref, total_ref, other_ref, sems):
+    chips, both, _ = other_ref.shape
+    copies = [pltpu.make_async_copy(other_hbm.at[at], other_ref.at[at], sems.at[at]) for at in range(chips)]
+    for copy in copies:
+        copy.start()
     groups, chunk_rows, _ = out_ref.shape
     width = rows_ref.shape[1]
     chunks = width // LANES
     each = chunk_rows // chunks
-    chips, both, _ = own_ref.shape
-    columns = both // 2
     core = index_ref[0] % 2
     chip = index_ref[0] // 2
 
-    def experts_part(first, second):
+    def experts_part(own_first):
         total = None
         for shift in range(chips):
             came = (chip - shift + chips) % chips
-            hidden = []
-            for pieces in (first, second):
-                projected = dot_nt(rows_ref[...], pieces[shift])
-                gate_val, up_val = projected[:, :columns], projected[:, columns:]
-                hidden.append(jax.nn.gelu(gate_val, approximate=True) * up_val)
-            hidden = jnp.concatenate(hidden, axis=1).astype(BF)
+            copies[shift].wait()
+            pair = [own_hidden_ref[shift], hidden_of(rows_ref[...], other_ref[shift])]
+            hidden = jnp.concatenate(pair if own_first else pair[::-1], axis=1)
             part = dot(hidden, down_ref[pl.ds(pl.multiple_of(came * both, 16), both), :])
             total = part if total is None else total + part
         total_ref[...] = total.astype(BF)
 
     @pl.when(core == 0)
     def _():
-        experts_part(own_ref, other_ref)
+        experts_part(True)
 
     @pl.when(core != 0)
     def _():
-        experts_part(other_ref, own_ref)
+        experts_part(False)
 
     for group in range(groups):
         mine = total_ref[group * each : (group + 1) * each]
@@ -411,24 +423,32 @@
         name="stack",
     )(spread, *own_core)
     other_core = lax.ppermute(stacked, "c", [(0, 1), (1, 0)])
-    rows = pl.pallas_call(
-        unpack_kernel,
-        out_shape=jax.ShapeDtypeStruct((split * experts * CAPACITY, width), BF),
-        in_specs=[VMEM] * 2,
-        out_specs=VMEM,
+    rows, own_hidden = pl.pallas_call(
+        own_kernel,
+        out_shape=(
+            jax.ShapeDtypeStruct((split * experts * CAPACITY, width), BF),
+            jax.ShapeDtypeStruct((row, split * experts * CAPACITY, w_in.shape[2]), BF),
+        ),
+        in_specs=[HBM, VMEM, VMEM],
+        out_specs=(VMEM,) * 2,
+        scratch_shapes=[pltpu.VMEM(spread.shape, BF), pltpu.SemaphoreType.DMA((split,))],
         compiler_params=PARAMS,
         cost_estimate=VERY_LONG,
-        name="unpack",
-    )(tokens, order)
+        name="own",
+    )(in_hbm(tokens), order, stacked)
     projected = pl.pallas_call(
         ffn_kernel,
         out_shape=jax.ShapeDtypeStruct((split, slot_count, LANES), BF),
-        in_specs=[SMEM] + [VMEM] * 5,
-        out_specs=VMEM,
-        scratch_shapes=[pltpu.VMEM((split * experts * CAPACITY, width), BF)],
+        in_specs=[SMEM] + [VMEM] * 4 + [HBM],
+        out_specs=VMEM,
+        scratch_shapes=[
+            pltpu.VMEM((split * experts * CAPACITY, width), BF),
+            pltpu.VMEM(stacked.shape, BF),
+            pltpu.SemaphoreType.DMA((row,)),
+        ],
         compiler_params=PARAMS,
         name="ffn",
-    )(hid_index, rows, order, w_out, stacked, other_core)
+    )(hid_index, rows, order, w_out, own_hidden, in_hbm(other_core))
     quarters = lax.all_to_all(projected, "y", 0, 0, tiled=True)
     summed = pl.pallas_call(
         sum_kernel,

time: 95.1 us -> 95.6 us (level)
  local copies, waits for them, and re-layouts: 0.01 us -> 1.31 us
  blocking collectives: 28.2 us -> 27 us
  Pallas kernels: 13.4 us -> 14.5 us
    all_to_all x1, blocking collectives: 18.4 us -> 17.1 us  [body(): returned = lax.all_to_all(summed.reshape(exchanged), 'z', 0, 0, tiled=True)]
    unnamed x6 -> x14, local copies, waits for them, and re-layouts: 0.01 us -> 1.31 us
    pallas_call x1, Pallas kernels: 1.46 us -> 2.51 us  [body(): pl.pallas_call(own_kernel, out_shape=(jax.ShapeDtypeStruct((split * exper...]
  transfers between devices with their start and end apart: 7 -> 7, of which waited for: 3 -> 2; matrix products, arithmetic and copies ran while one was open for 0% -> 0% of each run, Pallas kernels for 5% -> 6%
where the time goes in v4:
time: 95.6 us; the launch traced here: 95 us
  starting transfers between devices  37.9 us (40%)
  blocking collectives  27 us (28%)
  Pallas kernels  14.5 us (15%)
  waiting for transfers between devices  14.2 us (15%)
  local copies, waits for them, and re-layouts  1.31 us (1%)
    all_to_all x1, blocking collectives, body(): returned = lax.all_to_all(summed.reshape(exchanged), 'z', 0, 0, tiled=True)  17.1 us
    all_to_all x1, starting transfers between devices, body(): arrived = lax.all_to_all(outgoing.reshape(exchanged), 'z', 0, 0, tiled=True)  10.8 us
    all_to_all x1, blocking collectives, body(): quarters = lax.all_to_all(projected, 'y', 0, 0, tiled=True)  9.91 us
    all_to_all x1, starting transfers between devices, body(): lax.all_to_all(partial_mix.reshape(hid_count, block, width), hid, 0, 0, t...  9.21 us
    all_to_all x1, waiting for transfers between devices, body(): arrived = lax.all_to_all(outgoing.reshape(exchanged), 'z', 0, 0, tiled=True)  8.87 us
    ppermute x2, starting transfers between devices, body(): lax.ppermute(w_cols, 'x', move)  7.32 us
    all_to_all x1, waiting for transfers between devices, body(): tokens = lax.all_to_all(spread, 'y', 0, 0, tiled=True)  5.31 us
    all_to_all x1, starting transfers between devices, body(): tokens = lax.all_to_all(spread, 'y', 0, 0, tiled=True)  4.45 us
  transfers between devices with their start and end apart: 7, of which 2 were waited for; matrix products, arithmetic and copies ran while one was open for 0% of the time, Pallas kernels for 6%

profile of v4, /device:TPU:6, one launch (start us, length us, event | category | flops | bytes accessed | tf_op | source)
XLA Modules:
  0.0 95.0 jit_solution(3389713651765011499)
XLA Ops:
  0.0 0.0 copy-start.6
  0.0 0.0 copy-start.1
  0.0 4.0 %attention.1 = (bf16[128,1024]{1,0:T(8,128)(2,1)}, f32[16,1024]{1,0:T(8,128)S(1)}, f32[1,1024]{1,0:T(1,128)S(1)}, bf16[16,1024]{1,0:T(8,128)(2,1)S(1)}) custom-call(s32[1]{0:T(128)} %bitcast.index_ref, bf16[128,1024]{1,0:T(8,128)(2,1)} %resid_hbm.1, f32[1,1024]{1,0:T(1,128)} %bitcast.28, bf16[1024,128]{1,0:T(8,128)(2,1)} %wq_hbm.1, ...), custom_call_target="tpu_custom_call" | custom-call | tf_op jit(solution)/shard_map/attention/pallas_call | solution.py:337
  4.0 9.2 %all-to-all-start = ((bf16[8,16,1024]{2,1,0:T(8,128)(2,1)}), bf16[8,16,1024]{2,1,0:T(8,128)(2,1)S(1)}, u32[]{:S(2)}, u32[]{:S(2)}) async-start(bf16[8,16,1024]{2,1,0:T(8,128)(2,1)} %bitcast.5), calls=%async_computation | async-start | bytes 524288 | tf_op jit(solution)/shard_map/all_to_all | solution.py:367
  13.2 0.0 copy-done.6
  13.2 0.6 routing.1
  13.9 0.0 copy-start.2
  13.9 0.7 copy-done.2
  14.5 0.0 copy-done.1
  14.5 3.3 %collective-permute-start.1 = (bf16[2,88,1024]{2,1,0:T(8,128)(2,1)S(1)}, bf16[2,88,1024]{2,1,0:T(8,128)(2,1)S(1)}, u32[]{:S(2)}, u32[]{:S(2)}) collective-permute-start(bf16[2,88,1024]{2,1,0:T(8,128)(2,1)S(1)} %bitcast.19), channel_id=1, source_target_pairs={{0,4},{2,6},{4,0},{6,2},{1,5},{3,7},{5,1},{7,3},{8,12},{10,14},{12... | collective-permute-start | bytes 1081352 | tf_op jit(solution)/shard_map/ppermute | solution.py:366
  17.9 4.0 %collective-permute-start = (bf16[2,88,1024]{2,1,0:T(8,128)(2,1)S(1)}, bf16[2,88,1024]{2,1,0:T(8,128)(2,1)S(1)}, u32[]{:S(2)}, u32[]{:S(2)}) collective-permute-start(bf16[2,88,1024]{2,1,0:T(8,128)(2,1)S(1)} %bitcast.20), channel_id=1, source_target_pairs={{0,2},{2,4},{4,6},{6,0},{1,3},{3,5},{5,7},{7,1},{8,10},{10,12},{12... | collective-permute-start | bytes 1081352 | tf_op jit(solution)/shard_map/ppermute | solution.py:366
  21.9 0.0 all-to-all-done.parts_ref
  21.9 0.1 mix.1
  22.0 0.0 copy-start.4
  22.0 0.6 copy-done.4
  22.6 0.8 dispatch.1
  23.4 10.8 %all-to-all-start.1 = ((bf16[16,24,128]{2,1,0:T(8,128)(2,1)}), bf16[16,24,128]{2,1,0:T(8,128)(2,1)S(1)}, u32[]{:S(2)}, u32[]{:S(2)}) async-start(bf16[16,24,128]{2,1,0:T(8,128)(2,1)} %bitcast.7), calls=%async_computation.1 | async-start | bytes 196608 | tf_op jit(solution)/shard_map/all_to_all | solution.py:396
  34.2 0.2 gates.1.tokens_ref.gates_ref
  34.4 0.3 order.1.order_ref
  34.7 0.0 collective-permute-done.1
  34.7 0.0 collective-permute-done
  34.8 4.1 %collective-permute-start.2 = (bf16[2,88,1024]{2,1,0:T(8,128)(2,1)S(1)}, bf16[2,88,1024]{2,1,0:T(8,128)(2,1)S(1)}, u32[]{:S(2)}, u32[]{:S(2)}) collective-permute-start(bf16[2,88,1024]{2,1,0:T(8,128)(2,1)S(1)} %bitcast.21), channel_id=1, source_target_pairs={{0,6},{2,0},{4,2},{6,4},{1,7},{3,1},{5,3},{7,5},{8,14},{10,8},{12,... | collective-permute-start | bytes 1081352 | tf_op jit(solution)/shard_map/ppermute | solution.py:406
  38.9 8.9 %all-to-all-done.1 = bf16[16,24,128]{2,1,0:T(8,128)(2,1)S(1)} async-done(((bf16[16,24,128]{2,1,0:T(8,128)(2,1)}), bf16[16,24,128]{2,1,0:T(8,128)(2,1)S(1)}, u32[]{:S(2)}, u32[]{:S(2)}) %all-to-all-start.1) | async-done | bytes 98336 | tf_op jit(solution)/shard_map/all_to_all | solution.py:396
  47.7 0.8 spread.1.spread_ref
  48.5 4.5 %all-to-all-start.2 = ((bf16[4,384,128]{2,1,0:T(8,128)(2,1)}), bf16[4,384,128]{2,1,0:T(8,128)(2,1)}, u32[]{:S(2)}, u32[]{:S(2)}) async-start(bf16[4,384,128]{2,1,0:T(8,128)(2,1)} %spread.1.spread_ref), calls=%async_computation.2 | async-start | bytes 786432 | tf_op jit(solution)/shard_map/all_to_all | solution.py:415
  53.0 0.0 collective-permute-done.2
  53.0 0.1 stack.1.own_ref
  53.1 0.0 copy-start
  53.1 2.1 %collective-permute-start.3 = (bf16[4,176,1024]{2,1,0:T(8,128)(2,1)S(1)}, bf16[4,176,1024]{2,1,0:T(8,128)(2,1)}, u32[]{:S(2)}, u32[]{:S(2)}) collective-permute-start(bf16[4,176,1024]{2,1,0:T(8,128)(2,1)S(1)} %stack.1.own_ref), channel_id=1, source_target_pairs={{0,1},{1,0},{2,3},{3,2},{4,5},{5,4},{6,7},{7,6},{8,9},{9,8},{10,11... | collective-permute-start | bytes 4325384 | tf_op jit(solution)/shard_map/ppermute | solution.py:425
  55.1 5.3 %all-to-all-done.2.tokens_hbm = bf16[4,384,128]{2,1,0:T(8,128)(2,1)} async-done(((bf16[4,384,128]{2,1,0:T(8,128)(2,1)}), bf16[4,384,128]{2,1,0:T(8,128)(2,1)}, u32[]{:S(2)}, u32[]{:S(2)}) %all-to-all-start.2) | async-done | bytes 393248 | tf_op jit(solution)/shard_map/all_to_all | solution.py:415
  60.5 2.5 %own.1 = (bf16[192,1024]{1,0:T(8,128)(2,1)S(1)}, bf16[4,192,88]{2,1,0:T(8,128)(2,1)S(1)}) custom-call(bf16[4,384,128]{2,1,0:T(8,128)(2,1)} %all-to-all-done.2.tokens_hbm, bf16[384,384]{1,0:T(8,128)(2,1)S(1)} %order.1.order_ref, bf16[4,176,1024]{2,1,0:T(8,128)(2,1)S(1)} %stack.1.own_ref), custom_call_target="tpu_custom_call" | custom-call | flops 20000000000 | bytes 2097152 | tf_op jit(solution)/shard_map/own/pallas_call | solution.py:426
  63.0 0.0 collective-permute-done.3.other_hbm
  63.0 0.0 copy-done
  63.0 4.1 %ffn.1 = bf16[4,384,128]{2,1,0:T(8,128)(2,1)S(1)} custom-call(s32[1]{0:T(128)} %bitcast.index_ref, bf16[192,1024]{1,0:T(8,128)(2,1)S(1)} %get-tuple-element.35.rows_ref, bf16[384,384]{1,0:T(8,128)(2,1)S(1)} %order.1.order_ref, bf16[704,1024]{1,0:T(8,128)(2,1)S(1)} %copy-done, bf16[4,192,88]{2,1,0:T(8,128)(2,1)S(1)} %get-tuple-element.36.own_hidden_ref, ...), custom_call_target="tpu_custom_call" | custom-call | tf_op jit(solution)/shard_map/ffn/pallas_call | solution.py:439
  67.1 0.0 copy-start.3
  67.1 0.0 copy-start.5
  67.2 9.9 %all_to_all.25.parts_ref = bf16[4,384,128]{2,1,0:T(8,128)(2,1)S(1)} all-to-all(bf16[4,384,128]{2,1,0:T(8,128)(2,1)S(1)} %ffn.1), channel_id=1, replica_groups=mesh['z'=16,'y'=4,'x'=4,'c'=2] {'y'}, dimensions={0} | all-to-all | bytes 786432 | tf_op jit(solution)/shard_map/all_to_all | solution.py:452
  77.1 0.1 sum_quarters.1
  77.1 17.1 %all_to_all.26 = bf16[16,24,128]{2,1,0:T(8,128)(2,1)S(1)} all-to-all(bf16[16,24,128]{2,1,0:T(8,128)(2,1)S(1)} %bitcast.18), channel_id=1, replica_groups=mesh['z'=16,'y'=4,'x'=4,'c'=2] {'z'}, dimensions={0} | all-to-all | bytes 196608 | tf_op jit(solution)/shard_map/all_to_all | solution.py:461
  94.2 0.0 copy-done.3
  94.2 0.0 copy-done.5
  94.2 0.9 combine.1
Async XLA Ops:
  0.0 13.2 %copy-start.6 = (s32[128,2]{0,1:T(2,128)S(1)}, s32[128,2]{0,1:T(2,128)}, u32[]{:S(2)}) copy-start(s32[128,2]{0,1:T(2,128)} %param.25) | copy-start | bytes 3076
  0.0 14.5 %copy-start.1 = (bf16[2,1024,88]{1,2,0:T(8,128)(2,1)S(1)}, bf16[2,1024,88]{1,2,0:T(8,128)(2,1)}, u32[]{:S(2)}) copy-start(bf16[2,1024,88]{1,2,0:T(8,128)(2,1)} %param.26) | copy-start | bytes 1081348
  4.0 17.9 %all-to-all-start = ((bf16[8,16,1024]{2,1,0:T(8,128)(2,1)}), bf16[8,16,1024]{2,1,0:T(8,128)(2,1)S(1)}, u32[]{:S(2)}, u32[]{:S(2)}) async-start(bf16[8,16,1024]{2,1,0:T(8,128)(2,1)} %bitcast.5), calls=%async_computation | async-start | bytes 524288 | tf_op jit(solution)/shard_map/all_to_all | solution.py:367
  13.9 0.7 copy-start.2
  14.5 20.2 %collective-permute-start.1 = (bf16[2,88,1024]{2,1,0:T(8,128)(2,1)S(1)}, bf16[2,88,1024]{2,1,0:T(8,128)(2,1)S(1)}, u32[]{:S(2)}, u32[]{:S(2)}) collective-permute-start(bf16[2,88,1024]{2,1,0:T(8,128)(2,1)S(1)} %bitcast.19), channel_id=1, source_target_pairs={{0,4},{2,6},{4,0},{6,2},{1,5},{3,7},{5,1},{7,3},{8,12},{10,14},{12... | collective-permute-start | bytes 1081352 | tf_op jit(solution)/shard_map/ppermute | solution.py:366
  17.9 16.9 %collective-permute-start = (bf16[2,88,1024]{2,1,0:T(8,128)(2,1)S(1)}, bf16[2,88,1024]{2,1,0:T(8,128)(2,1)S(1)}, u32[]{:S(2)}, u32[]{:S(2)}) collective-permute-start(bf16[2,88,1024]{2,1,0:T(8,128)(2,1)S(1)} %bitcast.20), channel_id=1, source_target_pairs={{0,2},{2,4},{4,6},{6,0},{1,3},{3,5},{5,7},{7,1},{8,10},{10,12},{12... | collective-permute-start | bytes 1081352 | tf_op jit(solution)/shard_map/ppermute | solution.py:366
  22.0 0.6 copy-start.4
  23.4 24.3 %all-to-all-start.1 = ((bf16[16,24,128]{2,1,0:T(8,128)(2,1)}), bf16[16,24,128]{2,1,0:T(8,128)(2,1)S(1)}, u32[]{:S(2)}, u32[]{:S(2)}) async-start(bf16[16,24,128]{2,1,0:T(8,128)(2,1)} %bitcast.7), calls=%async_computation.1 | async-start | bytes 196608 | tf_op jit(solution)/shard_map/all_to_all | solution.py:396
  34.8 18.2 %collective-permute-start.2 = (bf16[2,88,1024]{2,1,0:T(8,128)(2,1)S(1)}, bf16[2,88,1024]{2,1,0:T(8,128)(2,1)S(1)}, u32[]{:S(2)}, u32[]{:S(2)}) collective-permute-start(bf16[2,88,1024]{2,1,0:T(8,128)(2,1)S(1)} %bitcast.21), channel_id=1, source_target_pairs={{0,6},{2,0},{4,2},{6,4},{1,7},{3,1},{5,3},{7,5},{8,14},{10,8},{12,... | collective-permute-start | bytes 1081352 | tf_op jit(solution)/shard_map/ppermute | solution.py:406
  48.5 11.9 %all-to-all-start.2 = ((bf16[4,384,128]{2,1,0:T(8,128)(2,1)}), bf16[4,384,128]{2,1,0:T(8,128)(2,1)}, u32[]{:S(2)}, u32[]{:S(2)}) async-start(bf16[4,384,128]{2,1,0:T(8,128)(2,1)} %spread.1.spread_ref), calls=%async_computation.2 | async-start | bytes 786432 | tf_op jit(solution)/shard_map/all_to_all | solution.py:415
  53.1 9.9 %copy-start = (bf16[704,1024]{1,0:T(8,128)(2,1)S(1)}, bf16[704,1024]{1,0:T(8,128)(2,1)}, u32[]{:S(2)}) copy-start(bf16[704,1024]{1,0:T(8,128)(2,1)} %down_ref.1) | copy-start | bytes 4325380
  53.1 9.9 %collective-permute-start.3 = (bf16[4,176,1024]{2,1,0:T(8,128)(2,1)S(1)}, bf16[4,176,1024]{2,1,0:T(8,128)(2,1)}, u32[]{:S(2)}, u32[]{:S(2)}) collective-permute-start(bf16[4,176,1024]{2,1,0:T(8,128)(2,1)S(1)} %stack.1.own_ref), channel_id=1, source_target_pairs={{0,1},{1,0},{2,3},{3,2},{4,5},{5,4},{6,7},{7,6},{8,9},{9,8},{10,11... | collective-permute-start | bytes 4325384 | tf_op jit(solution)/shard_map/ppermute | solution.py:425
  67.1 27.0 %copy-start.3 = (bf16[2,384,128]{2,1,0:T(8,128)(2,1)S(1)}, bf16[2,384,128]{2,1,0:T(8,128)(2,1)}, u32[]{:S(2)}) copy-start(bf16[2,384,128]{2,1,0:T(8,128)(2,1)} %copy-done.2) | copy-start | bytes 589828
  67.1 27.0 %copy-start.5 = (f32[16,1024]{1,0:T(8,128)S(1)}, f32[16,1024]{1,0:T(8,128)}, u32[]{:S(2)}) copy-start(f32[16,1024]{1,0:T(8,128)} %copy-done.4) | copy-start | bytes 196612

commit v5 on v4

--- a/solution.py
+++ b/solution.py
@@ -145,7 +145,7 @@
     ]
 
 
-def routing_kernel(index_ref, routes_ref, gain_ref, chosen_ref, select_ref, column_ref):
+def routing_kernel(index_ref, routes_ref, gain_ref, chosen_ref, target_ref, column_ref):
     block = column_ref.shape[1]
     chunks = gain_ref.shape[1] // LANES
     rows = [own_routes(routes_ref, which, index_ref[0], block) for which in range(2)]
@@ -156,18 +156,21 @@
     for which in range(2):
         target = placement(rows[which], columns, block, CAPACITY)
         here = jnp.where(same & (wanted == target), 1.0, 0.0)
-        select_ref[which] = here.astype(BF)
+        target_ref[pl.ds(which, 1), :] = target
         both = here if both is None else both + here
         column_ref[which] = jnp.broadcast_to(columns[which], (block, LANES))
     chosen_ref[...] = both.astype(BF)
 
 
-def mix_kernel(parts_ref, own_ref, gain_ref, after_ref, ffn_in_ref):
+def residual(parts_ref, own_ref):
     mixed = parts_ref[0].astype(F32)
     for source in range(1, parts_ref.shape[0]):
         mixed = mixed + parts_ref[source].astype(F32)
-    after = own_ref[...] + mixed
-    after_ref[...] = after
+    return own_ref[...] + mixed
+
+
+def mix_kernel(parts_ref, own_ref, gain_ref, ffn_in_ref):
+    after = residual(parts_ref, own_ref)
     inverse = lax.rsqrt(jnp.mean(after * after, axis=-1, keepdims=True) + EPS)
     ffn_in_ref[...] = (after * inverse * gain_ref[...]).astype(BF)
 
@@ -178,7 +181,8 @@
     out_ref[...] = dot(chosen_ref[...], stacked).astype(BF)
 
 
-def gates_kernel(ffn_in_ref, router_ref, column_ref, gates_ref):
+def gates_kernel(ffn_in_ref, router_ref, column_ref, parts_ref, own_ref, gates_ref, after_ref):
+    after_ref[...] = residual(parts_ref, own_ref)
     block = ffn_in_ref.shape[0]
     experts = router_ref.shape[0]
     logits = dot_nt(ffn_in_ref[...], router_ref[...])
@@ -218,11 +222,13 @@
     return (jax.nn.gelu(gate_val, approximate=True) * up_val).astype(BF)
 
 
-def own_kernel(tokens_hbm, order_ref, own_ref, rows_ref, hidden_ref, tokens_ref, sems):
-    groups, chunk_rows, _ = tokens_ref.shape
-    copies = [pltpu.make_async_copy(tokens_hbm.at[at], tokens_ref.at[at], sems.at[at]) for at in range(groups)]
+def own_kernel(tokens_hbm, order_ref, own_ref, down_hbm, rows_ref, hidden_ref, down_ref, tokens_ref, sems, sem):
+    copies = [pltpu.make_async_copy(tokens_hbm.at[at], tokens_ref.at[at], sems.at[at]) for at in range(tokens_ref.shape[0])]
     for copy in copies:
         copy.start()
+    fetch = pltpu.make_async_copy(down_hbm, down_ref, sem)
+    fetch.start()
+    groups, chunk_rows, _ = tokens_ref.shape
     chunks = rows_ref.shape[1] // LANES
     each = chunk_rows // chunks
     for group in range(groups):
@@ -234,13 +240,11 @@
             ]
     for shift in range(own_ref.shape[0]):
         hidden_ref[shift] = hidden_of(rows_ref[...], own_ref[shift])
-
-
-def ffn_kernel(index_ref, rows_ref, order_ref, down_ref, own_hidden_ref, other_hbm, out_ref, total_ref, other_ref, sems):
+    fetch.wait()
+
+
+def ffn_kernel(index_ref, rows_ref, order_ref, down_ref, own_hidden_ref, other_ref, out_ref, total_ref):
     chips, both, _ = other_ref.shape
-    copies = [pltpu.make_async_copy(other_hbm.at[at], other_ref.at[at], sems.at[at]) for at in range(chips)]
-    for copy in copies:
-        copy.start()
     groups, chunk_rows, _ = out_ref.shape
     width = rows_ref.shape[1]
     chunks = width // LANES
@@ -252,7 +256,6 @@
         total = None
         for shift in range(chips):
             came = (chip - shift + chips) % chips
-            copies[shift].wait()
             pair = [own_hidden_ref[shift], hidden_of(rows_ref[...], other_ref[shift])]
             hidden = jnp.concatenate(pair if own_first else pair[::-1], axis=1)
             part = dot(hidden, down_ref[pl.ds(pl.multiple_of(came * both, 16), both), :])
@@ -280,10 +283,15 @@
     out_ref[...] = total.astype(BF)
 
 
-def combine_kernel(experts_ref, after_ref, gates_ref, select_ref, out_ref):
+def combine_kernel(experts_ref, after_ref, gates_ref, target_ref, out_ref):
     block, width = after_ref.shape
     chunks = width // LANES
-    picked = [dot_tn(select_ref[which], experts_ref[...]) for which in range(2)]
+    wanted, chunk = slot_rows(experts_ref.shape[0], CAPACITY, chunks)
+    same = chunk == iota(chunk.shape, 1) // block
+    picked = []
+    for which in range(2):
+        chosen = same & (wanted == target_ref[pl.ds(which, 1), :])
+        picked.append(dot_tn(jnp.where(chosen, 1.0, 0.0).astype(BF), experts_ref[...]))
     for at in range(chunks):
         lanes = slice(at * LANES, (at + 1) * LANES)
         mine = slice(at * block, (at + 1) * block)
@@ -349,11 +357,11 @@
         compiler_params=PARAMS,
         name="attention",
     )(hid_index, *map(in_hbm, operands))
-    chosen, select, column = pl.pallas_call(
+    chosen, target, column = pl.pallas_call(
         routing_kernel,
         out_shape=(
             jax.ShapeDtypeStruct((slot_count, LANES), BF),
-            jax.ShapeDtypeStruct((2, slot_count, LANES), BF),
+            jax.ShapeDtypeStruct((2, LANES), jnp.int32),
             jax.ShapeDtypeStruct((2, block, LANES), jnp.int32),
         ),
         in_specs=[SMEM, VMEM, VMEM],
@@ -365,11 +373,11 @@
     moves = [[(at, (at + shift) % row) for at in range(row)] for shift in range(row)]
     own_core = [w_cols] + [lax.ppermute(w_cols, "x", move) for move in moves[1:-1]]
     parts = lax.all_to_all(partial_mix.reshape(hid_count, block, width), hid, 0, 0, tiled=True)
-    after, ffn_in = pl.pallas_call(
+    ffn_in = pl.pallas_call(
         mix_kernel,
-        out_shape=(jax.ShapeDtypeStruct((block, width), F32), jax.ShapeDtypeStruct((block, width), BF)),
+        out_shape=jax.ShapeDtypeStruct((block, width), BF),
         in_specs=[VMEM] * 3,
-        out_specs=(VMEM,) * 2,
+        out_specs=VMEM,
         compiler_params=PARAMS,
         cost_estimate=LONG,
         name="mix",
@@ -383,15 +391,15 @@
         cost_estimate=LONG,
         name="dispatch",
     )(ffn_in, chosen)
-    gates = pl.pallas_call(
+    gates, after = pl.pallas_call(
         gates_kernel,
-        out_shape=jax.ShapeDtypeStruct((2, block, LANES), F32),
-        in_specs=[VMEM] * 3,
-        out_specs=VMEM,
+        out_shape=(jax.ShapeDtypeStruct((2, block, LANES), F32), jax.ShapeDtypeStruct((block, width), F32)),
+        in_specs=[VMEM] * 5,
+        out_specs=(VMEM,) * 2,
         compiler_params=PARAMS,
         cost_estimate=LONG,
         name="gates",
-    )(ffn_in, router_rows, column)
+    )(ffn_in, router_rows, column, parts, own)
     exchanged = (experts, chunks * CAPACITY, LANES)
     arrived = lax.all_to_all(outgoing.reshape(exchanged), "z", 0, 0, tiled=True)
     order = pl.pallas_call(
@@ -423,32 +431,31 @@
         name="stack",
     )(spread, *own_core)
     other_core = lax.ppermute(stacked, "c", [(0, 1), (1, 0)])
-    rows, own_hidden = pl.pallas_call(
+    rows, own_hidden, down = pl.pallas_call(
         own_kernel,
         out_shape=(
             jax.ShapeDtypeStruct((split * experts * CAPACITY, width), BF),
             jax.ShapeDtypeStruct((row, split * experts * CAPACITY, w_in.shape[2]), BF),
+            jax.ShapeDtypeStruct(w_out.shape, BF),
         ),
-        in_specs=[HBM, VMEM, VMEM],
-        out_specs=(VMEM,) * 2,
-        scratch_shapes=[pltpu.VMEM(spread.shape, BF), pltpu.SemaphoreType.DMA((split,))],
+        in_specs=[HBM, VMEM, VMEM, HBM],
+        out_specs=(VMEM,) * 3,
+        scratch_shapes=[pltpu.VMEM(spread.shape, BF), pltpu.SemaphoreType.DMA((split,)), pltpu.SemaphoreType.DMA],
         compiler_params=PARAMS,
         cost_estimate=VERY_LONG,
         name="own",
-    )(in_hbm(tokens), order, stacked)
+    )(in_hbm(tokens), order, stacked, in_hbm(w_out))
     projected = pl.pallas_call(
         ffn_kernel,
         out_shape=jax.ShapeDtypeStruct((split, slot_count, LANES), BF),
-        in_specs=[SMEM] + [VMEM] * 4 + [HBM],
+        in_specs=[SMEM] + [VMEM] * 5,
         out_specs=VMEM,
         scratch_shapes=[
             pltpu.VMEM((split * experts * CAPACITY, width), BF),
-            pltpu.VMEM(stacked.shape, BF),
-            pltpu.SemaphoreType.DMA((row,)),
         ],
         compiler_params=PARAMS,
         name="ffn",
-    )(hid_index, rows, order, w_out, own_hidden, in_hbm(other_core))
+    )(hid_index, rows, order, down, own_hidden, other_core)
     quarters = lax.all_to_all(projected, "y", 0, 0, tiled=True)
     summed = pl.pallas_call(
         sum_kernel,
@@ -466,7 +473,7 @@
         out_specs=VMEM,
         compiler_params=PARAMS,
         name="combine",
-    )(returned.reshape(slot_count, LANES), after, gates, select)
+    )(returned.reshape(slot_count, LANES), after, gates, target)
 
 
 def solution(mesh):

time: 95.6 us -> 92.5 us (0.968)
  Pallas kernels: 14.5 us -> 13.2 us
  starting transfers between devices: 37.9 us -> 36.6 us
  local copies, waits for them, and re-layouts: 1.31 us -> 0.34 us
    pallas_call x1, Pallas kernels: 4.12 us -> 2.57 us  [body(): pl.pallas_call(ffn_kernel, out_shape=jax.ShapeDtypeStruct((split, slot_co...]
    unnamed x14 -> x12, local copies, waits for them, and re-layouts: 1.31 us -> 0.34 us
where the time goes in v5:
time: 92.5 us; the launch traced here: 91.9 us
  starting transfers between devices  36.6 us (40%)
  blocking collectives  27 us (29%)
  waiting for transfers between devices  14.6 us (16%)
  Pallas kernels  13.2 us (14%)
    all_to_all x1, blocking collectives, body(): returned = lax.all_to_all(summed.reshape(exchanged), 'z', 0, 0, tiled=True)  17.1 us
    all_to_all x1, starting transfers between devices, body(): arrived = lax.all_to_all(outgoing.reshape(exchanged), 'z', 0, 0, tiled=True)  10.8 us
    all_to_all x1, blocking collectives, body(): quarters = lax.all_to_all(projected, 'y', 0, 0, tiled=True)  9.91 us
    all_to_all x1, starting transfers between devices, body(): lax.all_to_all(partial_mix.reshape(hid_count, block, width), hid, 0, 0, t...  9.21 us
    all_to_all x1, waiting for transfers between devices, body(): arrived = lax.all_to_all(outgoing.reshape(exchanged), 'z', 0, 0, tiled=True)  9.14 us
    ppermute x2, starting transfers between devices, body(): lax.ppermute(w_cols, 'x', move)  6.73 us
    all_to_all x1, waiting for transfers between devices, body(): tokens = lax.all_to_all(spread, 'y', 0, 0, tiled=True)  5.46 us
    all_to_all x1, starting transfers between devices, body(): tokens = lax.all_to_all(spread, 'y', 0, 0, tiled=True)  4.44 us
  transfers between devices with their start and end apart: 7, of which 2 were waited for; matrix products, arithmetic and copies ran while one was open for 0% of the time, Pallas kernels for 6%

profile of v5, /device:TPU:6, one launch (start us, length us, event | category | flops | bytes accessed | tf_op | source)
XLA Modules:
  0.0 91.9 jit_solution(15222764186053755963)
XLA Ops:
  0.0 0.0 copy-start.5
  0.0 0.0 copy-start
  0.0 4.0 %attention.1 = (bf16[128,1024]{1,0:T(8,128)(2,1)}, f32[16,1024]{1,0:T(8,128)S(1)}, f32[1,1024]{1,0:T(1,128)S(1)}, bf16[16,1024]{1,0:T(8,128)(2,1)S(1)}) custom-call(s32[1]{0:T(128)} %bitcast.index_ref, bf16[128,1024]{1,0:T(8,128)(2,1)} %resid_hbm.1, f32[1,1024]{1,0:T(1,128)} %bitcast.28, bf16[1024,128]{1,0:T(8,128)(2,1)} %wq_hbm.1, ...), custom_call_target="tpu_custom_call" | custom-call | tf_op jit(solution)/shard_map/attention/pallas_call | solution.py:345
  4.0 9.2 %all-to-all-start = ((bf16[8,16,1024]{2,1,0:T(8,128)(2,1)}), bf16[8,16,1024]{2,1,0:T(8,128)(2,1)S(1)}, u32[]{:S(2)}, u32[]{:S(2)}) async-start(bf16[8,16,1024]{2,1,0:T(8,128)(2,1)} %bitcast.5), calls=%async_computation | async-start | bytes 524288 | tf_op jit(solution)/shard_map/all_to_all | solution.py:375
  13.2 0.0 copy-done.5
  13.2 0.6 routing.1
  13.8 0.0 copy-start.3
  13.8 0.0 copy-done
  13.9 2.0 %collective-permute-start = (bf16[2,88,1024]{2,1,0:T(8,128)(2,1)S(1)}, bf16[2,88,1024]{2,1,0:T(8,128)(2,1)S(1)}, u32[]{:S(2)}, u32[]{:S(2)}) collective-permute-start(bf16[2,88,1024]{2,1,0:T(8,128)(2,1)S(1)} %bitcast.19), channel_id=1, source_target_pairs={{0,2},{2,4},{4,6},{6,0},{1,3},{3,5},{5,7},{7,1},{8,10},{10,12},{12... | collective-permute-start | bytes 1081352 | tf_op jit(solution)/shard_map/ppermute | solution.py:374
  15.9 0.0 copy-done.3
  15.9 4.7 %collective-permute-start.1 = (bf16[2,88,1024]{2,1,0:T(8,128)(2,1)S(1)}, bf16[2,88,1024]{2,1,0:T(8,128)(2,1)S(1)}, u32[]{:S(2)}, u32[]{:S(2)}) collective-permute-start(bf16[2,88,1024]{2,1,0:T(8,128)(2,1)S(1)} %bitcast.20), channel_id=1, source_target_pairs={{0,4},{2,6},{4,0},{6,2},{1,5},{3,7},{5,1},{7,3},{8,12},{10,14},{12... | collective-permute-start | bytes 1081352 | tf_op jit(solution)/shard_map/ppermute | solution.py:374
  20.6 0.0 all-to-all-done.parts_ref
  20.6 0.1 mix.1.ffn_in_ref
  20.7 0.8 dispatch.1
  21.6 10.8 %all-to-all-start.1 = ((bf16[16,24,128]{2,1,0:T(8,128)(2,1)}), bf16[16,24,128]{2,1,0:T(8,128)(2,1)S(1)}, u32[]{:S(2)}, u32[]{:S(2)}) async-start(bf16[16,24,128]{2,1,0:T(8,128)(2,1)} %bitcast.7), calls=%async_computation.1 | async-start | bytes 196608 | tf_op jit(solution)/shard_map/all_to_all | solution.py:404
  32.3 0.2 gates.1
  32.6 0.0 copy-start.1
  32.6 0.3 order.1.order_ref
  32.9 0.0 collective-permute-done
  32.9 0.0 collective-permute-done.1
  32.9 0.3 copy-done.1
  33.2 3.5 %collective-permute-start.2 = (bf16[2,88,1024]{2,1,0:T(8,128)(2,1)S(1)}, bf16[2,88,1024]{2,1,0:T(8,128)(2,1)S(1)}, u32[]{:S(2)}, u32[]{:S(2)}) collective-permute-start(bf16[2,88,1024]{2,1,0:T(8,128)(2,1)S(1)} %bitcast.21), channel_id=1, source_target_pairs={{0,6},{2,0},{4,2},{6,4},{1,7},{3,1},{5,3},{7,5},{8,14},{10,8},{12,... | collective-permute-start | bytes 1081352 | tf_op jit(solution)/shard_map/ppermute | solution.py:414
  36.7 9.1 %all-to-all-done.1 = bf16[16,24,128]{2,1,0:T(8,128)(2,1)S(1)} async-done(((bf16[16,24,128]{2,1,0:T(8,128)(2,1)}), bf16[16,24,128]{2,1,0:T(8,128)(2,1)S(1)}, u32[]{:S(2)}, u32[]{:S(2)}) %all-to-all-start.1) | async-done | bytes 98336 | tf_op jit(solution)/shard_map/all_to_all | solution.py:404
  45.8 0.8 spread.1.spread_ref
  46.6 4.4 %all-to-all-start.2 = ((bf16[4,384,128]{2,1,0:T(8,128)(2,1)}), bf16[4,384,128]{2,1,0:T(8,128)(2,1)}, u32[]{:S(2)}, u32[]{:S(2)}) async-start(bf16[4,384,128]{2,1,0:T(8,128)(2,1)} %spread.1.spread_ref), calls=%async_computation.2 | async-start | bytes 786432 | tf_op jit(solution)/shard_map/all_to_all | solution.py:423
  51.1 0.0 collective-permute-done.2
  51.1 0.1 stack.1.own_ref
  51.2 1.9 %collective-permute-start.3 = (bf16[4,176,1024]{2,1,0:T(8,128)(2,1)S(1)}, bf16[4,176,1024]{2,1,0:T(8,128)(2,1)S(1)}, u32[]{:S(2)}, u32[]{:S(2)}) collective-permute-start(bf16[4,176,1024]{2,1,0:T(8,128)(2,1)S(1)} %stack.1.own_ref), channel_id=1, source_target_pairs={{0,1},{1,0},{2,3},{3,2},{4,5},{5,4},{6,7},{7,6},{8,9},{9,8},{10,11... | collective-permute-start | bytes 4325384 | tf_op jit(solution)/shard_map/ppermute | solution.py:433
  53.1 5.5 %all-to-all-done.2.tokens_hbm = bf16[4,384,128]{2,1,0:T(8,128)(2,1)} async-done(((bf16[4,384,128]{2,1,0:T(8,128)(2,1)}), bf16[4,384,128]{2,1,0:T(8,128)(2,1)}, u32[]{:S(2)}, u32[]{:S(2)}) %all-to-all-start.2) | async-done | bytes 393248 | tf_op jit(solution)/shard_map/all_to_all | solution.py:423
  58.5 2.5 %own.1 = (bf16[192,1024]{1,0:T(8,128)(2,1)S(1)}, bf16[4,192,88]{2,1,0:T(8,128)(2,1)S(1)}, bf16[704,1024]{1,0:T(8,128)(2,1)S(1)}) custom-call(bf16[4,384,128]{2,1,0:T(8,128)(2,1)} %all-to-all-done.2.tokens_hbm, bf16[384,384]{1,0:T(8,128)(2,1)S(1)} %order.1.order_ref, bf16[4,176,1024]{2,1,0:T(8,128)(2,1)S(1)} %stack.1.own_ref, bf16[704,1024]{1,0:T(8,128)(2,1)} %down_hbm.1), custom_call_target="tpu_custom_call" | custom-call | flops 20000000000 | bytes 2097152 | tf_op jit(solution)/shard_map/own/pallas_call | solution.py:434
  61.1 0.0 collective-permute-done.3.other_ref
  61.1 2.6 %ffn.1 = bf16[4,384,128]{2,1,0:T(8,128)(2,1)S(1)} custom-call(s32[1]{0:T(128)} %bitcast.index_ref, bf16[192,1024]{1,0:T(8,128)(2,1)S(1)} %get-tuple-element.36.rows_ref, bf16[384,384]{1,0:T(8,128)(2,1)S(1)} %order.1.order_ref, bf16[704,1024]{1,0:T(8,128)(2,1)S(1)} %get-tuple-element.37.down_ref, bf16[4,192,88]{2,1,0:T(8,128)(2,1)S(1)} %get-tuple-element.38.own_hidden_ref, ...), custom_call_target="tpu_custom_call" | custom-call | tf_op jit(solution)/shard_map/ffn/pallas_call | solution.py:448
  63.7 0.0 copy-start.2
  63.7 0.0 copy-start.4
  63.7 9.9 %all_to_all.25.parts_ref = bf16[4,384,128]{2,1,0:T(8,128)(2,1)S(1)} all-to-all(bf16[4,384,128]{2,1,0:T(8,128)(2,1)S(1)} %ffn.1), channel_id=1, replica_groups=mesh['z'=16,'y'=4,'x'=4,'c'=2] {'y'}, dimensions={0} | all-to-all | bytes 786432 | tf_op jit(solution)/shard_map/all_to_all | solution.py:459
  73.6 0.1 sum_quarters.1
  73.6 17.1 %all_to_all.26 = bf16[16,24,128]{2,1,0:T(8,128)(2,1)S(1)} all-to-all(bf16[16,24,128]{2,1,0:T(8,128)(2,1)S(1)} %bitcast.18), channel_id=1, replica_groups=mesh['z'=16,'y'=4,'x'=4,'c'=2] {'z'}, dimensions={0} | all-to-all | bytes 196608 | tf_op jit(solution)/shard_map/all_to_all | solution.py:468
  90.8 0.0 copy-done.2
  90.8 0.0 copy-done.4
  90.8 1.1 %combine.1 = bf16[16,1024]{1,0:T(8,128)(2,1)} custom-call(bf16[384,128]{1,0:T(8,128)(2,1)S(1)} %bitcast.16, f32[16,1024]{1,0:T(8,128)S(1)} %copy-done.2, f32[2,16,128]{2,1,0:T(8,128)S(1)} %get-tuple-element.30.tokens_ref.gates_ref, s32[2,128]{1,0:T(2,128)S(1)} %copy-done.4), custom_call_target="tpu_custom_call" | custom-call | tf_op jit(solution)/shard_map/combine/pallas_call | solution.py:469
Async XLA Ops:
  0.0 13.2 %copy-start.5 = (s32[128,2]{0,1:T(2,128)S(1)}, s32[128,2]{0,1:T(2,128)}, u32[]{:S(2)}) copy-start(s32[128,2]{0,1:T(2,128)} %param.25) | copy-start | bytes 3076
  0.0 13.8 %copy-start = (bf16[2,1024,88]{1,2,0:T(8,128)(2,1)S(1)}, bf16[2,1024,88]{1,2,0:T(8,128)(2,1)}, u32[]{:S(2)}) copy-start(bf16[2,1024,88]{1,2,0:T(8,128)(2,1)} %param.26) | copy-start | bytes 1081348
  4.0 16.6 %all-to-all-start = ((bf16[8,16,1024]{2,1,0:T(8,128)(2,1)}), bf16[8,16,1024]{2,1,0:T(8,128)(2,1)S(1)}, u32[]{:S(2)}, u32[]{:S(2)}) async-start(bf16[8,16,1024]{2,1,0:T(8,128)(2,1)} %bitcast.5), calls=%async_computation | async-start | bytes 524288 | tf_op jit(solution)/shard_map/all_to_all | solution.py:375
  13.8 2.1 %copy-start.3 = (s32[2,128]{1,0:T(2,128)}, s32[2,128]{1,0:T(2,128)S(1)}, u32[]{:S(2)}) copy-start(s32[2,128]{1,0:T(2,128)S(1)} %get-tuple-element.40.target_ref) | copy-start | bytes 3076
  13.9 19.0 %collective-permute-start = (bf16[2,88,1024]{2,1,0:T(8,128)(2,1)S(1)}, bf16[2,88,1024]{2,1,0:T(8,128)(2,1)S(1)}, u32[]{:S(2)}, u32[]{:S(2)}) collective-permute-start(bf16[2,88,1024]{2,1,0:T(8,128)(2,1)S(1)} %bitcast.19), channel_id=1, source_target_pairs={{0,2},{2,4},{4,6},{6,0},{1,3},{3,5},{5,7},{7,1},{8,10},{10,12},{12... | collective-permute-start | bytes 1081352 | tf_op jit(solution)/shard_map/ppermute | solution.py:374
  15.9 17.0 %collective-permute-start.1 = (bf16[2,88,1024]{2,1,0:T(8,128)(2,1)S(1)}, bf16[2,88,1024]{2,1,0:T(8,128)(2,1)S(1)}, u32[]{:S(2)}, u32[]{:S(2)}) collective-permute-start(bf16[2,88,1024]{2,1,0:T(8,128)(2,1)S(1)} %bitcast.20), channel_id=1, source_target_pairs={{0,4},{2,6},{4,0},{6,2},{1,5},{3,7},{5,1},{7,3},{8,12},{10,14},{12... | collective-permute-start | bytes 1081352 | tf_op jit(solution)/shard_map/ppermute | solution.py:374
  21.6 24.3 %all-to-all-start.1 = ((bf16[16,24,128]{2,1,0:T(8,128)(2,1)}), bf16[16,24,128]{2,1,0:T(8,128)(2,1)S(1)}, u32[]{:S(2)}, u32[]{:S(2)}) async-start(bf16[16,24,128]{2,1,0:T(8,128)(2,1)} %bitcast.7), calls=%async_computation.1 | async-start | bytes 196608 | tf_op jit(solution)/shard_map/all_to_all | solution.py:404
  32.6 0.6 copy-start.1
  33.2 17.8 %collective-permute-start.2 = (bf16[2,88,1024]{2,1,0:T(8,128)(2,1)S(1)}, bf16[2,88,1024]{2,1,0:T(8,128)(2,1)S(1)}, u32[]{:S(2)}, u32[]{:S(2)}) collective-permute-start(bf16[2,88,1024]{2,1,0:T(8,128)(2,1)S(1)} %bitcast.21), channel_id=1, source_target_pairs={{0,6},{2,0},{4,2},{6,4},{1,7},{3,1},{5,3},{7,5},{8,14},{10,8},{12,... | collective-permute-start | bytes 1081352 | tf_op jit(solution)/shard_map/ppermute | solution.py:414
  46.6 11.9 %all-to-all-start.2 = ((bf16[4,384,128]{2,1,0:T(8,128)(2,1)}), bf16[4,384,128]{2,1,0:T(8,128)(2,1)}, u32[]{:S(2)}, u32[]{:S(2)}) async-start(bf16[4,384,128]{2,1,0:T(8,128)(2,1)} %spread.1.spread_ref), calls=%async_computation.2 | async-start | bytes 786432 | tf_op jit(solution)/shard_map/all_to_all | solution.py:423
  51.2 9.9 %collective-permute-start.3 = (bf16[4,176,1024]{2,1,0:T(8,128)(2,1)S(1)}, bf16[4,176,1024]{2,1,0:T(8,128)(2,1)S(1)}, u32[]{:S(2)}, u32[]{:S(2)}) collective-permute-start(bf16[4,176,1024]{2,1,0:T(8,128)(2,1)S(1)} %stack.1.own_ref), channel_id=1, source_target_pairs={{0,1},{1,0},{2,3},{3,2},{4,5},{5,4},{6,7},{7,6},{8,9},{9,8},{10,11... | collective-permute-start | bytes 4325384 | tf_op jit(solution)/shard_map/ppermute | solution.py:433
  63.7 27.1 %copy-start.2 = (f32[16,1024]{1,0:T(8,128)S(1)}, f32[16,1024]{1,0:T(8,128)}, u32[]{:S(2)}) copy-start(f32[16,1024]{1,0:T(8,128)} %copy-done.1) | copy-start | bytes 196612
  63.7 27.1 %copy-start.4 = (s32[2,128]{1,0:T(2,128)S(1)}, s32[2,128]{1,0:T(2,128)}, u32[]{:S(2)}) copy-start(s32[2,128]{1,0:T(2,128)} %copy-done.3) | copy-start | bytes 3076

commit v6 on v5

--- a/solution.py
+++ b/solution.py
@@ -39,14 +39,14 @@
 
 def attention_kernel(
     index_ref, resid_hbm, gain_hbm, wq_hbm, wk_hbm, wv_hbm, wo_hbm, cache_hbm, lens_hbm, seg_hbm,
-    ffn_gain_hbm, router_hbm, out_ref, own_ref, ffn_gain_ref, router_ref,
+    ffn_gain_hbm, router_hbm, cols_hbm, out_ref, own_ref, ffn_gain_ref, router_ref, cols_ref,
     resid_ref, gain_ref, wq_ref, wk_ref, wv_ref, wo_ref, cache_ref, lens_ref, seg_ref, seg_row, sems
 ):
     sources = (
-        resid_hbm, gain_hbm, wq_hbm, wk_hbm, wv_hbm, seg_hbm, lens_hbm, cache_hbm, wo_hbm, ffn_gain_hbm, router_hbm
+        resid_hbm, gain_hbm, wq_hbm, wk_hbm, wv_hbm, seg_hbm, lens_hbm, cache_hbm, wo_hbm, ffn_gain_hbm, router_hbm, cols_hbm
     )
     targets = (
-        resid_ref, gain_ref, wq_ref, wk_ref, wv_ref, seg_ref, lens_ref, cache_ref, wo_ref, ffn_gain_ref, router_ref
+        resid_ref, gain_ref, wq_ref, wk_ref, wv_ref, seg_ref, lens_ref, cache_ref, wo_ref, ffn_gain_ref, router_ref, cols_ref
     )
     copies = [pltpu.make_async_copy(a, b, sems.at[i]) for i, (a, b) in enumerate(zip(sources, targets))]
     for copy in copies:
@@ -69,7 +69,6 @@
     values = dot(normed, wv_ref[...]).astype(BF)
     copies[5].wait()
     copies[6].wait()
-    copies[7].wait()
 
     seg_row[...] = iota((1, total), 1) + (1 << 20)
     seg_row[:, :packed] = seg_ref[...]
@@ -79,16 +78,18 @@
     slot_at = iota((decoded, decoded * slots), 1)
     own_cache = (slot_at // slots == iota((decoded, decoded * slots), 0)) & (slot_at % slots < lengths)
 
+    lane_head = iota((total, width), 1) // HDIM
+    queries = [jnp.where(lane_head == head, query, jnp.zeros_like(query)) for head in range(heads)]
+    packed_scores = [jnp.where(allowed, dot_nt(head_query, keys) * scale, -jnp.inf) for head_query in queries]
+    packed_highest = [jnp.max(scores, axis=-1, keepdims=True) for scores in packed_scores]
+    copies[7].wait()
     cached_keys = cache_ref[:, 0].reshape(decoded * slots, width)
     cached_values = cache_ref[:, 1].reshape(decoded * slots, width)
-    lane_head = iota((total, width), 1) // HDIM
     context = jnp.zeros((total, width), F32)
     for head in range(heads):
         mine = lane_head == head
-        head_query = jnp.where(mine, query, jnp.zeros_like(query))
-        scores = jnp.where(allowed, dot_nt(head_query, keys) * scale, -jnp.inf)
-        highest = jnp.max(scores, axis=-1, keepdims=True)
-        cached = jnp.where(own_cache, dot_nt(head_query[packed:], cached_keys) * scale, -jnp.inf)
+        scores, highest = packed_scores[head], packed_highest[head]
+        cached = jnp.where(own_cache, dot_nt(queries[head][packed:], cached_keys) * scale, -jnp.inf)
         top_dec = jnp.maximum(highest[packed:], jnp.max(cached, axis=-1, keepdims=True))
         highest = jnp.concatenate([highest[:packed], top_dec], axis=0)
         weights = jnp.exp(scores - highest)
@@ -108,6 +109,7 @@
     own_ref[...] = resid_ref[pl.ds(pl.multiple_of(index * block, block), block), :].astype(F32)
     copies[9].wait()
     copies[10].wait()
+    copies[11].wait()
 
 
 def own_routes(routes_ref, which, index, block):
@@ -169,15 +171,13 @@
     return own_ref[...] + mixed
 
 
-def mix_kernel(parts_ref, own_ref, gain_ref, ffn_in_ref):
+def dispatch_kernel(parts_ref, own_ref, gain_ref, chosen_ref, out_ref, ffn_in_ref):
     after = residual(parts_ref, own_ref)
     inverse = lax.rsqrt(jnp.mean(after * after, axis=-1, keepdims=True) + EPS)
-    ffn_in_ref[...] = (after * inverse * gain_ref[...]).astype(BF)
-
-
-def dispatch_kernel(ffn_in_ref, chosen_ref, out_ref):
-    chunks = ffn_in_ref.shape[1] // LANES
-    stacked = jnp.concatenate([ffn_in_ref[:, at * LANES : (at + 1) * LANES] for at in range(chunks)], axis=0)
+    ffn_in = (after * inverse * gain_ref[...]).astype(BF)
+    ffn_in_ref[...] = ffn_in
+    chunks = ffn_in.shape[1] // LANES
+    stacked = jnp.concatenate([ffn_in[:, at * LANES : (at + 1) * LANES] for at in range(chunks)], axis=0)
     out_ref[...] = dot(chosen_ref[...], stacked).astype(BF)
 
 
@@ -204,9 +204,12 @@
     order_ref[...] = jnp.where(wanted == iota((chunk_rows, chunk_rows), 1), 1.0, 0.0).astype(BF)
 
 
-def spread_kernel(tokens_ref, out_ref):
-    for at in range(out_ref.shape[0]):
-        out_ref[at] = tokens_ref[...]
+def spread_kernel(tokens_ref, out_hbm, sems):
+    copies = [pltpu.make_async_copy(tokens_ref, out_hbm.at[at], sems.at[at]) for at in range(out_hbm.shape[0])]
+    for copy in copies:
+        copy.start()
+    for copy in copies:
+        copy.wait()
 
 
 def stack_kernel(spread_ref, *refs):
@@ -341,17 +344,19 @@
         seg_ids,
         ffn_gain.reshape(1, width),
         router.T,
+        w_cols,
     )
-    partial_mix, own, gain, router_rows = pl.pallas_call(
+    partial_mix, own, gain, router_rows, w_cols = pl.pallas_call(
         attention_kernel,
         out_shape=(
             jax.ShapeDtypeStruct((group_rows, width), BF),
             jax.ShapeDtypeStruct((block, width), F32),
             jax.ShapeDtypeStruct((1, width), F32),
             jax.ShapeDtypeStruct((experts, width), BF),
+            jax.ShapeDtypeStruct(w_cols.shape, BF),
         ),
         in_specs=[SMEM] + [HBM] * len(operands),
-        out_specs=(VMEM,) * 4,
+        out_specs=(VMEM,) * 5,
         scratch_shapes=[pltpu.VMEM(each.shape, each.dtype) for each in operands[:9]]
         + [pltpu.VMEM((1, group_rows), jnp.int32), pltpu.SemaphoreType.DMA((len(operands),))],
         compiler_params=PARAMS,
@@ -373,24 +378,15 @@
     moves = [[(at, (at + shift) % row) for at in range(row)] for shift in range(row)]
     own_core = [w_cols] + [lax.ppermute(w_cols, "x", move) for move in moves[1:-1]]
     parts = lax.all_to_all(partial_mix.reshape(hid_count, block, width), hid, 0, 0, tiled=True)
-    ffn_in = pl.pallas_call(
-        mix_kernel,
-        out_shape=jax.ShapeDtypeStruct((block, width), BF),
-        in_specs=[VMEM] * 3,
-        out_specs=VMEM,
-        compiler_params=PARAMS,
-        cost_estimate=LONG,
-        name="mix",
-    )(parts, own, gain)
-    outgoing = pl.pallas_call(
+    outgoing, ffn_in = pl.pallas_call(
         dispatch_kernel,
-        out_shape=jax.ShapeDtypeStruct((slot_count, LANES), BF),
-        in_specs=[VMEM] * 2,
-        out_specs=VMEM,
-        compiler_params=PARAMS,
-        cost_estimate=LONG,
+        out_shape=(jax.ShapeDtypeStruct((slot_count, LANES), BF), jax.ShapeDtypeStruct((block, width), BF)),
+        in_specs=[VMEM] * 4,
+        out_specs=(VMEM,) * 2,
+        compiler_params=PARAMS,
+        cost_estimate=VERY_LONG,
         name="dispatch",
-    )(ffn_in, chosen)
+    )(parts, own, gain, chosen)
     gates, after = pl.pallas_call(
         gates_kernel,
         out_shape=(jax.ShapeDtypeStruct((2, block, LANES), F32), jax.ShapeDtypeStruct((block, width), F32)),
@@ -414,9 +410,10 @@
     own_core.append(lax.ppermute(own_core[0], "x", moves[-1]))
     spread = pl.pallas_call(
         spread_kernel,
-        out_shape=jax.ShapeDtypeStruct((split, slot_count, LANES), BF),
+        out_shape=pltpu.HBM((split, slot_count, LANES), BF),
         in_specs=[VMEM],
-        out_specs=VMEM,
+        out_specs=HBM,
+        scratch_shapes=[pltpu.SemaphoreType.DMA((split,))],
         compiler_params=PARAMS,
         name="spread",
     )(arrived.reshape(slot_count, LANES))
@@ -425,11 +422,11 @@
     stacked = pl.pallas_call(
         stack_kernel,
         out_shape=jax.ShapeDtypeStruct((row,) + own_core[0].shape, BF),
-        in_specs=[pl.BlockSpec(memory_space=pl.ANY)] + [VMEM] * row,
+        in_specs=[HBM] + [VMEM] * row,
         out_specs=VMEM,
         compiler_params=PARAMS,
         name="stack",
-    )(spread, *own_core)
+    )(in_hbm(spread), *own_core)
     other_core = lax.ppermute(stacked, "c", [(0, 1), (1, 0)])
     rows, own_hidden, down = pl.pallas_call(
         own_kernel,
@@ -440,7 +437,7 @@
         ),
         in_specs=[HBM, VMEM, VMEM, HBM],
         out_specs=(VMEM,) * 3,
-        scratch_shapes=[pltpu.VMEM(spread.shape, BF), pltpu.SemaphoreType.DMA((split,)), pltpu.SemaphoreType.DMA],
+        scratch_shapes=[pltpu.VMEM((split, slot_count, LANES), BF), pltpu.SemaphoreType.DMA((split,)), pltpu.SemaphoreType.DMA],
         compiler_params=PARAMS,
         cost_estimate=VERY_LONG,
         name="own",

time: 92.5 us -> 92.4 us (level)
  no operation moved by 1% of the time
where the time goes in v6:
time: 92.4 us; the launch traced here: 91.6 us
  starting transfers between devices  36.9 us (40%)
  blocking collectives  26.6 us (29%)
  waiting for transfers between devices  14.6 us (16%)
  Pallas kernels  13.3 us (14%)
    all_to_all x1, blocking collectives, body(): returned = lax.all_to_all(summed.reshape(exchanged), 'z', 0, 0, tiled=True)  16.9 us
    all_to_all x1, starting transfers between devices, body(): arrived = lax.all_to_all(outgoing.reshape(exchanged), 'z', 0, 0, tiled=True)  10.8 us
    all_to_all x1, blocking collectives, body(): quarters = lax.all_to_all(projected, 'y', 0, 0, tiled=True)  9.77 us
    all_to_all x1, starting transfers between devices, body(): lax.all_to_all(partial_mix.reshape(hid_count, block, width), hid, 0, 0, t...  9.21 us
    all_to_all x1, waiting for transfers between devices, body(): arrived = lax.all_to_all(outgoing.reshape(exchanged), 'z', 0, 0, tiled=True)  9.13 us
    ppermute x2, starting transfers between devices, body(): lax.ppermute(w_cols, 'x', move)  6.73 us
    all_to_all x1, waiting for transfers between devices, body(): tokens = lax.all_to_all(spread, 'y', 0, 0, tiled=True)  5.46 us
    all_to_all x1, starting transfers between devices, body(): tokens = lax.all_to_all(spread, 'y', 0, 0, tiled=True)  4.47 us
  transfers between devices with their start and end apart: 7, of which 2 were waited for; matrix products, arithmetic and copies ran while one was open for 0% of the time, Pallas kernels for 6%

profile of v6, /device:TPU:6, one launch (start us, length us, event | category | flops | bytes accessed | tf_op | source)
XLA Modules:
  0.0 91.6 jit_solution(9492594265579017157)
XLA Ops:
  0.0 0.0 copy-start
  0.0 4.1 %attention.1 = (bf16[128,1024]{1,0:T(8,128)(2,1)}, f32[16,1024]{1,0:T(8,128)S(1)}, f32[1,1024]{1,0:T(1,128)S(1)}, bf16[16,1024]{1,0:T(8,128)(2,1)S(1)}, bf16[2,88,1024]{2,1,0:T(8,128)(2,1)S(1)}) custom-call(s32[1]{0:T(128)} %bitcast.index_ref, bf16[128,1024]{1,0:T(8,128)(2,1)} %resid_hbm.1, f32[1,1024]{1,0:T(1,128)} %bitcast.26, bf16[1024,128]{1,0:T(8,128)(2,1)} %wq_hbm.1, ...), custom_call_target="tpu_custom_call" | custom-call | tf_op jit(solution)/shard_map/attention/pallas_call | solution.py:349
  4.1 9.2 %all-to-all-start = ((bf16[8,16,1024]{2,1,0:T(8,128)(2,1)}), bf16[8,16,1024]{2,1,0:T(8,128)(2,1)S(1)}, u32[]{:S(2)}, u32[]{:S(2)}) async-start(bf16[8,16,1024]{2,1,0:T(8,128)(2,1)} %bitcast.6), calls=%async_computation | async-start | bytes 524288 | tf_op jit(solution)/shard_map/all_to_all | solution.py:380
  13.4 0.0 copy-done
  13.4 0.6 routing.1
  14.0 2.0 %collective-permute-start = (bf16[2,88,1024]{2,1,0:T(8,128)(2,1)S(1)}, bf16[2,88,1024]{2,1,0:T(8,128)(2,1)S(1)}, u32[]{:S(2)}, u32[]{:S(2)}) collective-permute-start(bf16[2,88,1024]{2,1,0:T(8,128)(2,1)S(1)} %get-tuple-element.39), channel_id=1, source_target_pairs={{0,2},{2,4},{4,6},{6,0},{1,3},{3,5},{5,7},{7,1},{8,10},{10,12},{12... | collective-permute-start | bytes 1081352 | tf_op jit(solution)/shard_map/ppermute | solution.py:379
  16.0 4.7 %collective-permute-start.1 = (bf16[2,88,1024]{2,1,0:T(8,128)(2,1)S(1)}, bf16[2,88,1024]{2,1,0:T(8,128)(2,1)S(1)}, u32[]{:S(2)}, u32[]{:S(2)}) collective-permute-start(bf16[2,88,1024]{2,1,0:T(8,128)(2,1)S(1)} %get-tuple-element.39), channel_id=1, source_target_pairs={{0,4},{2,6},{4,0},{6,2},{1,5},{3,7},{5,1},{7,3},{8,12},{10,14},{12... | collective-permute-start | bytes 1081352 | tf_op jit(solution)/shard_map/ppermute | solution.py:379
  20.7 0.0 all-to-all-done.parts_ref
  20.7 0.9 %dispatch.1 = (bf16[384,128]{1,0:T(8,128)(2,1)}, bf16[16,1024]{1,0:T(8,128)(2,1)S(1)}) custom-call(bf16[8,16,1024]{2,1,0:T(8,128)(2,1)S(1)} %all-to-all-done.parts_ref, f32[16,1024]{1,0:T(8,128)S(1)} %get-tuple-element.27.own_ref, f32[1,1024]{1,0:T(1,128)S(1)} %get-tuple-element.28.gain_ref, bf16[384,128]{1,0:T(8,128)(2,1)S(1)} %get-tuple-element.29.chosen_ref), custom_call_target="tpu_custom_call" | custom-call | flops 20000000000 | bytes 2097152 | tf_op jit(solution)/shard_map/dispatch/pallas_call | solution.py:381
  21.7 10.8 %all-to-all-start.1 = ((bf16[16,24,128]{2,1,0:T(8,128)(2,1)}), bf16[16,24,128]{2,1,0:T(8,128)(2,1)S(1)}, u32[]{:S(2)}, u32[]{:S(2)}) async-start(bf16[16,24,128]{2,1,0:T(8,128)(2,1)} %bitcast.8), calls=%async_computation.1 | async-start | bytes 196608 | tf_op jit(solution)/shard_map/all_to_all | solution.py:400
  32.5 0.2 gates.1
  32.7 0.3 order.1.order_ref
  33.0 0.0 collective-permute-done
  33.0 0.0 collective-permute-done.1
  33.0 3.8 %collective-permute-start.2 = (bf16[2,88,1024]{2,1,0:T(8,128)(2,1)S(1)}, bf16[2,88,1024]{2,1,0:T(8,128)(2,1)S(1)}, u32[]{:S(2)}, u32[]{:S(2)}) collective-permute-start(bf16[2,88,1024]{2,1,0:T(8,128)(2,1)S(1)} %get-tuple-element.39), channel_id=1, source_target_pairs={{0,6},{2,0},{4,2},{6,4},{1,7},{3,1},{5,3},{7,5},{8,14},{10,8},{12,... | collective-permute-start | bytes 1081352 | tf_op jit(solution)/shard_map/ppermute | solution.py:410
  36.8 9.1 %all-to-all-done.1 = bf16[16,24,128]{2,1,0:T(8,128)(2,1)S(1)} async-done(((bf16[16,24,128]{2,1,0:T(8,128)(2,1)}), bf16[16,24,128]{2,1,0:T(8,128)(2,1)S(1)}, u32[]{:S(2)}, u32[]{:S(2)}) %all-to-all-start.1) | async-done | bytes 98336 | tf_op jit(solution)/shard_map/all_to_all | solution.py:400
  46.0 0.8 spread.1.spread_ref
  46.8 4.5 %all-to-all-start.2 = ((bf16[4,384,128]{2,1,0:T(8,128)(2,1)}), bf16[4,384,128]{2,1,0:T(8,128)(2,1)}, u32[]{:S(2)}, u32[]{:S(2)}) async-start(bf16[4,384,128]{2,1,0:T(8,128)(2,1)} %spread.1.spread_ref), calls=%async_computation.2 | async-start | bytes 786432 | tf_op jit(solution)/shard_map/all_to_all | solution.py:420
  51.2 0.0 collective-permute-done.2
  51.2 0.1 stack.1.own_ref
  51.3 1.9 %collective-permute-start.3 = (bf16[4,176,1024]{2,1,0:T(8,128)(2,1)S(1)}, bf16[4,176,1024]{2,1,0:T(8,128)(2,1)S(1)}, u32[]{:S(2)}, u32[]{:S(2)}) collective-permute-start(bf16[4,176,1024]{2,1,0:T(8,128)(2,1)S(1)} %stack.1.own_ref), channel_id=1, source_target_pairs={{0,1},{1,0},{2,3},{3,2},{4,5},{5,4},{6,7},{7,6},{8,9},{9,8},{10,11... | collective-permute-start | bytes 4325384 | tf_op jit(solution)/shard_map/ppermute | solution.py:430
  53.3 5.5 %all-to-all-done.2.tokens_hbm = bf16[4,384,128]{2,1,0:T(8,128)(2,1)} async-done(((bf16[4,384,128]{2,1,0:T(8,128)(2,1)}), bf16[4,384,128]{2,1,0:T(8,128)(2,1)}, u32[]{:S(2)}, u32[]{:S(2)}) %all-to-all-start.2) | async-done | bytes 393248 | tf_op jit(solution)/shard_map/all_to_all | solution.py:420
  58.7 2.5 %own.1 = (bf16[192,1024]{1,0:T(8,128)(2,1)S(1)}, bf16[4,192,88]{2,1,0:T(8,128)(2,1)S(1)}, bf16[704,1024]{1,0:T(8,128)(2,1)S(1)}) custom-call(bf16[4,384,128]{2,1,0:T(8,128)(2,1)} %all-to-all-done.2.tokens_hbm, bf16[384,384]{1,0:T(8,128)(2,1)S(1)} %order.1.order_ref, bf16[4,176,1024]{2,1,0:T(8,128)(2,1)S(1)} %stack.1.own_ref, bf16[704,1024]{1,0:T(8,128)(2,1)} %down_hbm.1), custom_call_target="tpu_custom_call" | custom-call | flops 20000000000 | bytes 2097152 | tf_op jit(solution)/shard_map/own/pallas_call | solution.py:431
  61.2 0.0 collective-permute-done.3.other_ref
  61.3 2.6 %ffn.1 = bf16[4,384,128]{2,1,0:T(8,128)(2,1)S(1)} custom-call(s32[1]{0:T(128)} %bitcast.index_ref, bf16[192,1024]{1,0:T(8,128)(2,1)S(1)} %get-tuple-element.42.rows_ref, bf16[384,384]{1,0:T(8,128)(2,1)S(1)} %order.1.order_ref, bf16[704,1024]{1,0:T(8,128)(2,1)S(1)} %get-tuple-element.43.down_ref, bf16[4,192,88]{2,1,0:T(8,128)(2,1)S(1)} %get-tuple-element.44.own_hidden_ref, ...), custom_call_target="tpu_custom_call" | custom-call | tf_op jit(solution)/shard_map/ffn/pallas_call | solution.py:445
  63.8 9.8 %all_to_all.25.parts_ref = bf16[4,384,128]{2,1,0:T(8,128)(2,1)S(1)} all-to-all(bf16[4,384,128]{2,1,0:T(8,128)(2,1)S(1)} %ffn.1), channel_id=1, replica_groups=mesh['z'=16,'y'=4,'x'=4,'c'=2] {'y'}, dimensions={0} | all-to-all | bytes 786432 | tf_op jit(solution)/shard_map/all_to_all | solution.py:456
  73.6 0.1 sum_quarters.1
  73.7 16.9 %all_to_all.26 = bf16[16,24,128]{2,1,0:T(8,128)(2,1)S(1)} all-to-all(bf16[16,24,128]{2,1,0:T(8,128)(2,1)S(1)} %bitcast.18), channel_id=1, replica_groups=mesh['z'=16,'y'=4,'x'=4,'c'=2] {'z'}, dimensions={0} | all-to-all | bytes 196608 | tf_op jit(solution)/shard_map/all_to_all | solution.py:465
  90.5 1.1 %combine.1 = bf16[16,1024]{1,0:T(8,128)(2,1)} custom-call(bf16[384,128]{1,0:T(8,128)(2,1)S(1)} %bitcast.16, f32[16,1024]{1,0:T(8,128)S(1)} %get-tuple-element.45.after_ref, f32[2,16,128]{2,1,0:T(8,128)S(1)} %get-tuple-element.36.tokens_ref.gates_ref, s32[2,128]{1,0:T(2,128)S(1)} %get-tuple-element.46.target_ref), custom_call_target="tpu_custom_call" | custom-call | tf_op jit(solution)/shard_map/combine/pallas_call | solution.py:466
Async XLA Ops:
  0.0 13.4 %copy-start = (s32[128,2]{0,1:T(2,128)S(1)}, s32[128,2]{0,1:T(2,128)}, u32[]{:S(2)}) copy-start(s32[128,2]{0,1:T(2,128)} %param.25) | copy-start | bytes 3076
  4.1 16.6 %all-to-all-start = ((bf16[8,16,1024]{2,1,0:T(8,128)(2,1)}), bf16[8,16,1024]{2,1,0:T(8,128)(2,1)S(1)}, u32[]{:S(2)}, u32[]{:S(2)}) async-start(bf16[8,16,1024]{2,1,0:T(8,128)(2,1)} %bitcast.6), calls=%async_computation | async-start | bytes 524288 | tf_op jit(solution)/shard_map/all_to_all | solution.py:380
  14.0 19.0 %collective-permute-start = (bf16[2,88,1024]{2,1,0:T(8,128)(2,1)S(1)}, bf16[2,88,1024]{2,1,0:T(8,128)(2,1)S(1)}, u32[]{:S(2)}, u32[]{:S(2)}) collective-permute-start(bf16[2,88,1024]{2,1,0:T(8,128)(2,1)S(1)} %get-tuple-element.39), channel_id=1, source_target_pairs={{0,2},{2,4},{4,6},{6,0},{1,3},{3,5},{5,7},{7,1},{8,10},{10,12},{12... | collective-permute-start | bytes 1081352 | tf_op jit(solution)/shard_map/ppermute | solution.py:379
  16.0 17.0 %collective-permute-start.1 = (bf16[2,88,1024]{2,1,0:T(8,128)(2,1)S(1)}, bf16[2,88,1024]{2,1,0:T(8,128)(2,1)S(1)}, u32[]{:S(2)}, u32[]{:S(2)}) collective-permute-start(bf16[2,88,1024]{2,1,0:T(8,128)(2,1)S(1)} %get-tuple-element.39), channel_id=1, source_target_pairs={{0,4},{2,6},{4,0},{6,2},{1,5},{3,7},{5,1},{7,3},{8,12},{10,14},{12... | collective-permute-start | bytes 1081352 | tf_op jit(solution)/shard_map/ppermute | solution.py:379
  21.7 24.3 %all-to-all-start.1 = ((bf16[16,24,128]{2,1,0:T(8,128)(2,1)}), bf16[16,24,128]{2,1,0:T(8,128)(2,1)S(1)}, u32[]{:S(2)}, u32[]{:S(2)}) async-start(bf16[16,24,128]{2,1,0:T(8,128)(2,1)} %bitcast.8), calls=%async_computation.1 | async-start | bytes 196608 | tf_op jit(solution)/shard_map/all_to_all | solution.py:400
  33.0 18.2 %collective-permute-start.2 = (bf16[2,88,1024]{2,1,0:T(8,128)(2,1)S(1)}, bf16[2,88,1024]{2,1,0:T(8,128)(2,1)S(1)}, u32[]{:S(2)}, u32[]{:S(2)}) collective-permute-start(bf16[2,88,1024]{2,1,0:T(8,128)(2,1)S(1)} %get-tuple-element.39), channel_id=1, source_target_pairs={{0,6},{2,0},{4,2},{6,4},{1,7},{3,1},{5,3},{7,5},{8,14},{10,8},{12,... | collective-permute-start | bytes 1081352 | tf_op jit(solution)/shard_map/ppermute | solution.py:410
  46.8 12.0 %all-to-all-start.2 = ((bf16[4,384,128]{2,1,0:T(8,128)(2,1)}), bf16[4,384,128]{2,1,0:T(8,128)(2,1)}, u32[]{:S(2)}, u32[]{:S(2)}) async-start(bf16[4,384,128]{2,1,0:T(8,128)(2,1)} %spread.1.spread_ref), calls=%async_computation.2 | async-start | bytes 786432 | tf_op jit(solution)/shard_map/all_to_all | solution.py:420
  51.3 9.9 %collective-permute-start.3 = (bf16[4,176,1024]{2,1,0:T(8,128)(2,1)S(1)}, bf16[4,176,1024]{2,1,0:T(8,128)(2,1)S(1)}, u32[]{:S(2)}, u32[]{:S(2)}) collective-permute-start(bf16[4,176,1024]{2,1,0:T(8,128)(2,1)S(1)} %stack.1.own_ref), channel_id=1, source_target_pairs={{0,1},{1,0},{2,3},{3,2},{4,5},{5,4},{6,7},{7,6},{8,9},{9,8},{10,11... | collective-permute-start | bytes 4325384 | tf_op jit(solution)/shard_map/ppermute | solution.py:430

commit v7 on v5

--- a/solution.py
+++ b/solution.py
@@ -30,6 +30,16 @@
 
 def iota(shape, dim):
     return lax.broadcasted_iota(jnp.int32, shape, dim)
+
+
+def quotient(number, by):
+    shift = (by & -by).bit_length() - 1
+    odd = by >> shift
+    if odd == 1:
+        return number >> shift
+    if odd == 3:
+        return ((number >> shift) * 21846) >> 16
+    return number // by
 
 
 def to_column(row, size):
@@ -56,6 +66,13 @@
     decoded, _, slots, width = cache_ref.shape
     heads = width // HDIM
     scale = HDIM ** (-0.5)
+    causal = iota((total, total), 1) <= iota((total, total), 0)
+    seg_row[...] = iota((1, total), 1) + (1 << 20)
+    slot_at = iota((decoded, decoded * slots), 1)
+    request = quotient(slot_at, slots)
+    own_request = request == iota((decoded, decoded * slots), 0)
+    slot_at = slot_at - request * slots
+    lane_head = quotient(iota((total, width), 1), HDIM)
     copies[0].wait()
     copies[1].wait()
     x = resid_ref[...].astype(F32)
@@ -71,17 +88,14 @@
     copies[6].wait()
     copies[7].wait()
 
-    seg_row[...] = iota((1, total), 1) + (1 << 20)
     seg_row[:, :packed] = seg_ref[...]
     segments = seg_row[...]
-    allowed = (iota((total, total), 1) <= iota((total, total), 0)) & (to_column(segments, total) == segments)
+    allowed = causal & (to_column(segments, total) == segments)
     lengths = to_column(lens_ref[...], decoded)
-    slot_at = iota((decoded, decoded * slots), 1)
-    own_cache = (slot_at // slots == iota((decoded, decoded * slots), 0)) & (slot_at % slots < lengths)
+    own_cache = own_request & (slot_at < lengths)
 
     cached_keys = cache_ref[:, 0].reshape(decoded * slots, width)
     cached_values = cache_ref[:, 1].reshape(decoded * slots, width)
-    lane_head = iota((total, width), 1) // HDIM
     context = jnp.zeros((total, width), F32)
     for head in range(heads):
         mine = lane_head == head
@@ -121,7 +135,8 @@
 
 
 def placement(row, columns, block, capacity):
-    token = iota((block, LANES), 1) % block
+    token = iota((block, LANES), 1)
+    token = token - quotient(token, block) * block
     before = iota((block, LANES), 0) < token
     slot = jnp.zeros((1, LANES), jnp.int32)
     for column in columns:
@@ -131,9 +146,9 @@
 
 def slot_rows(rows, capacity, chunks):
     at = iota((rows, LANES), 0)
-    expert = at // (chunks * capacity)
+    expert = quotient(at, chunks * capacity)
     rest = at - expert * (chunks * capacity)
-    chunk = rest // capacity
+    chunk = quotient(rest, capacity)
     return expert * capacity + rest - chunk * capacity, chunk
 
 
@@ -151,7 +166,7 @@
     rows = [own_routes(routes_ref, which, index_ref[0], block) for which in range(2)]
     columns = route_columns(rows, block)
     wanted, chunk = slot_rows(chosen_ref.shape[0], CAPACITY, chunks)
-    same = chunk == iota(chunk.shape, 1) // block
+    same = chunk == quotient(iota(chunk.shape, 1), block)
     both = None
     for which in range(2):
         target = placement(rows[which], columns, block, CAPACITY)
@@ -197,9 +212,9 @@
     chunk_rows = order_ref.shape[0]
     each = chunk_rows // chunks
     at = iota((chunk_rows, chunk_rows), 0)
-    chunk = at // each
+    chunk = quotient(at, each)
     rest = at - chunk * each
-    source = rest // CAPACITY
+    source = quotient(rest, CAPACITY)
     wanted = source * (chunks * CAPACITY) + chunk * CAPACITY + rest - source * CAPACITY
     order_ref[...] = jnp.where(wanted == iota((chunk_rows, chunk_rows), 1), 1.0, 0.0).astype(BF)
 
@@ -287,7 +302,7 @@
     block, width = after_ref.shape
     chunks = width // LANES
     wanted, chunk = slot_rows(experts_ref.shape[0], CAPACITY, chunks)
-    same = chunk == iota(chunk.shape, 1) // block
+    same = chunk == quotient(iota(chunk.shape, 1), block)
     picked = []
     for which in range(2):
         chosen = same & (wanted == target_ref[pl.ds(which, 1), :])

time: 92.5 us -> 92.2 us (level)
  no operation moved by 1% of the time
where the time goes in v7:
time: 92.2 us; the launch traced here: 91.5 us
  starting transfers between devices  36.6 us (40%)
  blocking collectives  26.9 us (29%)
  waiting for transfers between devices  14.6 us (16%)
  Pallas kernels  12.8 us (14%)
    all_to_all x1, blocking collectives, body(): returned = lax.all_to_all(summed.reshape(exchanged), 'z', 0, 0, tiled=True)  17 us
    all_to_all x1, starting transfers between devices, body(): arrived = lax.all_to_all(outgoing.reshape(exchanged), 'z', 0, 0, tiled=True)  10.8 us
    all_to_all x1, blocking collectives, body(): quarters = lax.all_to_all(projected, 'y', 0, 0, tiled=True)  9.91 us
    all_to_all x1, starting transfers between devices, body(): lax.all_to_all(partial_mix.reshape(hid_count, block, width), hid, 0, 0, t...  9.21 us
    all_to_all x1, waiting for transfers between devices, body(): arrived = lax.all_to_all(outgoing.reshape(exchanged), 'z', 0, 0, tiled=True)  9.14 us
    ppermute x2, starting transfers between devices, body(): lax.ppermute(w_cols, 'x', move)  6.73 us
    all_to_all x1, waiting for transfers between devices, body(): tokens = lax.all_to_all(spread, 'y', 0, 0, tiled=True)  5.46 us
    all_to_all x1, starting transfers between devices, body(): tokens = lax.all_to_all(spread, 'y', 0, 0, tiled=True)  4.47 us
  transfers between devices with their start and end apart: 7, of which 2 were waited for; matrix products, arithmetic and copies ran while one was open for 0% of the time, Pallas kernels for 6%

profile of v7, /device:TPU:6, one launch (start us, length us, event | category | flops | bytes accessed | tf_op | source)
XLA Modules:
  0.0 91.5 jit_solution(15485701278292482592)
XLA Ops:
  0.0 0.0 copy-start.5
  0.0 0.0 copy-start
  0.0 4.0 %attention.1 = (bf16[128,1024]{1,0:T(8,128)(2,1)}, f32[16,1024]{1,0:T(8,128)S(1)}, f32[1,1024]{1,0:T(1,128)S(1)}, bf16[16,1024]{1,0:T(8,128)(2,1)S(1)}) custom-call(s32[1]{0:T(128)} %bitcast.index_ref, bf16[128,1024]{1,0:T(8,128)(2,1)} %resid_hbm.1, f32[1,1024]{1,0:T(1,128)} %bitcast.28, bf16[1024,128]{1,0:T(8,128)(2,1)} %wq_hbm.1, ...), custom_call_target="tpu_custom_call" | custom-call | tf_op jit(solution)/shard_map/attention/pallas_call | solution.py:360
  4.0 9.2 %all-to-all-start = ((bf16[8,16,1024]{2,1,0:T(8,128)(2,1)}), bf16[8,16,1024]{2,1,0:T(8,128)(2,1)S(1)}, u32[]{:S(2)}, u32[]{:S(2)}) async-start(bf16[8,16,1024]{2,1,0:T(8,128)(2,1)} %bitcast.5), calls=%async_computation | async-start | bytes 524288 | tf_op jit(solution)/shard_map/all_to_all | solution.py:390
  13.2 0.0 copy-done.5
  13.2 0.5 routing.1
  13.7 0.0 copy-start.3
  13.7 0.0 copy-done
  13.7 2.0 %collective-permute-start = (bf16[2,88,1024]{2,1,0:T(8,128)(2,1)S(1)}, bf16[2,88,1024]{2,1,0:T(8,128)(2,1)S(1)}, u32[]{:S(2)}, u32[]{:S(2)}) collective-permute-start(bf16[2,88,1024]{2,1,0:T(8,128)(2,1)S(1)} %bitcast.19), channel_id=1, source_target_pairs={{0,2},{2,4},{4,6},{6,0},{1,3},{3,5},{5,7},{7,1},{8,10},{10,12},{12... | collective-permute-start | bytes 1081352 | tf_op jit(solution)/shard_map/ppermute | solution.py:389
  15.7 0.0 copy-done.3
  15.7 4.7 %collective-permute-start.1 = (bf16[2,88,1024]{2,1,0:T(8,128)(2,1)S(1)}, bf16[2,88,1024]{2,1,0:T(8,128)(2,1)S(1)}, u32[]{:S(2)}, u32[]{:S(2)}) collective-permute-start(bf16[2,88,1024]{2,1,0:T(8,128)(2,1)S(1)} %bitcast.20), channel_id=1, source_target_pairs={{0,4},{2,6},{4,0},{6,2},{1,5},{3,7},{5,1},{7,3},{8,12},{10,14},{12... | collective-permute-start | bytes 1081352 | tf_op jit(solution)/shard_map/ppermute | solution.py:389
  20.5 0.0 all-to-all-done.parts_ref
  20.5 0.1 mix.1.ffn_in_ref
  20.6 0.8 dispatch.1
  21.4 10.8 %all-to-all-start.1 = ((bf16[16,24,128]{2,1,0:T(8,128)(2,1)}), bf16[16,24,128]{2,1,0:T(8,128)(2,1)S(1)}, u32[]{:S(2)}, u32[]{:S(2)}) async-start(bf16[16,24,128]{2,1,0:T(8,128)(2,1)} %bitcast.7), calls=%async_computation.1 | async-start | bytes 196608 | tf_op jit(solution)/shard_map/all_to_all | solution.py:419
  32.2 0.2 gates.1
  32.4 0.0 copy-start.1
  32.4 0.1 order.1.order_ref
  32.6 0.0 collective-permute-done
  32.6 0.0 collective-permute-done.1
  32.6 0.4 copy-done.1
  33.1 3.5 %collective-permute-start.2 = (bf16[2,88,1024]{2,1,0:T(8,128)(2,1)S(1)}, bf16[2,88,1024]{2,1,0:T(8,128)(2,1)S(1)}, u32[]{:S(2)}, u32[]{:S(2)}) collective-permute-start(bf16[2,88,1024]{2,1,0:T(8,128)(2,1)S(1)} %bitcast.21), channel_id=1, source_target_pairs={{0,6},{2,0},{4,2},{6,4},{1,7},{3,1},{5,3},{7,5},{8,14},{10,8},{12,... | collective-permute-start | bytes 1081352 | tf_op jit(solution)/shard_map/ppermute | solution.py:429
  36.5 9.1 %all-to-all-done.1 = bf16[16,24,128]{2,1,0:T(8,128)(2,1)S(1)} async-done(((bf16[16,24,128]{2,1,0:T(8,128)(2,1)}), bf16[16,24,128]{2,1,0:T(8,128)(2,1)S(1)}, u32[]{:S(2)}, u32[]{:S(2)}) %all-to-all-start.1) | async-done | bytes 98336 | tf_op jit(solution)/shard_map/all_to_all | solution.py:419
  45.7 0.8 spread.1.spread_ref
  46.5 4.5 %all-to-all-start.2 = ((bf16[4,384,128]{2,1,0:T(8,128)(2,1)}), bf16[4,384,128]{2,1,0:T(8,128)(2,1)}, u32[]{:S(2)}, u32[]{:S(2)}) async-start(bf16[4,384,128]{2,1,0:T(8,128)(2,1)} %spread.1.spread_ref), calls=%async_computation.2 | async-start | bytes 786432 | tf_op jit(solution)/shard_map/all_to_all | solution.py:438
  50.9 0.0 collective-permute-done.2
  50.9 0.1 stack.1.own_ref
  51.0 1.9 %collective-permute-start.3 = (bf16[4,176,1024]{2,1,0:T(8,128)(2,1)S(1)}, bf16[4,176,1024]{2,1,0:T(8,128)(2,1)S(1)}, u32[]{:S(2)}, u32[]{:S(2)}) collective-permute-start(bf16[4,176,1024]{2,1,0:T(8,128)(2,1)S(1)} %stack.1.own_ref), channel_id=1, source_target_pairs={{0,1},{1,0},{2,3},{3,2},{4,5},{5,4},{6,7},{7,6},{8,9},{9,8},{10,11... | collective-permute-start | bytes 4325384 | tf_op jit(solution)/shard_map/ppermute | solution.py:448
  53.0 5.5 %all-to-all-done.2.tokens_hbm = bf16[4,384,128]{2,1,0:T(8,128)(2,1)} async-done(((bf16[4,384,128]{2,1,0:T(8,128)(2,1)}), bf16[4,384,128]{2,1,0:T(8,128)(2,1)}, u32[]{:S(2)}, u32[]{:S(2)}) %all-to-all-start.2) | async-done | bytes 393248 | tf_op jit(solution)/shard_map/all_to_all | solution.py:438
  58.4 2.5 %own.1 = (bf16[192,1024]{1,0:T(8,128)(2,1)S(1)}, bf16[4,192,88]{2,1,0:T(8,128)(2,1)S(1)}, bf16[704,1024]{1,0:T(8,128)(2,1)S(1)}) custom-call(bf16[4,384,128]{2,1,0:T(8,128)(2,1)} %all-to-all-done.2.tokens_hbm, bf16[384,384]{1,0:T(8,128)(2,1)S(1)} %order.1.order_ref, bf16[4,176,1024]{2,1,0:T(8,128)(2,1)S(1)} %stack.1.own_ref, bf16[704,1024]{1,0:T(8,128)(2,1)} %down_hbm.1), custom_call_target="tpu_custom_call" | custom-call | flops 20000000000 | bytes 2097152 | tf_op jit(solution)/shard_map/own/pallas_call | solution.py:449
  61.0 0.0 collective-permute-done.3.other_ref
  61.0 2.6 %ffn.1 = bf16[4,384,128]{2,1,0:T(8,128)(2,1)S(1)} custom-call(s32[1]{0:T(128)} %bitcast.index_ref, bf16[192,1024]{1,0:T(8,128)(2,1)S(1)} %get-tuple-element.36.rows_ref, bf16[384,384]{1,0:T(8,128)(2,1)S(1)} %order.1.order_ref, bf16[704,1024]{1,0:T(8,128)(2,1)S(1)} %get-tuple-element.37.down_ref, bf16[4,192,88]{2,1,0:T(8,128)(2,1)S(1)} %get-tuple-element.38.own_hidden_ref, ...), custom_call_target="tpu_custom_call" | custom-call | tf_op jit(solution)/shard_map/ffn/pallas_call | solution.py:463
  63.5 0.0 copy-start.2
  63.6 0.0 copy-start.4
  63.6 9.9 %all_to_all.25.parts_ref = bf16[4,384,128]{2,1,0:T(8,128)(2,1)S(1)} all-to-all(bf16[4,384,128]{2,1,0:T(8,128)(2,1)S(1)} %ffn.1), channel_id=1, replica_groups=mesh['z'=16,'y'=4,'x'=4,'c'=2] {'y'}, dimensions={0} | all-to-all | bytes 786432 | tf_op jit(solution)/shard_map/all_to_all | solution.py:474
  73.5 0.1 sum_quarters.1
  73.5 17.0 %all_to_all.26 = bf16[16,24,128]{2,1,0:T(8,128)(2,1)S(1)} all-to-all(bf16[16,24,128]{2,1,0:T(8,128)(2,1)S(1)} %bitcast.18), channel_id=1, replica_groups=mesh['z'=16,'y'=4,'x'=4,'c'=2] {'z'}, dimensions={0} | all-to-all | bytes 196608 | tf_op jit(solution)/shard_map/all_to_all | solution.py:483
  90.6 0.0 copy-done.2
  90.6 0.0 copy-done.4
  90.6 1.0 %combine.1 = bf16[16,1024]{1,0:T(8,128)(2,1)} custom-call(bf16[384,128]{1,0:T(8,128)(2,1)S(1)} %bitcast.16, f32[16,1024]{1,0:T(8,128)S(1)} %copy-done.2, f32[2,16,128]{2,1,0:T(8,128)S(1)} %get-tuple-element.30.tokens_ref.gates_ref, s32[2,128]{1,0:T(2,128)S(1)} %copy-done.4), custom_call_target="tpu_custom_call" | custom-call | tf_op jit(solution)/shard_map/combine/pallas_call | solution.py:484
Async XLA Ops:
  0.0 13.2 %copy-start.5 = (s32[128,2]{0,1:T(2,128)S(1)}, s32[128,2]{0,1:T(2,128)}, u32[]{:S(2)}) copy-start(s32[128,2]{0,1:T(2,128)} %param.25) | copy-start | bytes 3076
  0.0 13.7 %copy-start = (bf16[2,1024,88]{1,2,0:T(8,128)(2,1)S(1)}, bf16[2,1024,88]{1,2,0:T(8,128)(2,1)}, u32[]{:S(2)}) copy-start(bf16[2,1024,88]{1,2,0:T(8,128)(2,1)} %param.26) | copy-start | bytes 1081348
  4.0 16.5 %all-to-all-start = ((bf16[8,16,1024]{2,1,0:T(8,128)(2,1)}), bf16[8,16,1024]{2,1,0:T(8,128)(2,1)S(1)}, u32[]{:S(2)}, u32[]{:S(2)}) async-start(bf16[8,16,1024]{2,1,0:T(8,128)(2,1)} %bitcast.5), calls=%async_computation | async-start | bytes 524288 | tf_op jit(solution)/shard_map/all_to_all | solution.py:390
  13.7 2.1 %copy-start.3 = (s32[2,128]{1,0:T(2,128)}, s32[2,128]{1,0:T(2,128)S(1)}, u32[]{:S(2)}) copy-start(s32[2,128]{1,0:T(2,128)S(1)} %get-tuple-element.40.target_ref) | copy-start | bytes 3076
  13.7 18.9 %collective-permute-start = (bf16[2,88,1024]{2,1,0:T(8,128)(2,1)S(1)}, bf16[2,88,1024]{2,1,0:T(8,128)(2,1)S(1)}, u32[]{:S(2)}, u32[]{:S(2)}) collective-permute-start(bf16[2,88,1024]{2,1,0:T(8,128)(2,1)S(1)} %bitcast.19), channel_id=1, source_target_pairs={{0,2},{2,4},{4,6},{6,0},{1,3},{3,5},{5,7},{7,1},{8,10},{10,12},{12... | collective-permute-start | bytes 1081352 | tf_op jit(solution)/shard_map/ppermute | solution.py:389
  15.7 16.9 %collective-permute-start.1 = (bf16[2,88,1024]{2,1,0:T(8,128)(2,1)S(1)}, bf16[2,88,1024]{2,1,0:T(8,128)(2,1)S(1)}, u32[]{:S(2)}, u32[]{:S(2)}) collective-permute-start(bf16[2,88,1024]{2,1,0:T(8,128)(2,1)S(1)} %bitcast.20), channel_id=1, source_target_pairs={{0,4},{2,6},{4,0},{6,2},{1,5},{3,7},{5,1},{7,3},{8,12},{10,14},{12... | collective-permute-start | bytes 1081352 | tf_op jit(solution)/shard_map/ppermute | solution.py:389
  21.4 24.3 %all-to-all-start.1 = ((bf16[16,24,128]{2,1,0:T(8,128)(2,1)}), bf16[16,24,128]{2,1,0:T(8,128)(2,1)S(1)}, u32[]{:S(2)}, u32[]{:S(2)}) async-start(bf16[16,24,128]{2,1,0:T(8,128)(2,1)} %bitcast.7), calls=%async_computation.1 | async-start | bytes 196608 | tf_op jit(solution)/shard_map/all_to_all | solution.py:419
  32.4 0.6 copy-start.1
  33.1 17.9 %collective-permute-start.2 = (bf16[2,88,1024]{2,1,0:T(8,128)(2,1)S(1)}, bf16[2,88,1024]{2,1,0:T(8,128)(2,1)S(1)}, u32[]{:S(2)}, u32[]{:S(2)}) collective-permute-start(bf16[2,88,1024]{2,1,0:T(8,128)(2,1)S(1)} %bitcast.21), channel_id=1, source_target_pairs={{0,6},{2,0},{4,2},{6,4},{1,7},{3,1},{5,3},{7,5},{8,14},{10,8},{12,... | collective-permute-start | bytes 1081352 | tf_op jit(solution)/shard_map/ppermute | solution.py:429
  46.5 12.0 %all-to-all-start.2 = ((bf16[4,384,128]{2,1,0:T(8,128)(2,1)}), bf16[4,384,128]{2,1,0:T(8,128)(2,1)}, u32[]{:S(2)}, u32[]{:S(2)}) async-start(bf16[4,384,128]{2,1,0:T(8,128)(2,1)} %spread.1.spread_ref), calls=%async_computation.2 | async-start | bytes 786432 | tf_op jit(solution)/shard_map/all_to_all | solution.py:438
  51.0 9.9 %collective-permute-start.3 = (bf16[4,176,1024]{2,1,0:T(8,128)(2,1)S(1)}, bf16[4,176,1024]{2,1,0:T(8,128)(2,1)S(1)}, u32[]{:S(2)}, u32[]{:S(2)}) collective-permute-start(bf16[4,176,1024]{2,1,0:T(8,128)(2,1)S(1)} %stack.1.own_ref), channel_id=1, source_target_pairs={{0,1},{1,0},{2,3},{3,2},{4,5},{5,4},{6,7},{7,6},{8,9},{9,8},{10,11... | collective-permute-start | bytes 4325384 | tf_op jit(solution)/shard_map/ppermute | solution.py:448
  63.5 27.0 %copy-start.2 = (f32[16,1024]{1,0:T(8,128)S(1)}, f32[16,1024]{1,0:T(8,128)}, u32[]{:S(2)}) copy-start(f32[16,1024]{1,0:T(8,128)} %copy-done.1) | copy-start | bytes 196612
  63.6 27.0 %copy-start.4 = (s32[2,128]{1,0:T(2,128)S(1)}, s32[2,128]{1,0:T(2,128)}, u32[]{:S(2)}) copy-start(s32[2,128]{1,0:T(2,128)} %copy-done.3) | copy-start | bytes 3076

commit v8 on v7

--- a/solution.py
+++ b/solution.py
@@ -241,7 +241,7 @@
     copies = [pltpu.make_async_copy(tokens_hbm.at[at], tokens_ref.at[at], sems.at[at]) for at in range(tokens_ref.shape[0])]
     for copy in copies:
         copy.start()
-    fetch = pltpu.make_async_copy(down_hbm, down_ref, sem)
+    fetch = pltpu.make_async_copy(down_hbm.at[pl.ds(0, down_ref.shape[0])], down_ref, sem)
     fetch.start()
     groups, chunk_rows, _ = tokens_ref.shape
     chunks = rows_ref.shape[1] // LANES
@@ -258,7 +258,13 @@
     fetch.wait()
 
 
-def ffn_kernel(index_ref, rows_ref, order_ref, down_ref, own_hidden_ref, other_ref, out_ref, total_ref):
+def ffn_kernel(
+    index_ref, rows_ref, order_ref, first_ref, own_hidden_ref, other_ref, down_hbm, out_ref, total_ref, other_hidden_ref,
+    second_ref, sem
+):
+    half = second_ref.shape[0]
+    fetch = pltpu.make_async_copy(down_hbm.at[pl.ds(half, half)], second_ref, sem)
+    fetch.start()
     chips, both, _ = other_ref.shape
     groups, chunk_rows, _ = out_ref.shape
     width = rows_ref.shape[1]
@@ -267,15 +273,22 @@
     core = index_ref[0] % 2
     chip = index_ref[0] // 2
 
+    for shift in range(chips):
+        other_hidden_ref[shift] = hidden_of(rows_ref[...], other_ref[shift])
+
     def experts_part(own_first):
         total = None
-        for shift in range(chips):
-            came = (chip - shift + chips) % chips
-            pair = [own_hidden_ref[shift], hidden_of(rows_ref[...], other_ref[shift])]
+        for source in range(chips):
+            shift = (chip - source + chips) % chips
+            pair = [own_hidden_ref[shift], other_hidden_ref[shift]]
             hidden = jnp.concatenate(pair if own_first else pair[::-1], axis=1)
-            part = dot(hidden, down_ref[pl.ds(pl.multiple_of(came * both, 16), both), :])
+            down_ref = first_ref if source * both < half else second_ref
+            start = source * both % half
+            part = dot(hidden, down_ref[start : start + both, :])
             total = part if total is None else total + part
         total_ref[...] = total.astype(BF)
+
+    fetch.wait()
 
     @pl.when(core == 0)
     def _():
@@ -451,7 +464,7 @@
         out_shape=(
             jax.ShapeDtypeStruct((split * experts * CAPACITY, width), BF),
             jax.ShapeDtypeStruct((row, split * experts * CAPACITY, w_in.shape[2]), BF),
-            jax.ShapeDtypeStruct(w_out.shape, BF),
+            jax.ShapeDtypeStruct((w_out.shape[0] // 2, width), BF),
         ),
         in_specs=[HBM, VMEM, VMEM, HBM],
         out_specs=(VMEM,) * 3,
@@ -463,14 +476,17 @@
     projected = pl.pallas_call(
         ffn_kernel,
         out_shape=jax.ShapeDtypeStruct((split, slot_count, LANES), BF),
-        in_specs=[SMEM] + [VMEM] * 5,
+        in_specs=[SMEM] + [VMEM] * 5 + [HBM],
         out_specs=VMEM,
         scratch_shapes=[
             pltpu.VMEM((split * experts * CAPACITY, width), BF),
+            pltpu.VMEM(own_hidden.shape, BF),
+            pltpu.VMEM(down.shape, BF),
+            pltpu.SemaphoreType.DMA,
         ],
         compiler_params=PARAMS,
         name="ffn",
-    )(hid_index, rows, order, down, own_hidden, other_core)
+    )(hid_index, rows, order, down, own_hidden, other_core, in_hbm(w_out))
     quarters = lax.all_to_all(projected, "y", 0, 0, tiled=True)
     summed = pl.pallas_call(
         sum_kernel,

time: 92.2 us -> 93.1 us (level)
  starting transfers between devices: 36.6 us -> 38.1 us
  transfers between devices with their start and end apart: 7 -> 7, of which waited for: 2 -> 3; matrix products, arithmetic and copies ran while one was open for 0% -> 0% of each run, Pallas kernels for 6% -> 6%
where the time goes in v8:
time: 93.1 us; the launch traced here: 92.2 us
  starting transfers between devices  38.1 us (41%)
  blocking collectives  27.4 us (29%)
  waiting for transfers between devices  14 us (15%)
  Pallas kernels  12.4 us (13%)
    all_to_all x1, blocking collectives, body(): returned = lax.all_to_all(summed.reshape(exchanged), 'z', 0, 0, tiled=True)  17.5 us
    all_to_all x1, starting transfers between devices, body(): arrived = lax.all_to_all(outgoing.reshape(exchanged), 'z', 0, 0, tiled=True)  10.8 us
    all_to_all x1, blocking collectives, body(): quarters = lax.all_to_all(projected, 'y', 0, 0, tiled=True)  9.91 us
    all_to_all x1, starting transfers between devices, body(): lax.all_to_all(partial_mix.reshape(hid_count, block, width), hid, 0, 0, t...  9.21 us
    all_to_all x1, waiting for transfers between devices, body(): arrived = lax.all_to_all(outgoing.reshape(exchanged), 'z', 0, 0, tiled=True)  8.24 us
    ppermute x2, starting transfers between devices, body(): lax.ppermute(w_cols, 'x', move)  7.33 us
    all_to_all x1, waiting for transfers between devices, body(): tokens = lax.all_to_all(spread, 'y', 0, 0, tiled=True)  5.46 us
    all_to_all x1, starting transfers between devices, body(): tokens = lax.all_to_all(spread, 'y', 0, 0, tiled=True)  4.47 us
  transfers between devices with their start and end apart: 7, of which 3 were waited for; matrix products, arithmetic and copies ran while one was open for 0% of the time, Pallas kernels for 6%

profile of v8, /device:TPU:6, one launch (start us, length us, event | category | flops | bytes accessed | tf_op | source)
XLA Modules:
  0.0 92.2 jit_solution(11755812763593654634)
XLA Ops:
  0.0 0.0 copy-start.5
  0.0 0.0 copy-start
  0.0 4.0 %attention.1 = (bf16[128,1024]{1,0:T(8,128)(2,1)}, f32[16,1024]{1,0:T(8,128)S(1)}, f32[1,1024]{1,0:T(1,128)S(1)}, bf16[16,1024]{1,0:T(8,128)(2,1)S(1)}) custom-call(s32[1]{0:T(128)} %bitcast.index_ref, bf16[128,1024]{1,0:T(8,128)(2,1)} %resid_hbm.1, f32[1,1024]{1,0:T(1,128)} %bitcast.28, bf16[1024,128]{1,0:T(8,128)(2,1)} %wq_hbm.1, ...), custom_call_target="tpu_custom_call" | custom-call | tf_op jit(solution)/shard_map/attention/pallas_call | solution.py:373
  4.0 9.2 %all-to-all-start = ((bf16[8,16,1024]{2,1,0:T(8,128)(2,1)}), bf16[8,16,1024]{2,1,0:T(8,128)(2,1)S(1)}, u32[]{:S(2)}, u32[]{:S(2)}) async-start(bf16[8,16,1024]{2,1,0:T(8,128)(2,1)} %bitcast.5), calls=%async_computation | async-start | bytes 524288 | tf_op jit(solution)/shard_map/all_to_all | solution.py:403
  13.2 0.0 copy-done.5
  13.2 0.5 routing.1
  13.7 0.0 copy-start.3
  13.7 0.0 copy-done
  13.7 3.3 %collective-permute-start.1 = (bf16[2,88,1024]{2,1,0:T(8,128)(2,1)S(1)}, bf16[2,88,1024]{2,1,0:T(8,128)(2,1)S(1)}, u32[]{:S(2)}, u32[]{:S(2)}) collective-permute-start(bf16[2,88,1024]{2,1,0:T(8,128)(2,1)S(1)} %bitcast.19), channel_id=1, source_target_pairs={{0,4},{2,6},{4,0},{6,2},{1,5},{3,7},{5,1},{7,3},{8,12},{10,14},{12... | collective-permute-start | bytes 1081352 | tf_op jit(solution)/shard_map/ppermute | solution.py:402
  17.1 0.0 copy-done.3
  17.1 4.0 %collective-permute-start = (bf16[2,88,1024]{2,1,0:T(8,128)(2,1)S(1)}, bf16[2,88,1024]{2,1,0:T(8,128)(2,1)S(1)}, u32[]{:S(2)}, u32[]{:S(2)}) collective-permute-start(bf16[2,88,1024]{2,1,0:T(8,128)(2,1)S(1)} %bitcast.20), channel_id=1, source_target_pairs={{0,2},{2,4},{4,6},{6,0},{1,3},{3,5},{5,7},{7,1},{8,10},{10,12},{12... | collective-permute-start | bytes 1081352 | tf_op jit(solution)/shard_map/ppermute | solution.py:402
  21.1 0.0 all-to-all-done.parts_ref
  21.1 0.1 mix.1.ffn_in_ref
  21.2 0.8 dispatch.1
  22.0 10.8 %all-to-all-start.1 = ((bf16[16,24,128]{2,1,0:T(8,128)(2,1)}), bf16[16,24,128]{2,1,0:T(8,128)(2,1)S(1)}, u32[]{:S(2)}, u32[]{:S(2)}) async-start(bf16[16,24,128]{2,1,0:T(8,128)(2,1)} %bitcast.7), calls=%async_computation.1 | async-start | bytes 196608 | tf_op jit(solution)/shard_map/all_to_all | solution.py:432
  32.8 0.2 gates.1
  33.0 0.0 copy-start.1
  33.1 0.1 order.1.order_ref
  33.2 0.0 collective-permute-done.1
  33.2 0.3 collective-permute-done
  33.5 0.1 copy-done.1
  33.7 4.4 %collective-permute-start.2 = (bf16[2,88,1024]{2,1,0:T(8,128)(2,1)S(1)}, bf16[2,88,1024]{2,1,0:T(8,128)(2,1)S(1)}, u32[]{:S(2)}, u32[]{:S(2)}) collective-permute-start(bf16[2,88,1024]{2,1,0:T(8,128)(2,1)S(1)} %bitcast.21), channel_id=1, source_target_pairs={{0,6},{2,0},{4,2},{6,4},{1,7},{3,1},{5,3},{7,5},{8,14},{10,8},{12,... | collective-permute-start | bytes 1081352 | tf_op jit(solution)/shard_map/ppermute | solution.py:442
  38.0 8.2 %all-to-all-done.1 = bf16[16,24,128]{2,1,0:T(8,128)(2,1)S(1)} async-done(((bf16[16,24,128]{2,1,0:T(8,128)(2,1)}), bf16[16,24,128]{2,1,0:T(8,128)(2,1)S(1)}, u32[]{:S(2)}, u32[]{:S(2)}) %all-to-all-start.1) | async-done | bytes 98336 | tf_op jit(solution)/shard_map/all_to_all | solution.py:432
  46.3 0.8 spread.1.spread_ref
  47.1 4.5 %all-to-all-start.2 = ((bf16[4,384,128]{2,1,0:T(8,128)(2,1)}), bf16[4,384,128]{2,1,0:T(8,128)(2,1)}, u32[]{:S(2)}, u32[]{:S(2)}) async-start(bf16[4,384,128]{2,1,0:T(8,128)(2,1)} %spread.1.spread_ref), calls=%async_computation.2 | async-start | bytes 786432 | tf_op jit(solution)/shard_map/all_to_all | solution.py:451
  51.5 0.0 collective-permute-done.2
  51.5 0.1 stack.1.own_ref
  51.6 1.9 %collective-permute-start.3 = (bf16[4,176,1024]{2,1,0:T(8,128)(2,1)S(1)}, bf16[4,176,1024]{2,1,0:T(8,128)(2,1)S(1)}, u32[]{:S(2)}, u32[]{:S(2)}) collective-permute-start(bf16[4,176,1024]{2,1,0:T(8,128)(2,1)S(1)} %stack.1.own_ref), channel_id=1, source_target_pairs={{0,1},{1,0},{2,3},{3,2},{4,5},{5,4},{6,7},{7,6},{8,9},{9,8},{10,11... | collective-permute-start | bytes 4325384 | tf_op jit(solution)/shard_map/ppermute | solution.py:461
  53.6 5.5 %all-to-all-done.2.tokens_hbm = bf16[4,384,128]{2,1,0:T(8,128)(2,1)} async-done(((bf16[4,384,128]{2,1,0:T(8,128)(2,1)}), bf16[4,384,128]{2,1,0:T(8,128)(2,1)}, u32[]{:S(2)}, u32[]{:S(2)}) %all-to-all-start.2) | async-done | bytes 393248 | tf_op jit(solution)/shard_map/all_to_all | solution.py:451
  59.0 2.5 %own.1 = (bf16[192,1024]{1,0:T(8,128)(2,1)S(1)}, bf16[4,192,88]{2,1,0:T(8,128)(2,1)S(1)}, bf16[352,1024]{1,0:T(8,128)(2,1)S(1)}) custom-call(bf16[4,384,128]{2,1,0:T(8,128)(2,1)} %all-to-all-done.2.tokens_hbm, bf16[384,384]{1,0:T(8,128)(2,1)S(1)} %order.1.order_ref, bf16[4,176,1024]{2,1,0:T(8,128)(2,1)S(1)} %stack.1.own_ref, bf16[704,1024]{1,0:T(8,128)(2,1)} %down_hbm.3), custom_call_target="tpu_custom_call" | custom-call | flops 20000000000 | bytes 2097152 | tf_op jit(solution)/shard_map/own/pallas_call | solution.py:462
  61.6 0.0 collective-permute-done.3.other_ref
  61.6 2.2 %ffn.1 = bf16[4,384,128]{2,1,0:T(8,128)(2,1)S(1)} custom-call(s32[1]{0:T(128)} %bitcast.index_ref, bf16[192,1024]{1,0:T(8,128)(2,1)S(1)} %get-tuple-element.36.rows_ref, bf16[384,384]{1,0:T(8,128)(2,1)S(1)} %order.1.order_ref, bf16[352,1024]{1,0:T(8,128)(2,1)S(1)} %get-tuple-element.37.first_ref, bf16[4,192,88]{2,1,0:T(8,128)(2,1)S(1)} %get-tuple-element.38.own_hidden_ref, ...), custom_call_target="tpu_custom_call" | custom-call | tf_op jit(solution)/shard_map/ffn/pallas_call | solution.py:476
  63.8 0.0 copy-start.2
  63.8 0.0 copy-start.4
  63.8 9.9 %all_to_all.25.parts_ref = bf16[4,384,128]{2,1,0:T(8,128)(2,1)S(1)} all-to-all(bf16[4,384,128]{2,1,0:T(8,128)(2,1)S(1)} %ffn.1), channel_id=1, replica_groups=mesh['z'=16,'y'=4,'x'=4,'c'=2] {'y'}, dimensions={0} | all-to-all | bytes 786432 | tf_op jit(solution)/shard_map/all_to_all | solution.py:490
  73.7 0.1 sum_quarters.1
  73.8 17.5 %all_to_all.26 = bf16[16,24,128]{2,1,0:T(8,128)(2,1)S(1)} all-to-all(bf16[16,24,128]{2,1,0:T(8,128)(2,1)S(1)} %bitcast.18), channel_id=1, replica_groups=mesh['z'=16,'y'=4,'x'=4,'c'=2] {'z'}, dimensions={0} | all-to-all | bytes 196608 | tf_op jit(solution)/shard_map/all_to_all | solution.py:499
  91.3 0.0 copy-done.2
  91.3 0.0 copy-done.4
  91.3 1.0 %combine.1 = bf16[16,1024]{1,0:T(8,128)(2,1)} custom-call(bf16[384,128]{1,0:T(8,128)(2,1)S(1)} %bitcast.16, f32[16,1024]{1,0:T(8,128)S(1)} %copy-done.2, f32[2,16,128]{2,1,0:T(8,128)S(1)} %get-tuple-element.30.tokens_ref.gates_ref, s32[2,128]{1,0:T(2,128)S(1)} %copy-done.4), custom_call_target="tpu_custom_call" | custom-call | tf_op jit(solution)/shard_map/combine/pallas_call | solution.py:500
Async XLA Ops:
  0.0 13.2 %copy-start.5 = (s32[128,2]{0,1:T(2,128)S(1)}, s32[128,2]{0,1:T(2,128)}, u32[]{:S(2)}) copy-start(s32[128,2]{0,1:T(2,128)} %param.25) | copy-start | bytes 3076
  0.0 13.7 %copy-start = (bf16[2,1024,88]{1,2,0:T(8,128)(2,1)S(1)}, bf16[2,1024,88]{1,2,0:T(8,128)(2,1)}, u32[]{:S(2)}) copy-start(bf16[2,1024,88]{1,2,0:T(8,128)(2,1)} %param.26) | copy-start | bytes 1081348
  4.0 17.1 %all-to-all-start = ((bf16[8,16,1024]{2,1,0:T(8,128)(2,1)}), bf16[8,16,1024]{2,1,0:T(8,128)(2,1)S(1)}, u32[]{:S(2)}, u32[]{:S(2)}) async-start(bf16[8,16,1024]{2,1,0:T(8,128)(2,1)} %bitcast.5), calls=%async_computation | async-start | bytes 524288 | tf_op jit(solution)/shard_map/all_to_all | solution.py:403
  13.7 3.4 %copy-start.3 = (s32[2,128]{1,0:T(2,128)}, s32[2,128]{1,0:T(2,128)S(1)}, u32[]{:S(2)}) copy-start(s32[2,128]{1,0:T(2,128)S(1)} %get-tuple-element.40.target_ref) | copy-start | bytes 3076
  13.7 19.5 %collective-permute-start.1 = (bf16[2,88,1024]{2,1,0:T(8,128)(2,1)S(1)}, bf16[2,88,1024]{2,1,0:T(8,128)(2,1)S(1)}, u32[]{:S(2)}, u32[]{:S(2)}) collective-permute-start(bf16[2,88,1024]{2,1,0:T(8,128)(2,1)S(1)} %bitcast.19), channel_id=1, source_target_pairs={{0,4},{2,6},{4,0},{6,2},{1,5},{3,7},{5,1},{7,3},{8,12},{10,14},{12... | collective-permute-start | bytes 1081352 | tf_op jit(solution)/shard_map/ppermute | solution.py:402
  17.1 16.5 %collective-permute-start = (bf16[2,88,1024]{2,1,0:T(8,128)(2,1)S(1)}, bf16[2,88,1024]{2,1,0:T(8,128)(2,1)S(1)}, u32[]{:S(2)}, u32[]{:S(2)}) collective-permute-start(bf16[2,88,1024]{2,1,0:T(8,128)(2,1)S(1)} %bitcast.20), channel_id=1, source_target_pairs={{0,2},{2,4},{4,6},{6,0},{1,3},{3,5},{5,7},{7,1},{8,10},{10,12},{12... | collective-permute-start | bytes 1081352 | tf_op jit(solution)/shard_map/ppermute | solution.py:402
  22.0 24.3 %all-to-all-start.1 = ((bf16[16,24,128]{2,1,0:T(8,128)(2,1)}), bf16[16,24,128]{2,1,0:T(8,128)(2,1)S(1)}, u32[]{:S(2)}, u32[]{:S(2)}) async-start(bf16[16,24,128]{2,1,0:T(8,128)(2,1)} %bitcast.7), calls=%async_computation.1 | async-start | bytes 196608 | tf_op jit(solution)/shard_map/all_to_all | solution.py:432
  33.0 0.6 copy-start.1
  33.7 17.9 %collective-permute-start.2 = (bf16[2,88,1024]{2,1,0:T(8,128)(2,1)S(1)}, bf16[2,88,1024]{2,1,0:T(8,128)(2,1)S(1)}, u32[]{:S(2)}, u32[]{:S(2)}) collective-permute-start(bf16[2,88,1024]{2,1,0:T(8,128)(2,1)S(1)} %bitcast.21), channel_id=1, source_target_pairs={{0,6},{2,0},{4,2},{6,4},{1,7},{3,1},{5,3},{7,5},{8,14},{10,8},{12,... | collective-permute-start | bytes 1081352 | tf_op jit(solution)/shard_map/ppermute | solution.py:442
  47.1 12.0 %all-to-all-start.2 = ((bf16[4,384,128]{2,1,0:T(8,128)(2,1)}), bf16[4,384,128]{2,1,0:T(8,128)(2,1)}, u32[]{:S(2)}, u32[]{:S(2)}) async-start(bf16[4,384,128]{2,1,0:T(8,128)(2,1)} %spread.1.spread_ref), calls=%async_computation.2 | async-start | bytes 786432 | tf_op jit(solution)/shard_map/all_to_all | solution.py:451
  51.6 9.9 %collective-permute-start.3 = (bf16[4,176,1024]{2,1,0:T(8,128)(2,1)S(1)}, bf16[4,176,1024]{2,1,0:T(8,128)(2,1)S(1)}, u32[]{:S(2)}, u32[]{:S(2)}) collective-permute-start(bf16[4,176,1024]{2,1,0:T(8,128)(2,1)S(1)} %stack.1.own_ref), channel_id=1, source_target_pairs={{0,1},{1,0},{2,3},{3,2},{4,5},{5,4},{6,7},{7,6},{8,9},{9,8},{10,11... | collective-permute-start | bytes 4325384 | tf_op jit(solution)/shard_map/ppermute | solution.py:461
  63.8 27.4 %copy-start.2 = (f32[16,1024]{1,0:T(8,128)S(1)}, f32[16,1024]{1,0:T(8,128)}, u32[]{:S(2)}) copy-start(f32[16,1024]{1,0:T(8,128)} %copy-done.1) | copy-start | bytes 196612
  63.8 27.4 %copy-start.4 = (s32[2,128]{1,0:T(2,128)S(1)}, s32[2,128]{1,0:T(2,128)}, u32[]{:S(2)}) copy-start(s32[2,128]{1,0:T(2,128)} %copy-done.3) | copy-start | bytes 3076

commit v9 on v8

--- a/solution.py
+++ b/solution.py
@@ -438,7 +438,8 @@
         compiler_params=PARAMS,
         name="order",
     )(gates)
-    order, *own_core = lax.optimization_barrier((order, *own_core))
+    order, across, beside, w_cols = lax.optimization_barrier((order, own_core[2], own_core[1], own_core[0]))
+    own_core = [w_cols, beside, across]
     own_core.append(lax.ppermute(own_core[0], "x", moves[-1]))
     spread = pl.pallas_call(
         spread_kernel,

time: 93.1 us -> 92.3 us (level)
  starting transfers between devices: 38.1 us -> 36.6 us
  transfers between devices with their start and end apart: 7 -> 7, of which waited for: 3 -> 2; matrix products, arithmetic and copies ran while one was open for 0% -> 0% of each run, Pallas kernels for 6% -> 6%
where the time goes in v9:
time: 92.3 us; the launch traced here: 91.6 us
  starting transfers between devices  36.6 us (40%)
  blocking collectives  27.4 us (30%)
  waiting for transfers between devices  14.6 us (16%)
  Pallas kernels  12.4 us (13%)
    all_to_all x1, blocking collectives, body(): returned = lax.all_to_all(summed.reshape(exchanged), 'z', 0, 0, tiled=True)  17.5 us
    all_to_all x1, starting transfers between devices, body(): arrived = lax.all_to_all(outgoing.reshape(exchanged), 'z', 0, 0, tiled=True)  10.8 us
    all_to_all x1, blocking collectives, body(): quarters = lax.all_to_all(projected, 'y', 0, 0, tiled=True)  9.91 us
    all_to_all x1, starting transfers between devices, body(): lax.all_to_all(partial_mix.reshape(hid_count, block, width), hid, 0, 0, t...  9.21 us
    all_to_all x1, waiting for transfers between devices, body(): arrived = lax.all_to_all(outgoing.reshape(exchanged), 'z', 0, 0, tiled=True)  9.14 us
    ppermute x2, starting transfers between devices, body(): lax.ppermute(w_cols, 'x', move)  6.73 us
    all_to_all x1, waiting for transfers between devices, body(): tokens = lax.all_to_all(spread, 'y', 0, 0, tiled=True)  5.46 us
    all_to_all x1, starting transfers between devices, body(): tokens = lax.all_to_all(spread, 'y', 0, 0, tiled=True)  4.47 us
  transfers between devices with their start and end apart: 7, of which 2 were waited for; matrix products, arithmetic and copies ran while one was open for 0% of the time, Pallas kernels for 6%

profile of v9, /device:TPU:6, one launch (start us, length us, event | category | flops | bytes accessed | tf_op | source)
XLA Modules:
  0.0 91.6 jit_solution(10350345116089979058)
XLA Ops:
  0.0 0.0 copy-start.5
  0.0 0.0 copy-start
  0.0 4.0 %attention.1 = (bf16[128,1024]{1,0:T(8,128)(2,1)}, f32[16,1024]{1,0:T(8,128)S(1)}, f32[1,1024]{1,0:T(1,128)S(1)}, bf16[16,1024]{1,0:T(8,128)(2,1)S(1)}) custom-call(s32[1]{0:T(128)} %bitcast.index_ref, bf16[128,1024]{1,0:T(8,128)(2,1)} %resid_hbm.1, f32[1,1024]{1,0:T(1,128)} %bitcast.28, bf16[1024,128]{1,0:T(8,128)(2,1)} %wq_hbm.1, ...), custom_call_target="tpu_custom_call" | custom-call | tf_op jit(solution)/shard_map/attention/pallas_call | solution.py:373
  4.0 9.2 %all-to-all-start = ((bf16[8,16,1024]{2,1,0:T(8,128)(2,1)}), bf16[8,16,1024]{2,1,0:T(8,128)(2,1)S(1)}, u32[]{:S(2)}, u32[]{:S(2)}) async-start(bf16[8,16,1024]{2,1,0:T(8,128)(2,1)} %bitcast.5), calls=%async_computation | async-start | bytes 524288 | tf_op jit(solution)/shard_map/all_to_all | solution.py:403
  13.2 0.0 copy-done.5
  13.2 0.5 routing.1
  13.7 0.0 copy-start.3
  13.7 0.0 copy-done
  13.7 2.0 %collective-permute-start.1 = (bf16[2,88,1024]{2,1,0:T(8,128)(2,1)S(1)}, bf16[2,88,1024]{2,1,0:T(8,128)(2,1)S(1)}, u32[]{:S(2)}, u32[]{:S(2)}) collective-permute-start(bf16[2,88,1024]{2,1,0:T(8,128)(2,1)S(1)} %bitcast.19), channel_id=1, source_target_pairs={{0,2},{2,4},{4,6},{6,0},{1,3},{3,5},{5,7},{7,1},{8,10},{10,12},{12... | collective-permute-start | bytes 1081352 | tf_op jit(solution)/shard_map/ppermute | solution.py:402
  15.7 0.0 copy-done.3
  15.7 4.7 %collective-permute-start = (bf16[2,88,1024]{2,1,0:T(8,128)(2,1)S(1)}, bf16[2,88,1024]{2,1,0:T(8,128)(2,1)S(1)}, u32[]{:S(2)}, u32[]{:S(2)}) collective-permute-start(bf16[2,88,1024]{2,1,0:T(8,128)(2,1)S(1)} %bitcast.20), channel_id=1, source_target_pairs={{0,4},{2,6},{4,0},{6,2},{1,5},{3,7},{5,1},{7,3},{8,12},{10,14},{12... | collective-permute-start | bytes 1081352 | tf_op jit(solution)/shard_map/ppermute | solution.py:402
  20.5 0.0 all-to-all-done.parts_ref
  20.5 0.1 mix.1.ffn_in_ref
  20.6 0.8 dispatch.1
  21.4 10.8 %all-to-all-start.1 = ((bf16[16,24,128]{2,1,0:T(8,128)(2,1)}), bf16[16,24,128]{2,1,0:T(8,128)(2,1)S(1)}, u32[]{:S(2)}, u32[]{:S(2)}) async-start(bf16[16,24,128]{2,1,0:T(8,128)(2,1)} %bitcast.7), calls=%async_computation.1 | async-start | bytes 196608 | tf_op jit(solution)/shard_map/all_to_all | solution.py:432
  32.2 0.2 gates.1
  32.4 0.0 copy-start.1
  32.4 0.1 order.1.order_ref
  32.6 0.0 collective-permute-done.1
  32.6 0.0 collective-permute-done
  32.6 0.4 copy-done.1
  33.1 3.5 %collective-permute-start.2 = (bf16[2,88,1024]{2,1,0:T(8,128)(2,1)S(1)}, bf16[2,88,1024]{2,1,0:T(8,128)(2,1)S(1)}, u32[]{:S(2)}, u32[]{:S(2)}) collective-permute-start(bf16[2,88,1024]{2,1,0:T(8,128)(2,1)S(1)} %bitcast.21), channel_id=1, source_target_pairs={{0,6},{2,0},{4,2},{6,4},{1,7},{3,1},{5,3},{7,5},{8,14},{10,8},{12,... | collective-permute-start | bytes 1081352 | tf_op jit(solution)/shard_map/ppermute | solution.py:443
  36.5 9.1 %all-to-all-done.1 = bf16[16,24,128]{2,1,0:T(8,128)(2,1)S(1)} async-done(((bf16[16,24,128]{2,1,0:T(8,128)(2,1)}), bf16[16,24,128]{2,1,0:T(8,128)(2,1)S(1)}, u32[]{:S(2)}, u32[]{:S(2)}) %all-to-all-start.1) | async-done | bytes 98336 | tf_op jit(solution)/shard_map/all_to_all | solution.py:432
  45.7 0.8 spread.1.spread_ref
  46.5 4.5 %all-to-all-start.2 = ((bf16[4,384,128]{2,1,0:T(8,128)(2,1)}), bf16[4,384,128]{2,1,0:T(8,128)(2,1)}, u32[]{:S(2)}, u32[]{:S(2)}) async-start(bf16[4,384,128]{2,1,0:T(8,128)(2,1)} %spread.1.spread_ref), calls=%async_computation.2 | async-start | bytes 786432 | tf_op jit(solution)/shard_map/all_to_all | solution.py:452
  50.9 0.0 collective-permute-done.2
  50.9 0.1 stack.1.own_ref
  51.0 1.9 %collective-permute-start.3 = (bf16[4,176,1024]{2,1,0:T(8,128)(2,1)S(1)}, bf16[4,176,1024]{2,1,0:T(8,128)(2,1)S(1)}, u32[]{:S(2)}, u32[]{:S(2)}) collective-permute-start(bf16[4,176,1024]{2,1,0:T(8,128)(2,1)S(1)} %stack.1.own_ref), channel_id=1, source_target_pairs={{0,1},{1,0},{2,3},{3,2},{4,5},{5,4},{6,7},{7,6},{8,9},{9,8},{10,11... | collective-permute-start | bytes 4325384 | tf_op jit(solution)/shard_map/ppermute | solution.py:462
  53.0 5.5 %all-to-all-done.2.tokens_hbm = bf16[4,384,128]{2,1,0:T(8,128)(2,1)} async-done(((bf16[4,384,128]{2,1,0:T(8,128)(2,1)}), bf16[4,384,128]{2,1,0:T(8,128)(2,1)}, u32[]{:S(2)}, u32[]{:S(2)}) %all-to-all-start.2) | async-done | bytes 393248 | tf_op jit(solution)/shard_map/all_to_all | solution.py:452
  58.4 2.5 %own.1 = (bf16[192,1024]{1,0:T(8,128)(2,1)S(1)}, bf16[4,192,88]{2,1,0:T(8,128)(2,1)S(1)}, bf16[352,1024]{1,0:T(8,128)(2,1)S(1)}) custom-call(bf16[4,384,128]{2,1,0:T(8,128)(2,1)} %all-to-all-done.2.tokens_hbm, bf16[384,384]{1,0:T(8,128)(2,1)S(1)} %order.1.order_ref, bf16[4,176,1024]{2,1,0:T(8,128)(2,1)S(1)} %stack.1.own_ref, bf16[704,1024]{1,0:T(8,128)(2,1)} %down_hbm.3), custom_call_target="tpu_custom_call" | custom-call | flops 20000000000 | bytes 2097152 | tf_op jit(solution)/shard_map/own/pallas_call | solution.py:463
  61.0 0.0 collective-permute-done.3.other_ref
  61.0 2.2 %ffn.1 = bf16[4,384,128]{2,1,0:T(8,128)(2,1)S(1)} custom-call(s32[1]{0:T(128)} %bitcast.index_ref, bf16[192,1024]{1,0:T(8,128)(2,1)S(1)} %get-tuple-element.36.rows_ref, bf16[384,384]{1,0:T(8,128)(2,1)S(1)} %order.1.order_ref, bf16[352,1024]{1,0:T(8,128)(2,1)S(1)} %get-tuple-element.37.first_ref, bf16[4,192,88]{2,1,0:T(8,128)(2,1)S(1)} %get-tuple-element.38.own_hidden_ref, ...), custom_call_target="tpu_custom_call" | custom-call | tf_op jit(solution)/shard_map/ffn/pallas_call | solution.py:477
  63.2 0.0 copy-start.2
  63.2 0.0 copy-start.4
  63.2 9.9 %all_to_all.25.parts_ref = bf16[4,384,128]{2,1,0:T(8,128)(2,1)S(1)} all-to-all(bf16[4,384,128]{2,1,0:T(8,128)(2,1)S(1)} %ffn.1), channel_id=1, replica_groups=mesh['z'=16,'y'=4,'x'=4,'c'=2] {'y'}, dimensions={0} | all-to-all | bytes 786432 | tf_op jit(solution)/shard_map/all_to_all | solution.py:491
  73.1 0.1 sum_quarters.1
  73.2 17.5 %all_to_all.26 = bf16[16,24,128]{2,1,0:T(8,128)(2,1)S(1)} all-to-all(bf16[16,24,128]{2,1,0:T(8,128)(2,1)S(1)} %bitcast.18), channel_id=1, replica_groups=mesh['z'=16,'y'=4,'x'=4,'c'=2] {'z'}, dimensions={0} | all-to-all | bytes 196608 | tf_op jit(solution)/shard_map/all_to_all | solution.py:500
  90.7 0.0 copy-done.2
  90.7 0.0 copy-done.4
  90.7 1.0 %combine.1 = bf16[16,1024]{1,0:T(8,128)(2,1)} custom-call(bf16[384,128]{1,0:T(8,128)(2,1)S(1)} %bitcast.16, f32[16,1024]{1,0:T(8,128)S(1)} %copy-done.2, f32[2,16,128]{2,1,0:T(8,128)S(1)} %get-tuple-element.30.tokens_ref.gates_ref, s32[2,128]{1,0:T(2,128)S(1)} %copy-done.4), custom_call_target="tpu_custom_call" | custom-call | tf_op jit(solution)/shard_map/combine/pallas_call | solution.py:501
Async XLA Ops:
  0.0 13.2 %copy-start.5 = (s32[128,2]{0,1:T(2,128)S(1)}, s32[128,2]{0,1:T(2,128)}, u32[]{:S(2)}) copy-start(s32[128,2]{0,1:T(2,128)} %param.25) | copy-start | bytes 3076
  0.0 13.7 %copy-start = (bf16[2,1024,88]{1,2,0:T(8,128)(2,1)S(1)}, bf16[2,1024,88]{1,2,0:T(8,128)(2,1)}, u32[]{:S(2)}) copy-start(bf16[2,1024,88]{1,2,0:T(8,128)(2,1)} %param.26) | copy-start | bytes 1081348
  4.0 16.5 %all-to-all-start = ((bf16[8,16,1024]{2,1,0:T(8,128)(2,1)}), bf16[8,16,1024]{2,1,0:T(8,128)(2,1)S(1)}, u32[]{:S(2)}, u32[]{:S(2)}) async-start(bf16[8,16,1024]{2,1,0:T(8,128)(2,1)} %bitcast.5), calls=%async_computation | async-start | bytes 524288 | tf_op jit(solution)/shard_map/all_to_all | solution.py:403
  13.7 2.1 %copy-start.3 = (s32[2,128]{1,0:T(2,128)}, s32[2,128]{1,0:T(2,128)S(1)}, u32[]{:S(2)}) copy-start(s32[2,128]{1,0:T(2,128)S(1)} %get-tuple-element.40.target_ref) | copy-start | bytes 3076
  13.7 18.9 %collective-permute-start.1 = (bf16[2,88,1024]{2,1,0:T(8,128)(2,1)S(1)}, bf16[2,88,1024]{2,1,0:T(8,128)(2,1)S(1)}, u32[]{:S(2)}, u32[]{:S(2)}) collective-permute-start(bf16[2,88,1024]{2,1,0:T(8,128)(2,1)S(1)} %bitcast.19), channel_id=1, source_target_pairs={{0,2},{2,4},{4,6},{6,0},{1,3},{3,5},{5,7},{7,1},{8,10},{10,12},{12... | collective-permute-start | bytes 1081352 | tf_op jit(solution)/shard_map/ppermute | solution.py:402
  15.7 16.9 %collective-permute-start = (bf16[2,88,1024]{2,1,0:T(8,128)(2,1)S(1)}, bf16[2,88,1024]{2,1,0:T(8,128)(2,1)S(1)}, u32[]{:S(2)}, u32[]{:S(2)}) collective-permute-start(bf16[2,88,1024]{2,1,0:T(8,128)(2,1)S(1)} %bitcast.20), channel_id=1, source_target_pairs={{0,4},{2,6},{4,0},{6,2},{1,5},{3,7},{5,1},{7,3},{8,12},{10,14},{12... | collective-permute-start | bytes 1081352 | tf_op jit(solution)/shard_map/ppermute | solution.py:402
  21.4 24.3 %all-to-all-start.1 = ((bf16[16,24,128]{2,1,0:T(8,128)(2,1)}), bf16[16,24,128]{2,1,0:T(8,128)(2,1)S(1)}, u32[]{:S(2)}, u32[]{:S(2)}) async-start(bf16[16,24,128]{2,1,0:T(8,128)(2,1)} %bitcast.7), calls=%async_computation.1 | async-start | bytes 196608 | tf_op jit(solution)/shard_map/all_to_all | solution.py:432
  32.4 0.6 copy-start.1
  33.1 17.9 %collective-permute-start.2 = (bf16[2,88,1024]{2,1,0:T(8,128)(2,1)S(1)}, bf16[2,88,1024]{2,1,0:T(8,128)(2,1)S(1)}, u32[]{:S(2)}, u32[]{:S(2)}) collective-permute-start(bf16[2,88,1024]{2,1,0:T(8,128)(2,1)S(1)} %bitcast.21), channel_id=1, source_target_pairs={{0,6},{2,0},{4,2},{6,4},{1,7},{3,1},{5,3},{7,5},{8,14},{10,8},{12,... | collective-permute-start | bytes 1081352 | tf_op jit(solution)/shard_map/ppermute | solution.py:443
  46.5 12.0 %all-to-all-start.2 = ((bf16[4,384,128]{2,1,0:T(8,128)(2,1)}), bf16[4,384,128]{2,1,0:T(8,128)(2,1)}, u32[]{:S(2)}, u32[]{:S(2)}) async-start(bf16[4,384,128]{2,1,0:T(8,128)(2,1)} %spread.1.spread_ref), calls=%async_computation.2 | async-start | bytes 786432 | tf_op jit(solution)/shard_map/all_to_all | solution.py:452
  51.0 9.9 %collective-permute-start.3 = (bf16[4,176,1024]{2,1,0:T(8,128)(2,1)S(1)}, bf16[4,176,1024]{2,1,0:T(8,128)(2,1)S(1)}, u32[]{:S(2)}, u32[]{:S(2)}) collective-permute-start(bf16[4,176,1024]{2,1,0:T(8,128)(2,1)S(1)} %stack.1.own_ref), channel_id=1, source_target_pairs={{0,1},{1,0},{2,3},{3,2},{4,5},{5,4},{6,7},{7,6},{8,9},{9,8},{10,11... | collective-permute-start | bytes 4325384 | tf_op jit(solution)/shard_map/ppermute | solution.py:462
  63.2 27.5 %copy-start.2 = (f32[16,1024]{1,0:T(8,128)S(1)}, f32[16,1024]{1,0:T(8,128)}, u32[]{:S(2)}) copy-start(f32[16,1024]{1,0:T(8,128)} %copy-done.1) | copy-start | bytes 196612
  63.2 27.5 %copy-start.4 = (s32[2,128]{1,0:T(2,128)S(1)}, s32[2,128]{1,0:T(2,128)}, u32[]{:S(2)}) copy-start(s32[2,128]{1,0:T(2,128)} %copy-done.3) | copy-start | bytes 3076
